TPU v7x, 32 devices: a whole 2x2x4 slice. The times are simulated.
32 devices in a mesh: fsdp: 2 (over x), ctx: 4 (over z), tp: 4 (over y, core).
Axes of the slice: x: 2, y: 2, z: 4, core: 2. Of those that a mesh axis runs over, the one named last changes fastest.
Arguments:
- tokens: bfloat16 [4, 2048, 2048], P('fsdp', 'ctx'), may hold values from -6 to 6
- tree_position: int32 [4, 2048], P('fsdp', 'ctx'), may hold values from 0 to 2047, as said below
- segment: int32 [4, 2048], P('fsdp', 'ctx'), may hold values from 0 to 6, as said below
- parent_table: int32 [4, 7], P('fsdp'), may hold values from 0 to 2, as said below
- norm1_gain: float32 [2048], replicated, may hold values from 0.5 to 1.5
- norm1_shift: float32 [2048], replicated, may hold values from -4 to 4
- query_weight: bfloat16 [2048, 2048], P('fsdp', 'tp'), may hold values from -0.125 to 0.125
- query_bias: float32 [2048], P('tp'), may hold values from -4 to 4
- key_weight: bfloat16 [2048, 2048], P('fsdp', 'tp'), may hold values from -0.125 to 0.125
- value_weight: bfloat16 [2048, 2048], P('fsdp', 'tp'), may hold values from -0.125 to 0.125
- value_bias: float32 [2048], P('tp'), may hold values from -0.75 to 0.75
- out_weight: bfloat16 [2048, 2048], P('tp', 'fsdp'), may hold values from -1.5 to 1.5
- out_bias: float32 [2048], replicated, may hold values from -4 to 4
- norm2_gain: float32 [2048], replicated, may hold values from 0.5 to 1.5
- norm2_shift: float32 [2048], replicated, may hold values from -4 to 4
- up_weight: bfloat16 [2048, 8192], P('fsdp', 'tp'), may hold values from -0.125 to 0.125
- up_bias: float32 [8192], P('tp'), may hold values from -4 to 4
- down_weight: bfloat16 [8192, 2048], P('tp', 'fsdp'), may hold values from -0.0625 to 0.0625
- down_bias: float32 [2048], replicated, may hold values from -4 to 4
- cotangent: bfloat16 [4, 2048, 2048], P('fsdp', 'ctx'), may hold values from -6 to 6
Outputs:
- layer_out: bfloat16 [4, 2048, 2048], P('fsdp', 'ctx')
- grad_tokens: bfloat16 [4, 2048, 2048], P('fsdp', 'ctx')
- grad_norm1_gain: float32 [2048], P(('fsdp', 'ctx'))
- grad_norm1_shift: float32 [2048], P(('fsdp', 'ctx'))
- grad_query_weight: float32 [2048, 2048], P(('fsdp', 'ctx'), 'tp')
- grad_query_bias: float32 [2048], P('tp')
- grad_key_weight: float32 [2048, 2048], P(('fsdp', 'ctx'), 'tp')
- grad_value_weight: float32 [2048, 2048], P(('fsdp', 'ctx'), 'tp')
- grad_value_bias: float32 [2048], P('tp')
- grad_out_weight: float32 [2048, 2048], P('tp', ('fsdp', 'ctx'))
- grad_out_bias: float32 [2048], P(('fsdp', 'ctx'))
- grad_norm2_gain: float32 [2048], P(('fsdp', 'ctx'))
- grad_norm2_shift: float32 [2048], P(('fsdp', 'ctx'))
- grad_up_weight: float32 [2048, 8192], P(('fsdp', 'ctx'), 'tp')
- grad_up_bias: float32 [8192], P('tp')
- grad_down_weight: float32 [8192, 2048], P('tp', ('fsdp', 'ctx'))
- grad_down_bias: float32 [2048], P(('fsdp', 'ctx'))
Inputs may be any that keep to these rules, and one draw needn't show every extreme that they name: `tree_position`: within each tree the rows hold the positions 0 to 2047 once each; every aligned run of 64 rows holds 64 consecutive positions in increasing order. `segment`: along increasing positions a tree runs through segments 0 to 6 in order, each nonempty and contiguous: the trunk 0 with 1024 positions, branches 1 and 2 with 512 together, leaves 3 to 6 with 512 together. `parent_table`: entry s of a tree's row is the parent of segment s: 0 for segments 0, 1 and 2; 1 for leaf 3; 2 for leaf 6; 1 or 2 for leaves 4 and 5.
All inputs are finite; a program needn't handle non-finite values.
Results may differ from a plain program's by a relative error of at most 0.024.
Values may be sent and summed in bfloat16 or wider, within the bound.
No kernel may reach another device: no remote copies, remote signals or barrier semaphores. Data moves between devices by JAX's collectives and lax.ppermute only.
A program may use at most 256 MiB of HBM per device.

v0:
```python
from functools import partial
import math

import jax
import jax.numpy as jnp
from jax import lax
from jax.sharding import PartitionSpec as P

HD = 128


NEGATIVE = -1000000000.0


def norm_rows(values, gain, shift):
    centre = jnp.mean(values, axis=-1, keepdims=True)
    centred = values - centre
    spread = jnp.mean(centred * centred, axis=-1, keepdims=True)
    return centred * lax.rsqrt(spread + 1e-05) * gain + shift


def on_path(query_pos, query_seg, key_pos, key_seg, parent):
    labels = jnp.arange(parent.shape[0], dtype=jnp.int32)
    first = jnp.sum(jnp.where(query_seg[:, None] == labels[None, :], parent[None, :], 0), axis=1)
    second = jnp.sum(jnp.where(first[:, None] == labels[None, :], parent[None, :], 0), axis=1)
    along = (
        (key_seg[None, :] == query_seg[:, None])
        | (key_seg[None, :] == first[:, None])
        | (key_seg[None, :] == second[:, None])
    )
    return along & (key_pos[None, :] <= query_pos[:, None])


def inner_rows(left, right):
    return lax.dot_general(
        left, right, (((0,), (0,)), ((), ())), preferred_element_type=jnp.float32
    )


def times_transposed(left, right):
    return lax.dot_general(
        left, right, (((1,), (1,)), ((), ())), preferred_element_type=jnp.float32
    )


def per_device(
    tokens,
    tree_position,
    segment,
    parent_table,
    norm1_gain,
    norm1_shift,
    query_weight,
    query_bias,
    key_weight,
    value_weight,
    value_bias,
    out_weight,
    out_bias,
    norm2_gain,
    norm2_shift,
    up_weight,
    up_bias,
    down_weight,
    down_bias,
    cotangent,
):
    w_query, w_key, w_value, w_out, w_up, w_down = (
        lax.all_gather(query_weight, "fsdp", axis=0, tiled=True),
        lax.all_gather(key_weight, "fsdp", axis=0, tiled=True),
        lax.all_gather(value_weight, "fsdp", axis=0, tiled=True),
        lax.all_gather(out_weight, "fsdp", axis=1, tiled=True),
        lax.all_gather(up_weight, "fsdp", axis=0, tiled=True),
        lax.all_gather(down_weight, "fsdp", axis=1, tiled=True),
    )
    key_position, key_segment = (
        lax.all_gather(tree_position, "ctx", axis=1, tiled=True),
        lax.all_gather(segment, "ctx", axis=1, tiled=True),
    )
    local_width = w_query.shape[1]
    head_count = local_width // HD
    score_scale = 1.0 / math.sqrt(HD)
    gelu_exact = partial(jax.nn.gelu, approximate=False)
    layer_rows = []
    input_grads = []
    running = [
        jnp.zeros(w_query.shape, jnp.float32),
        jnp.zeros(w_key.shape, jnp.float32),
        jnp.zeros(w_value.shape, jnp.float32),
        jnp.zeros(w_out.shape, jnp.float32),
        jnp.zeros(w_up.shape, jnp.float32),
        jnp.zeros(w_down.shape, jnp.float32),
        jnp.zeros(norm1_gain.shape, jnp.float32),
        jnp.zeros(norm1_shift.shape, jnp.float32),
        jnp.zeros(norm2_gain.shape, jnp.float32),
        jnp.zeros(norm2_shift.shape, jnp.float32),
        jnp.zeros(out_bias.shape, jnp.float32),
        jnp.zeros(down_bias.shape, jnp.float32),
    ]
    head_sums = [
        jnp.zeros(query_bias.shape, jnp.float32),
        jnp.zeros(value_bias.shape, jnp.float32),
        jnp.zeros(up_bias.shape, jnp.float32),
    ]
    for batch_index in range(tokens.shape[0]):
        inputs = tokens[batch_index].astype(jnp.float32)
        local_rows = inputs.shape[0]
        normed = norm_rows(inputs, norm1_gain, norm1_shift).astype(jnp.bfloat16)
        queries = (
            jnp.dot(normed, w_query, preferred_element_type=jnp.float32) + query_bias
        ).astype(jnp.bfloat16)
        keys_local = jnp.dot(normed, w_key, preferred_element_type=jnp.float32).astype(jnp.bfloat16)
        values_local = (
            jnp.dot(normed, w_value, preferred_element_type=jnp.float32) + value_bias
        ).astype(jnp.bfloat16)
        keys_tree, values_tree = (
            lax.all_gather(keys_local, "ctx", axis=0, tiled=True),
            lax.all_gather(values_local, "ctx", axis=0, tiled=True),
        )
        tree_rows = keys_tree.shape[0]
        visible = on_path(
            tree_position[batch_index],
            segment[batch_index],
            key_position[batch_index],
            key_segment[batch_index],
            parent_table[batch_index],
        )
        query_heads = queries.reshape(local_rows, head_count, HD)
        key_heads = keys_tree.reshape(tree_rows, head_count, HD)
        value_heads = values_tree.reshape(tree_rows, head_count, HD)
        scores = (
            jnp.einsum("qhd,khd->hqk", query_heads, key_heads, preferred_element_type=jnp.float32)
            * score_scale
        )
        scores = jnp.where(visible[None], scores, NEGATIVE)
        row_max = jnp.max(scores, axis=-1, keepdims=True)
        shifted = jnp.exp(scores - row_max)
        row_total = jnp.sum(shifted, axis=-1, keepdims=True)
        log_total = row_max + jnp.log(row_total)
        soft_low = (shifted / row_total).astype(jnp.bfloat16)
        attended = (
            jnp.einsum("hqk,khd->qhd", soft_low, value_heads, preferred_element_type=jnp.float32)
            .reshape(local_rows, local_width)
            .astype(jnp.bfloat16)
        )
        middle = inputs + (
            lax.psum(
                jnp.dot(attended, w_out, preferred_element_type=jnp.float32).astype(jnp.bfloat16),
                "tp",
            ).astype(jnp.float32)
            + out_bias
        )
        normed_mid = norm_rows(middle, norm2_gain, norm2_shift).astype(jnp.bfloat16)
        hidden = jnp.dot(normed_mid, w_up, preferred_element_type=jnp.float32) + up_bias
        active = gelu_exact(hidden).astype(jnp.bfloat16)
        result = middle + (
            lax.psum(
                jnp.dot(active, w_down, preferred_element_type=jnp.float32).astype(jnp.bfloat16),
                "tp",
            ).astype(jnp.float32)
            + down_bias
        )
        layer_rows.append(result.astype(jnp.bfloat16))
        grad_out = cotangent[batch_index]
        grad_float = grad_out.astype(jnp.float32)
        down_bias_term = jnp.sum(grad_float, axis=0)
        down_term = inner_rows(active, grad_out)
        _, gelu_pull = jax.vjp(gelu_exact, hidden)
        grad_hidden = gelu_pull(times_transposed(grad_out, w_down))[0].astype(jnp.bfloat16)
        up_bias_term = jnp.sum(grad_hidden.astype(jnp.float32), axis=0)
        up_term = inner_rows(normed_mid, grad_hidden)
        grad_normed_mid = lax.psum(
            times_transposed(grad_hidden, w_up).astype(jnp.bfloat16), "tp"
        ).astype(jnp.float32)
        _, second_pull = jax.vjp(norm_rows, middle, norm2_gain, norm2_shift)
        grad_mid_norm, second_gain_term, second_shift_term = second_pull(grad_normed_mid)
        grad_middle = grad_float + grad_mid_norm
        grad_branch = grad_middle.astype(jnp.bfloat16)
        out_bias_term = jnp.sum(grad_branch.astype(jnp.float32), axis=0)
        out_term = inner_rows(attended, grad_branch)
        grad_attended = times_transposed(grad_branch, w_out).astype(jnp.bfloat16)
        grad_heads = grad_attended.reshape(local_rows, head_count, HD)
        again = (
            jnp.einsum("qhd,khd->hqk", query_heads, key_heads, preferred_element_type=jnp.float32)
            * score_scale
        )
        again = jnp.where(visible[None], again, NEGATIVE)
        soft = jnp.exp(again - log_total)
        soft_again = soft.astype(jnp.bfloat16)
        grad_soft = jnp.einsum(
            "qhd,khd->hqk", grad_heads, value_heads, preferred_element_type=jnp.float32
        )
        inner = jnp.sum(soft * grad_soft, axis=-1, keepdims=True)
        grad_scores = (soft * (grad_soft - inner)).astype(jnp.bfloat16)
        grad_queries = (
            (
                jnp.einsum(
                    "hqk,khd->qhd", grad_scores, key_heads, preferred_element_type=jnp.float32
                )
                * score_scale
            )
            .reshape(local_rows, local_width)
            .astype(jnp.bfloat16)
        )
        key_part = (
            jnp.einsum("hqk,qhd->khd", grad_scores, query_heads, preferred_element_type=jnp.float32)
            * score_scale
        ).reshape(tree_rows, local_width)
        value_part = jnp.einsum(
            "hqk,qhd->khd", soft_again, grad_heads, preferred_element_type=jnp.float32
        ).reshape(tree_rows, local_width)
        grad_keys, grad_values = (
            lax.psum_scatter(
                key_part.astype(jnp.bfloat16), "ctx", scatter_dimension=0, tiled=True
            ).astype(jnp.float32),
            lax.psum_scatter(
                value_part.astype(jnp.bfloat16), "ctx", scatter_dimension=0, tiled=True
            ).astype(jnp.float32),
        )
        grad_keys = grad_keys.astype(jnp.bfloat16)
        grad_values = grad_values.astype(jnp.bfloat16)
        query_bias_term = jnp.sum(grad_queries.astype(jnp.float32), axis=0)
        value_bias_term = jnp.sum(grad_values.astype(jnp.float32), axis=0)
        query_term = inner_rows(normed, grad_queries)
        key_term = inner_rows(normed, grad_keys)
        value_term = inner_rows(normed, grad_values)
        grad_normed = lax.psum(
            (
                times_transposed(grad_queries, w_query)
                + times_transposed(grad_keys, w_key)
                + times_transposed(grad_values, w_value)
            ).astype(jnp.bfloat16),
            "tp",
        ).astype(jnp.float32)
        _, first_pull = jax.vjp(norm_rows, inputs, norm1_gain, norm1_shift)
        grad_in_norm, first_gain_term, first_shift_term = first_pull(grad_normed)
        input_grads.append((grad_middle + grad_in_norm).astype(jnp.bfloat16))
        head_sums = [
            head_sums[0] + query_bias_term,
            head_sums[1] + value_bias_term,
            head_sums[2] + up_bias_term,
        ]
        fresh = [
            query_term,
            key_term,
            value_term,
            out_term,
            up_term,
            down_term,
            first_gain_term,
            first_shift_term,
            second_gain_term,
            second_shift_term,
            out_bias_term,
            down_bias_term,
        ]
        running = [older + newer for older, newer in zip(running, fresh)]
    final = (
        lax.psum_scatter(
            running[0].astype(jnp.bfloat16), ("fsdp", "ctx"), scatter_dimension=0, tiled=True
        ).astype(jnp.float32),
        lax.psum_scatter(
            running[1].astype(jnp.bfloat16), ("fsdp", "ctx"), scatter_dimension=0, tiled=True
        ).astype(jnp.float32),
        lax.psum_scatter(
            running[2].astype(jnp.bfloat16), ("fsdp", "ctx"), scatter_dimension=0, tiled=True
        ).astype(jnp.float32),
        lax.psum_scatter(
            running[3].astype(jnp.bfloat16), ("fsdp", "ctx"), scatter_dimension=1, tiled=True
        ).astype(jnp.float32),
        lax.psum_scatter(
            running[4].astype(jnp.bfloat16), ("fsdp", "ctx"), scatter_dimension=0, tiled=True
        ).astype(jnp.float32),
        lax.psum_scatter(
            running[5].astype(jnp.bfloat16), ("fsdp", "ctx"), scatter_dimension=1, tiled=True
        ).astype(jnp.float32),
        lax.psum_scatter(
            running[6].astype(jnp.bfloat16), ("fsdp", "ctx"), scatter_dimension=0, tiled=True
        ).astype(jnp.float32),
        lax.psum_scatter(
            running[7].astype(jnp.bfloat16), ("fsdp", "ctx"), scatter_dimension=0, tiled=True
        ).astype(jnp.float32),
        lax.psum_scatter(
            running[8].astype(jnp.bfloat16), ("fsdp", "ctx"), scatter_dimension=0, tiled=True
        ).astype(jnp.float32),
        lax.psum_scatter(
            running[9].astype(jnp.bfloat16), ("fsdp", "ctx"), scatter_dimension=0, tiled=True
        ).astype(jnp.float32),
        lax.psum_scatter(
            running[10].astype(jnp.bfloat16), ("fsdp", "ctx"), scatter_dimension=0, tiled=True
        ).astype(jnp.float32),
        lax.psum_scatter(
            running[11].astype(jnp.bfloat16), ("fsdp", "ctx"), scatter_dimension=0, tiled=True
        ).astype(jnp.float32),
    )
    bias_totals = lax.psum((head_sums[0], head_sums[1], head_sums[2]), ("fsdp", "ctx"))
    return (
        jnp.stack(layer_rows),
        jnp.stack(input_grads),
        final[6],
        final[7],
        final[0],
        bias_totals[0],
        final[1],
        final[2],
        bias_totals[1],
        final[3],
        final[10],
        final[8],
        final[9],
        final[4],
        bias_totals[2],
        final[5],
        final[11],
    )


def solution(mesh):
    in_specs = (
        P("fsdp", "ctx", None),
        P("fsdp", "ctx"),
        P("fsdp", "ctx"),
        P("fsdp", None),
        P(),
        P(),
        P("fsdp", "tp"),
        P("tp"),
        P("fsdp", "tp"),
        P("fsdp", "tp"),
        P("tp"),
        P("tp", "fsdp"),
        P(),
        P(),
        P(),
        P("fsdp", "tp"),
        P("tp"),
        P("tp", "fsdp"),
        P(),
        P("fsdp", "ctx", None),
    )
    out_specs = (
        P("fsdp", "ctx", None),
        P("fsdp", "ctx", None),
        P(("fsdp", "ctx")),
        P(("fsdp", "ctx")),
        P(("fsdp", "ctx"), "tp"),
        P("tp"),
        P(("fsdp", "ctx"), "tp"),
        P(("fsdp", "ctx"), "tp"),
        P("tp"),
        P("tp", ("fsdp", "ctx")),
        P(("fsdp", "ctx")),
        P(("fsdp", "ctx")),
        P(("fsdp", "ctx")),
        P(("fsdp", "ctx"), "tp"),
        P("tp"),
        P("tp", ("fsdp", "ctx")),
        P(("fsdp", "ctx")),
    )
    return jax.shard_map(
        per_device, mesh=mesh, in_specs=in_specs, out_specs=out_specs, check_vma=False
    )
```

profile of v0, /device:TPU:0, one launch (start us, length us, event | category | flops | bytes accessed | tf_op | source)
XLA Modules:
  0.0 1765.6 jit_solution(16813001893812341595)
XLA Ops:
  14.5 30.9 %all-gather.17.cloned.1.call-done = bf16[2048,512]{1,0:T(8,128)(2,1)} async-done(((bf16[1024,512]{1,0:T(8,128)(2,1)}), bf16[2048,512]{1,0:T(8,128)(2,1)}) %all-gather.17.cloned.1.call-update) | async-done | bytes 2097168 | tf_op jit(solution)/shard_map/all_gather | solution.py:70
  49.2 30.9 %all-gather.11.cloned.1.call-done = bf16[2048,512]{1,0:T(8,128)(2,1)} async-done(((bf16[1024,512]{1,0:T(8,128)(2,1)}), bf16[2048,512]{1,0:T(8,128)(2,1)}) %all-gather.11.cloned.1.call-update) | async-done | bytes 2097168 | tf_op jit(solution)/shard_map/all_gather | solution.py:71
  84.4 13.3 all_gather.39
  97.6 13.4 all_gather.38
  118.4 44.0 %all-gather.19.cloned.1.call-done = bf16[2048,512]{1,0:T(8,128)(2,1)} async-done(((bf16[512,512]{1,0:T(8,128)(2,1)}), bf16[2048,512]{1,0:T(8,128)(2,1)}) %all-gather.19.cloned.1.call-update) | async-done | bytes 2097168 | tf_op jit(solution)/shard_map/all_gather | solution.py:117
  165.4 9.3 fusion.162
  174.7 8.2 fusion
  182.8 26.1 %all-gather.13.cloned.1.call-done = bf16[2048,512]{1,0:T(8,128)(2,1)} async-done(((bf16[512,512]{1,0:T(8,128)(2,1)}), bf16[2048,512]{1,0:T(8,128)(2,1)}) %all-gather.13.cloned.1.call-update) | async-done | bytes 2097168 | tf_op jit(solution)/shard_map/all_gather | solution.py:118
  208.9 8.5 fusion.127
  217.4 24.8 %all-gather.21.cloned.1.call-done = bf16[512,2048]{1,0:T(8,128)(2,1)} async-done(((bf16[512,1024]{1,0:T(8,128)(2,1)}), bf16[512,2048]{1,0:T(8,128)(2,1)}) %all-gather.21.cloned.1.call-update) | async-done | bytes 2097168 | tf_op jit(solution)/shard_map/all_gather | solution.py:72
  242.3 4.2 convolution_convert_fusion.5
  246.9 51.0 %all-reduce.15.cloned.1.call-done = bf16[512,2048]{1,0:T(8,128)(2,1)} async-done(((bf16[512,2048]{1,0:T(8,128)(2,1)}), bf16[512,2048]{1,0:T(8,128)(2,1)}) %all-reduce.15.cloned.1.call-update) | async-done | bytes 2097168 | tf_op jit(solution)/shard_map/psum | solution.py:147
  298.0 4.3 fusion.69
  312.4 4.8 fusion.123
  317.3 35.4 %all-gather.29.cloned.1.call-done = bf16[2048,512]{1,0:T(8,128)(2,1)} async-done(((bf16[512,512]{1,0:T(8,128)(2,1)}), bf16[2048,512]{1,0:T(8,128)(2,1)}) %all-gather.29.cloned.1.call-update) | async-done | bytes 2097168 | tf_op jit(solution)/shard_map/all_gather | solution.py:117
  355.6 9.5 fusion.163
  365.0 8.2 fusion.1
  373.2 26.0 %all-gather.27.cloned.1.call-done = bf16[2048,512]{1,0:T(8,128)(2,1)} async-done(((bf16[512,512]{1,0:T(8,128)(2,1)}), bf16[2048,512]{1,0:T(8,128)(2,1)}) %all-gather.27.cloned.1.call-update) | async-done | bytes 2097168 | tf_op jit(solution)/shard_map/all_gather | solution.py:118
  399.3 8.3 fusion.124
  412.6 48.8 %all-reduce.17.cloned.1.call-done = bf16[512,2048]{1,0:T(8,128)(2,1)} async-done(((bf16[512,2048]{1,0:T(8,128)(2,1)}), bf16[512,2048]{1,0:T(8,128)(2,1)}) %all-reduce.17.cloned.1.call-update) | async-done | bytes 2097168 | tf_op jit(solution)/shard_map/psum | solution.py:147
  461.4 4.5 multiply_reduce_fusion.3
  467.8 99.3 %all-gather.23.cloned.1.call-done = bf16[2048,2048]{1,0:T(8,128)(2,1)} async-done(((bf16[1024,2048]{1,0:T(8,128)(2,1)}), bf16[2048,2048]{1,0:T(8,128)(2,1)}) %all-gather.23.cloned.1.call-update) | async-done | bytes 8388624 | tf_op jit(solution)/shard_map/all_gather | solution.py:73
  567.1 8.0 fusion.142
  577.3 26.2 %multiply_convert_fusion.5 = (bf16[512,2048]{1,0:T(8,128)(2,1)}, f32[512,2048]{1,0:T(8,128)}, bf16[512,2048]{1,0:T(8,128)(2,1)}, f32[512,2048]{1,0:T(8,128)}, f32[512,2048]{1,0:T(8,128)}) fusion(f32[2048]{0:T(1024)S(1)} %copy-done.101, f32[512,2048]{1,0:T(8,128)S(1)} %fusion.142, bf16[2048,2048]{1,0:T(8,128)(2,1)S(1)} %copy-done.99, ...), kind=kOutput, calls=%fused_computation.131 | convolution fusion | flops 4442816512 | bytes 33591296 | tf_op jit(solution)/shard_map/dot_general | solution.py:154
  603.5 68.9 %all-gather.25.cloned.1.call-done = bf16[2048,2048]{1,0:T(8,128)(2,1)} async-done(((bf16[2048,1024]{1,0:T(8,128)(2,1)}), bf16[2048,2048]{1,0:T(8,128)(2,1)}) %all-gather.25.cloned.1.call-update) | async-done | bytes 8388624 | tf_op jit(solution)/shard_map/all_gather | solution.py:74
  672.5 14.2 convert_reduce_fusion.8
  686.6 10.0 convolution_convert_fusion
  696.6 12.2 convert_reduce_fusion.9
  708.8 9.9 convolution_convert_fusion.1
  719.4 85.0 %all-reduce.21.cloned.1.call-done = (bf16[512,2048]{1,0:T(8,128)(2,1)}, bf16[512,2048]{1,0:T(8,128)(2,1)}) async-done(((bf16[512,2048]{1,0:T(8,128)(2,1)}, bf16[512,2048]{1,0:T(8,128)(2,1)}), (bf16[512,2048]{1,0:T(8,128)(2,1)}, bf16[512,2048]{1,0:T(8,128)(2,1)})) %all-reduce.21.cloned.1.call-update) | async-done | bytes 4194320 | tf_op jit(solution)/shard_map/psum | solution.py:172
  804.4 6.9 fusion.37
  811.5 5.7 fusion.52
  817.3 8.8 convert_reduce_fusion.10
  829.6 4.4 fusion.70
  837.1 10.7 fusion.73
  847.9 11.3 multiply_reduce_fusion.1
  859.2 12.0 multiply_convert_fusion.1
  875.6 11.5 multiply_reduce_fusion
  887.1 11.9 multiply_convert_fusion
  908.5 6.6 convert_reduce_fusion.15
  916.7 6.4 convert_reduce_fusion.14
  926.2 4.4 fusion.169
  930.5 5.9 add_convert_fusion.3
  936.5 31.4 %reduce-scatter.11.cloned.1.call-done = bf16[512,512]{0,1:T(8,128)(2,1)} async-done(((bf16[2048,512]{0,1:T(8,128)(2,1)}), bf16[512,512]{0,1:T(8,128)(2,1)}) %reduce-scatter.11.cloned.1.call-update) | async-done | bytes 524304 | tf_op jit(solution)/shard_map/reduce_scatter | solution.py:213
  967.9 4.4 fusion.168
  972.3 40.7 %reduce-scatter.15.cloned.1.call-done = bf16[512,512]{0,1:T(8,128)(2,1)} async-done(((bf16[2048,512]{0,1:T(8,128)(2,1)}), bf16[512,512]{0,1:T(8,128)(2,1)}) %reduce-scatter.15.cloned.1.call-update) | async-done | bytes 524304 | tf_op jit(solution)/shard_map/reduce_scatter | solution.py:213
  1012.9 5.9 add_convert_fusion.4
  1019.1 9.2 convolution_convert_fusion.4
  1028.3 9.3 convolution_convert_fusion.2
  1049.6 13.8 fusion.140
  1063.4 15.7 add_convert_fusion.1
  1080.7 9.9 fusion.98
  1090.6 11.0 add_convert_fusion
  1108.8 46.7 %reduce-scatter.19.cloned.1.call-done = bf16[256,512]{1,0:T(8,128)(2,1)} async-done(((bf16[2048,512]{1,0:T(8,128)(2,1)}), bf16[256,512]{1,0:T(8,128)(2,1)}) %reduce-scatter.19.cloned.1.call-update) | async-done | bytes 262160 | tf_op jit(solution)/shard_map/reduce_scatter | solution.py:259
  1157.3 35.1 %all-reduce.6 = (f32[512]{0:T(512)}, f32[512]{0:T(512)}, f32[2048]{0:T(1024)}) all-reduce(f32[512]{0:T(512)S(1)} %add_bitcast_fusion, f32[512]{0:T(512)S(1)} %add.353, f32[2048]{0:T(1024)S(1)} %add.359), channel_id=1, replica_groups=mesh['fsdp'=2,'ctx'=4,'tp'=4] {'fsdp','ctx'}, use_global_device_ids=true, to_apply=%region_47.48 | all-reduce | flops 3072 | bytes 24576 | tf_op jit(solution)/shard_map/psum | solution.py:296
  1192.4 34.0 %reduce-scatter.23.cloned.1.call-done = bf16[256,512]{1,0:T(8,128)(2,1)} async-done(((bf16[2048,512]{1,0:T(8,128)(2,1)}), bf16[256,512]{1,0:T(8,128)(2,1)}) %reduce-scatter.23.cloned.1.call-update) | async-done | bytes 262160 | tf_op jit(solution)/shard_map/reduce_scatter | solution.py:265
  1228.2 69.2 %reduce-scatter.21.cloned.1.call-done = bf16[256,512]{1,0:T(8,128)(2,1)} async-done(((bf16[2048,512]{1,0:T(8,128)(2,1)}), bf16[256,512]{1,0:T(8,128)(2,1)}) %reduce-scatter.21.cloned.1.call-update) | async-done | bytes 262160 | tf_op jit(solution)/shard_map/reduce_scatter | solution.py:262
  1299.2 153.4 %all-reduce.19.cloned.1.call-done = (bf16[512,2048]{1,0:T(8,128)(2,1)}, bf16[512,2048]{1,0:T(8,128)(2,1)}, bf16[512,2048]{1,0:T(8,128)(2,1)}, bf16[512,2048]{1,0:T(8,128)(2,1)}) async-done(((bf16[512,2048]{1,0:T(8,128)(2,1)}, bf16[512,2048]{1,0:T(8,128)(2,1)}, bf16[512,2048]{1,0:T(8,128)(2,1)}, bf16[512,2048]{1,0:T(8,128)(2,1)}), (bf16[512,2048]{1,0:T(8,128)(2,1)}, bf16[512,2048]{1,0:T(8,128)(2,1)}, ...) | async-done | bytes 8388624 | tf_op jit(solution)/shard_map/psum | solution.py:157
  1452.6 4.7 fusion.41
  1462.6 40.6 %all-reduce.7 = (bf16[2048]{0:T(1024)(128)(2,1)S(1)}, bf16[2048]{0:T(1024)(128)(2,1)S(1)}, bf16[2048]{0:T(1024)(128)(2,1)S(1)}, bf16[2048]{0:T(1024)(128)(2,1)S(...) all-reduce(bf16[2048]{0:T(1024)(128)(2,1)S(1)} %add_convert_fusion., ...), channel_id=6, replica_groups=mesh['fsdp'=2,'ctx'=4,'tp'=4] {'fsdp','ctx'}, use_global_device_ids=true, to_apply=%region_40.41.clone | all-reduce | flops 12288 | bytes 49152
  1507.2 7.8 fusion.112
  1516.2 5.0 fusion.113
  1525.9 79.1 %reduce-scatter.27.cloned.1.call-done = bf16[256,2048]{1,0:T(8,128)(2,1)} async-done(((bf16[2048,2048]{1,0:T(8,128)(2,1)}), bf16[256,2048]{1,0:T(8,128)(2,1)}) %reduce-scatter.27.cloned.1.call-update) | async-done | bytes 1048592 | tf_op jit(solution)/shard_map/reduce_scatter | solution.py:271
  1607.9 147.7 %reduce-scatter.29.cloned.1.call-done = bf16[2048,256]{1,0:T(8,128)(2,1)} async-done(((bf16[2048,2048]{1,0:T(8,128)(2,1)}), bf16[2048,256]{1,0:T(8,128)(2,1)}) %reduce-scatter.29.cloned.1.call-update) | async-done | bytes 1048592 | tf_op jit(solution)/shard_map/reduce_scatter | solution.py:274
  (367 shorter events, 119.9 us)
Async XLA Ops:
  7.2 38.2 %all-gather.17.cloned.1.call-start = ((), (), s32[]{:S(2)}) async-start(), calls=%async_computation.13 | async-start | bytes 3145728 | tf_op jit(solution)/shard_map/all_gather | solution.py:70
  7.9 72.1 %all-gather.11.cloned.1.call-start = ((), (), s32[]{:S(2)}) async-start(), calls=%async_computation.10 | async-start | bytes 3145728 | tf_op jit(solution)/shard_map/all_gather | solution.py:71
  8.7 106.0 %all-gather.15.cloned.1.call-start = ((), (), s32[]{:S(2)}) async-start(), calls=%async_computation.12 | async-start | bytes 3145728 | tf_op jit(solution)/shard_map/all_gather | solution.py:69
  9.4 153.0 %all-gather.19.cloned.1.call-start = ((), (), s32[]{:S(2)}) async-start(), calls=%async_computation.14 | async-start | bytes 2621440 | tf_op jit(solution)/shard_map/all_gather | solution.py:117
  12.9 36.1 %copy-start.61 = (f32[512]{0:T(512)}, f32[512]{0:T(512)S(1)}, u32[]{:S(2)}) copy-start(f32[512]{0:T(512)S(1)} %broadcast_multiply_fusion.3) | copy-start | bytes 6148
  13.6 35.4 %copy-start.90 = (f32[512]{0:T(512)}, f32[512]{0:T(512)S(1)}, u32[]{:S(2)}) copy-start(f32[512]{0:T(512)S(1)} %fusion.40) | copy-start | bytes 6148
  13.7 35.4 %copy-start.68 = (f32[512]{0:T(512)}, f32[512]{0:T(512)S(1)}, u32[]{:S(2)}) copy-start(f32[512]{0:T(512)S(1)} %fusion.134) | copy-start | bytes 6148
  14.5 100.2 %copy-start.27 = (bf16[512,2048]{1,0:T(8,128)(2,1)}, bf16[512,2048]{1,0:T(8,128)(2,1)S(1)}, u32[]{:S(2)}) copy-start(bf16[512,2048]{1,0:T(8,128)(2,1)S(1)} %fusion.33) | copy-start | bytes 6291460
  14.5 65.5 %copy-start.104 = (f32[512]{0:T(512)S(1)}, f32[512]{0:T(512)}, u32[]{:S(2)}) copy-start(f32[512]{0:T(512)} %param.30) | copy-start | bytes 6148
  49.1 35.3 %copy-start.92 = (s32[2,512]{1,0:T(2,128)S(1)}, s32[2,512]{1,0:T(2,128)}, u32[]{:S(2)}) copy-start(s32[2,512]{1,0:T(2,128)} %param.21) | copy-start | bytes 12292
  49.1 48.6 %copy-start.93 = (s32[2,512]{1,0:T(2,128)S(1)}, s32[2,512]{1,0:T(2,128)}, u32[]{:S(2)}) copy-start(s32[2,512]{1,0:T(2,128)} %param.22) | copy-start | bytes 12292
  49.1 62.0 %copy-start.98 = (s32[2,7]{1,0:T(2,128)S(1)}, s32[2,7]{1,0:T(2,128)}, u32[]{:S(2)}) copy-start(s32[2,7]{1,0:T(2,128)} %param.23) | copy-start | bytes 172
  49.1 65.6 %copy-start.105 = (f32[512]{0:T(512)S(1)}, f32[512]{0:T(512)}, u32[]{:S(2)}) copy-start(f32[512]{0:T(512)} %param.27) | copy-start | bytes 6148
  49.1 159.8 %all-gather.13.cloned.1.call-start = ((), (), s32[]{:S(2)}) async-start(), calls=%async_computation.11 | async-start | bytes 2621440 | tf_op jit(solution)/shard_map/all_gather | solution.py:118
  83.7 158.5 %all-gather.21.cloned.1.call-start = ((), (), s32[]{:S(2)}) async-start(), calls=%async_computation.15 | async-start | bytes 3145728 | tf_op jit(solution)/shard_map/all_gather | solution.py:72
  84.3 213.7 %all-reduce.15.cloned.1.call-start = ((), (), s32[]{:S(2)}) async-start(), calls=%async_computation.16 | async-start | bytes 4194304 | tf_op jit(solution)/shard_map/psum | solution.py:147
  174.7 34.3 %copy-start.57 = (f32[4,512]{1,0:T(4,128)}, f32[4,512]{1,0:T(4,128)S(1)}, u32[]{:S(2)}) copy-start(f32[4,512]{1,0:T(4,128)S(1)} %get-tuple-element.86) | copy-start | bytes 24580
  182.8 34.6 %copy-start.66 = (f32[4,512]{1,0:T(4,128)}, f32[4,512]{1,0:T(4,128)S(1)}, u32[]{:S(2)}) copy-start(f32[4,512]{1,0:T(4,128)S(1)} %fusion) | copy-start | bytes 24580
  217.4 84.9 %copy-start.52 = (bf16[4,128,512]{2,1,0:T(8,128)(2,1)}, bf16[4,128,512]{2,1,0:T(8,128)(2,1)S(1)}, u32[]{:S(2)}) copy-start(bf16[4,128,512]{2,1,0:T(8,128)(2,1)S(1)} %fusion.127) | copy-start | bytes 1572868
  217.4 80.6 %copy-start.51 = (f32[2048]{0:T(1024)S(1)}, f32[2048]{0:T(1024)}, u32[]{:S(2)}) copy-start(f32[2048]{0:T(1024)} %param.32) | copy-start | bytes 24580
  246.5 106.1 %all-gather.29.cloned.1.call-start = ((), (), s32[]{:S(2)}) async-start(), calls=%async_computation.20 | async-start | bytes 2621440 | tf_op jit(solution)/shard_map/all_gather | solution.py:117
  246.9 65.5 %copy-start.63 = (f32[512]{0:T(512)}, f32[512]{0:T(512)S(1)}, u32[]{:S(2)}) copy-start(f32[512]{0:T(512)S(1)} %broadcast_multiply_fusion.1) | copy-start | bytes 6148
  306.7 92.5 %all-gather.27.cloned.1.call-start = ((), (), s32[]{:S(2)}) async-start(), calls=%async_computation.19 | async-start | bytes 2621440 | tf_op jit(solution)/shard_map/all_gather | solution.py:118
  310.5 150.9 %all-reduce.17.cloned.1.call-start = ((), (), s32[]{:S(2)}) async-start(), calls=%async_computation.21 | async-start | bytes 4194304 | tf_op jit(solution)/shard_map/psum | solution.py:147
  373.2 35.2 %copy-start.100 = (bf16[512,2048]{1,0:T(8,128)(2,1)S(1)}, bf16[512,2048]{1,0:T(8,128)(2,1)}, u32[]{:S(2)}) copy-start(bf16[512,2048]{1,0:T(8,128)(2,1)} %all-gather.21.cloned.1.call-done) | copy-start | bytes 6291460
  411.0 156.0 %all-gather.23.cloned.1.call-start = ((), (), s32[]{:S(2)}) async-start(), calls=%async_computation.17 | async-start | bytes 12582912 | tf_op jit(solution)/shard_map/all_gather | solution.py:73
  411.8 260.7 %all-gather.25.cloned.1.call-start = ((), (), s32[]{:S(2)}) async-start(), calls=%async_computation.18 | async-start | bytes 12582912 | tf_op jit(solution)/shard_map/all_gather | solution.py:74
  412.3 392.0 %all-reduce.21.cloned.1.call-start = ((), (), s32[]{:S(2)}) async-start(), calls=%async_computation.33 | async-start | bytes 8388608 | tf_op jit(solution)/shard_map/psum | solution.py:172
  465.9 101.2 %copy-start.56 = (f32[2048]{0:T(1024)S(1)}, f32[2048]{0:T(1024)}, u32[]{:S(2)}) copy-start(f32[2048]{0:T(1024)} %param.33) | copy-start | bytes 24580
  465.9 101.2 %copy-start.102 = (f32[2048]{0:T(1024)S(1)}, f32[2048]{0:T(1024)}, u32[]{:S(2)}) copy-start(f32[2048]{0:T(1024)} %param.34) | copy-start | bytes 24580
  465.9 351.3 %copy-start.59 = (f32[512]{0:T(512)}, f32[512]{0:T(512)S(1)}, u32[]{:S(2)}) copy-start(f32[512]{0:T(512)S(1)} %get-tuple-element.104) | copy-start | bytes 6148
  467.8 349.4 %copy-start.74 = (f32[512]{0:T(512)}, f32[512]{0:T(512)S(1)}, u32[]{:S(2)}) copy-start(f32[512]{0:T(512)S(1)} %fusion.137) | copy-start | bytes 6148
  467.8 109.5 %copy-start.101 = (f32[2048]{0:T(1024)S(1)}, f32[2048]{0:T(1024)}, u32[]{:S(2)}) copy-start(f32[2048]{0:T(1024)} %param.36) | copy-start | bytes 24580
  567.0 10.2 copy-start.3
  567.1 10.2 copy-start.13
  567.1 10.2 copy-start.99
  686.6 10.0 copy-start.16
  686.6 10.0 copy-start.110
  718.7 207.5 %reduce-scatter.13.cloned.1.call-start = ((), (), s32[]{:S(2)}) async-start(), calls=%async_computation.23 | async-start | bytes 2621440 | tf_op jit(solution)/shard_map/reduce_scatter | solution.py:216
  811.5 18.1 %slice-start = ((s8[16777216]{0:T(1024)(128)(4,1)}), s8[4194304]{0:T(1024)(128)(4,1)S(1)}, s32[]{:S(2)}) async-start(s8[16777216]{0:T(1024)(128)(4,1)} %bitcast.329), calls=%async_computation.34 | async-start | bytes 8388608
  811.5 18.1 %slice-start.1 = ((s8[16777216]{0:T(1024)(128)(4,1)}), s8[4194304]{0:T(1024)(128)(4,1)S(1)}, s32[]{:S(2)}) async-start(s8[16777216]{0:T(1024)(128)(4,1)} %bitcast.329), calls=%async_computation.35 | async-start | bytes 8388608
  817.3 12.3 slice-start.2
  817.3 12.3 slice-start.3
  834.0 96.5 %reduce-scatter.17.cloned.1.call-start = ((), (), s32[]{:S(2)}) async-start(), calls=%async_computation.25 | async-start | bytes 2621440 | tf_op jit(solution)/shard_map/reduce_scatter | solution.py:216
  837.1 10.8 copy-start.43
  847.8 120.1 %reduce-scatter.11.cloned.1.call-start = ((), (), s32[]{:S(2)}) async-start(), calls=%async_computation.22 | async-start | bytes 2621440 | tf_op jit(solution)/shard_map/reduce_scatter | solution.py:213
  859.2 12.0 copy-start.41
  875.5 137.4 %reduce-scatter.15.cloned.1.call-start = ((), (), s32[]{:S(2)}) async-start(), calls=%async_computation.24 | async-start | bytes 2621440 | tf_op jit(solution)/shard_map/reduce_scatter | solution.py:213
  887.1 12.0 copy-start.42
  903.5 203.5 %reduce-scatter.25.cloned.1.call-start = ((), (), s32[]{:S(2)}) async-start(), calls=%async_computation.29 | async-start | bytes 2359296 | tf_op jit(solution)/shard_map/reduce_scatter | solution.py:268
  908.0 247.5 %reduce-scatter.19.cloned.1.call-start = ((), (), s32[]{:S(2)}) async-start(), calls=%async_computation.26 | async-start | bytes 2359296 | tf_op jit(solution)/shard_map/reduce_scatter | solution.py:259
  926.1 300.4 %reduce-scatter.23.cloned.1.call-start = ((), (), s32[]{:S(2)}) async-start(), calls=%async_computation.28 | async-start | bytes 2359296 | tf_op jit(solution)/shard_map/reduce_scatter | solution.py:265
  936.5 361.0 %reduce-scatter.21.cloned.1.call-start = ((), (), s32[]{:S(2)}) async-start(), calls=%async_computation.27 | async-start | bytes 2359296 | tf_op jit(solution)/shard_map/reduce_scatter | solution.py:262
  972.3 46.8 %copy-start.107 = (bf16[512,2048]{1,0:T(8,128)(2,1)S(1)}, bf16[512,2048]{1,0:T(8,128)(2,1)}, u32[]{:S(2)}) copy-start(bf16[512,2048]{1,0:T(8,128)(2,1)} %get-tuple-element.64) | copy-start | bytes 6291460
  1018.8 433.8 %all-reduce.19.cloned.1.call-start = ((), (), s32[]{:S(2)}) async-start(), calls=%async_computation.32 | async-start | bytes 16777216 | tf_op jit(solution)/shard_map/psum | solution.py:157
  1048.9 14.5 copy-start.60
  1048.9 14.5 copy-start.75
  1048.9 556.1 %reduce-scatter.27.cloned.1.call-start = ((), (), s32[]{:S(2)}) async-start(), calls=%async_computation.30 | async-start | bytes 9437184 | tf_op jit(solution)/shard_map/reduce_scatter | solution.py:271
  1049.6 13.8 copy-start.6
  1079.1 676.5 %reduce-scatter.29.cloned.1.call-start = ((), (), s32[]{:S(2)}) async-start(), calls=%async_computation.31 | async-start | bytes 9437184 | tf_op jit(solution)/shard_map/reduce_scatter | solution.py:274
  1458.5 48.5 %copy-start.15 = (bf16[512,2048]{1,0:T(8,128)(2,1)S(1)}, bf16[512,2048]{1,0:T(8,128)(2,1)}, u32[]{:S(2)}) copy-start(bf16[512,2048]{1,0:T(8,128)(2,1)} %all-reduce.15.cloned.1.call-done) | copy-start | bytes 6291460
  1458.6 48.5 %copy-start.65 = (f32[2048]{0:T(1024)S(1)}, f32[2048]{0:T(1024)}, u32[]{:S(2)}) copy-start(f32[2048]{0:T(1024)} %param.38) | copy-start | bytes 24580
  1458.6 48.5 %copy-start.73 = (f32[512]{0:T(512)S(1)}, f32[512]{0:T(512)}, u32[]{:S(2)}) copy-start(f32[512]{0:T(512)} %copy-done.72) | copy-start | bytes 6148
  1458.6 48.5 %copy-start.89 = (f32[512]{0:T(512)S(1)}, f32[512]{0:T(512)}, u32[]{:S(2)}) copy-start(f32[512]{0:T(512)} %copy-done.88) | copy-start | bytes 6148
  (76 other events, 394.3 us)
Sparse Core Ops, SparseCore 0:
  9.5 35.8 all-gather.16
  46.9 33.0 all-gather.10
  81.6 33.0 all-gather.14
  116.7 45.6 all-gather.18
  164.4 44.4 all-gather.12
  210.3 31.8 all-gather.20
  246.6 51.3 all-reduce.14
  306.8 45.7 all-gather.28
  354.8 44.4 all-gather.26
  411.1 50.1 all-reduce.16
  462.9 104.0 all-gather.22
  568.4 103.9 all-gather.24
  718.8 85.5 all-reduce.20
  834.1 43.7 reduce-scatter.12
  880.1 42.8 reduce-scatter.16
  925.1 42.8 reduce-scatter.10
  970.1 42.8 reduce-scatter.14
  1016.3 68.1 reduce-scatter.24
  1088.0 67.4 reduce-scatter.18
  1158.9 67.5 reduce-scatter.22
  1230.0 67.3 reduce-scatter.20
  1300.7 151.8 all-reduce.18
  1456.2 148.7 reduce-scatter.26
  1608.6 146.9 reduce-scatter.28
where the time goes:
time: 1770 us
  waiting for transfers between devices  1180 us (67%)
  matrix products  317 us (18%)
  other arithmetic  126 us (7%)
  blocking collectives  102 us (6%)
  local copies, waits for them, and re-layouts  21.5 us (1%)
    psum x1, waiting for transfers between devices, per_device(): lax.psum(jnp.dot(active, w_down, preferred_element_type=jnp.float32).asty...  153 us
    reduce_scatter x1, waiting for transfers between devices, per_device(): lax.psum_scatter(running[5].astype(jnp.bfloat16), ('fsdp', 'ctx'), scatte...  148 us
    psum x2, waiting for transfers between devices, per_device(): lax.psum(jnp.dot(attended, w_out, preferred_element_type=jnp.float32).ast...  99.8 us
    all_gather x1, waiting for transfers between devices, per_device(): lax.all_gather(up_weight, 'fsdp', axis=0, tiled=True)  99.3 us
    psum x1, waiting for transfers between devices, per_device(): lax.psum(times_transposed(grad_hidden, w_up).astype(jnp.bfloat16), 'tp')  85 us
    all_gather x2, waiting for transfers between devices, per_device(): lax.all_gather(keys_local, 'ctx', axis=0, tiled=True)  79.4 us
    dot_general x12, matrix products, inner_rows(): lax.dot_general(left, right, (((0,), (0,)), ((), ())), preferred_element_...  79.2 us
    reduce_scatter x1, waiting for transfers between devices, per_device(): lax.psum_scatter(running[4].astype(jnp.bfloat16), ('fsdp', 'ctx'), scatte...  79.1 us
  transfers between devices with their start and end apart: 24, of which 21 were waited for; matrix products, arithmetic and copies ran while one was open for 20% of the time, Pallas kernels for 0%

commit v1 on v0

v1 whole, which is shorter than its diff:
```python
import math
from functools import partial

import jax
import jax.numpy as jnp
from jax import lax
from jax.experimental import pallas as pl
from jax.experimental.pallas import tpu as pltpu
from jax.sharding import PartitionSpec as P

HD = 128
RUN = 64
TILE = 256
SCALE = 1.0 / math.sqrt(HD)
SCALE2 = SCALE * math.log2(math.e)
NEG = -1e30
EPS = 1e-05
F32 = jnp.float32
BF16 = jnp.bfloat16


def nn(a, b):
    return lax.dot_general(a, b, (((1,), (0,)), ((), ())), preferred_element_type=F32)


def nt(a, b):
    return lax.dot_general(a, b, (((1,), (1,)), ((), ())), preferred_element_type=F32)


def tn(a, b):
    return lax.dot_general(a, b, (((0,), (0,)), ((), ())), preferred_element_type=F32)


def seg_of(pos,starts_ref,t,nseg):
    s=jnp.zeros_like(pos)
    for i in range(1,nseg): s=s+(pos>=starts_ref[t,i]).astype(jnp.int32)
    return s
def path_of(seg,path_ref,t,nseg):
    p=jnp.zeros_like(seg)
    for i in range(nseg): p=jnp.where(seg==i,path_ref[t,i],p)
    return p

def fwd_kernel(nsrc,place,starts,path,code,*refs):
    ins=refs[:nsrc]; outs=refs[nsrc:2*nsrc]; lse_ref=refs[2*nsrc]
    qs,ks,vs,os,kbit,qpath,m_s,l_s,acc_s=refs[2*nsrc+1:]
    t=pl.program_id(0)
    local=ins[0].shape[1]; per=local//RUN; rows=nsrc*local; n=rows//TILE
    nseg=path.shape[1]
    for s in range(nsrc):
        for j in range(per):
            d=pl.multiple_of(place[t,s*per+j]*RUN,RUN)
            blk=ins[s][0,j*RUN:(j+1)*RUN,:]
            qs[pl.ds(d,RUN),:]=blk[:,0:HD]; ks[pl.ds(d,RUN),:]=blk[:,HD:2*HD]; vs[pl.ds(d,RUN),:]=blk[:,2*HD:]
    pos=lax.broadcasted_iota(jnp.int32,(rows,HD),0)
    kbit[...]=jnp.left_shift(1,seg_of(pos,starts,t,nseg))
    qpos=lax.broadcasted_iota(jnp.int32,(n,TILE),0)*TILE+lax.broadcasted_iota(jnp.int32,(n,TILE),1)
    qpath[...]=path_of(seg_of(qpos,starts,t,nseg),path,t,nseg)
    def qloop(qi,_):
        q0=pl.multiple_of(qi*TILE,TILE)
        m_s[...]=jnp.full_like(m_s,NEG); l_s[...]=jnp.zeros_like(l_s); acc_s[...]=jnp.zeros_like(acc_s)
        qt=qs[pl.ds(q0,TILE),:]
        qp=qpath[pl.ds(qi,1),:]
        def kloop(ki,_):
            k0=pl.multiple_of(ki*TILE,TILE)
            c=code[t,qi*n+ki]
            def step(masked):
                sT=nt(ks[pl.ds(k0,TILE),:],qt)
                if masked:
                    kb=kbit[pl.ds(k0,TILE),:]
                    kb=jnp.concatenate([kb]*(TILE//HD),axis=1)
                    diff=(q0-k0)+lax.broadcasted_iota(jnp.int32,(TILE,TILE),1)-lax.broadcasted_iota(jnp.int32,(TILE,TILE),0)
                    vis=((kb&qp)!=0)&(diff>=0)
                    sT=jnp.where(vis,sT,NEG)
                m0=m_s[...]
                m1=jnp.maximum(m0,jnp.max(sT,axis=0,keepdims=True))
                pT=jnp.exp2((sT-m1)*SCALE2)
                al=jnp.exp2((m0-m1)*SCALE2)
                l_s[...]=l_s[...]*al+jnp.sum(pT,axis=0,keepdims=True)
                acc_s[...]=acc_s[...]*al+tn(vs[pl.ds(k0,TILE),:],pT.astype(BF16))
                m_s[...]=m1
            @pl.when(c==2)
            def _(): step(False)
            @pl.when(c==1)
            def _(): step(True)
            return 0
        lax.fori_loop(0,qi+1,kloop,0)
        l=l_s[...]
        os[pl.ds(q0,TILE),:]=jnp.transpose(acc_s[...]/l).astype(BF16)
        lse_ref[0,pl.ds(qi,1),:]=m_s[...]*SCALE2+jnp.log2(l)
        return 0
    lax.fori_loop(0,n,qloop,0)
    for s in range(nsrc):
        for j in range(per):
            d=pl.multiple_of(place[t,s*per+j]*RUN,RUN)
            outs[s][0,j*RUN:(j+1)*RUN,:]=os[pl.ds(d,RUN),:]

def attention_fwd(tables,parts):
    place,starts,path,code=tables
    nsrc=len(parts); T,local,_=parts[0].shape; rows=nsrc*local; n=rows//TILE
    bs=lambda w: pl.BlockSpec((1,local,w),lambda t,*_:(t,0,0))
    return pl.pallas_call(partial(fwd_kernel,nsrc),
        grid_spec=pltpu.PrefetchScalarGridSpec(num_scalar_prefetch=4,grid=(T,),
            in_specs=[bs(3*HD)]*nsrc,
            out_specs=[bs(HD)]*nsrc+[pl.BlockSpec((1,n,TILE),lambda t,*_:(t,0,0))],
            scratch_shapes=[pltpu.VMEM((rows,HD),BF16)]*4+[pltpu.VMEM((rows,HD),jnp.int32),pltpu.VMEM((n,TILE),jnp.int32),
               pltpu.VMEM((1,TILE),F32),pltpu.VMEM((1,TILE),F32),pltpu.VMEM((HD,TILE),F32)]),
        out_shape=[jax.ShapeDtypeStruct((T,local,HD),BF16)]*nsrc+[jax.ShapeDtypeStruct((T,n,TILE),F32)],
        cost_estimate=pl.CostEstimate(flops=T*rows*rows*HD*2,bytes_accessed=T*rows*HD*8,transcendentals=T*rows*rows//2),
        name="tree_attention")(place,starts,path,code,*parts)

def bwd_kernel(nsrc,place,starts,path,code,*refs):
    ins=refs[:nsrc]; oin=refs[nsrc:2*nsrc]; gin=refs[2*nsrc:3*nsrc]; lse_ref=refs[3*nsrc]
    outs=refs[3*nsrc+1:4*nsrc+1]
    qs,ks,vs,gs,os,kbit,qpath,dsum,dq,dk,dv,sorted_out=refs[4*nsrc+1:]
    t=pl.program_id(0)
    local=ins[0].shape[1]; per=local//RUN; rows=nsrc*local; n=rows//TILE
    nseg=path.shape[1]
    for s in range(nsrc):
        for j in range(per):
            d=pl.multiple_of(place[t,s*per+j]*RUN,RUN)
            blk=ins[s][0,j*RUN:(j+1)*RUN,:]
            qs[pl.ds(d,RUN),:]=blk[:,0:HD]; ks[pl.ds(d,RUN),:]=blk[:,HD:2*HD]; vs[pl.ds(d,RUN),:]=blk[:,2*HD:]
            gs[pl.ds(d,RUN),:]=gin[s][0,j*RUN:(j+1)*RUN,:]; os[pl.ds(d,RUN),:]=oin[s][0,j*RUN:(j+1)*RUN,:]
    pos=lax.broadcasted_iota(jnp.int32,(rows,HD),0)
    kbit[...]=jnp.left_shift(1,seg_of(pos,starts,t,nseg))
    qpos=lax.broadcasted_iota(jnp.int32,(n,TILE),0)*TILE+lax.broadcasted_iota(jnp.int32,(n,TILE),1)
    qpath[...]=path_of(seg_of(qpos,starts,t,nseg),path,t,nseg)
    def dloop(qi,_):
        q0=pl.multiple_of(qi*TILE,TILE)
        prod=gs[pl.ds(q0,TILE),:].astype(F32)*os[pl.ds(q0,TILE),:].astype(F32)
        dsum[pl.ds(qi,1),:]=jnp.sum(jnp.transpose(prod),axis=0,keepdims=True)
        return 0
    lax.fori_loop(0,n,dloop,0)
    dq[...]=jnp.zeros_like(dq)
    def kloop(ki,_):
        k0=pl.multiple_of(ki*TILE,TILE)
        kt=ks[pl.ds(k0,TILE),:]; vt=vs[pl.ds(k0,TILE),:]
        dk[...]=jnp.zeros_like(dk); dv[...]=jnp.zeros_like(dv)
        def qloop(qi,_):
            q0=pl.multiple_of(qi*TILE,TILE)
            c=code[t,qi*n+ki]
            def step(masked):
                qt=qs[pl.ds(q0,TILE),:]; gt=gs[pl.ds(q0,TILE),:]
                sT=nt(kt,qt)
                dpT=nt(vt,gt)
                pT=jnp.exp2(sT*SCALE2-lse_ref[0,pl.ds(qi,1),:])
                if masked:
                    kb=kbit[pl.ds(k0,TILE),:]
                    kb=jnp.concatenate([kb]*(TILE//HD),axis=1)
                    qp=qpath[pl.ds(qi,1),:]
                    diff=(q0-k0)+lax.broadcasted_iota(jnp.int32,(TILE,TILE),1)-lax.broadcasted_iota(jnp.int32,(TILE,TILE),0)
                    vis=((kb&qp)!=0)&(diff>=0)
                    pT=jnp.where(vis,pT,0.0)
                dsT=(pT*(dpT-dsum[pl.ds(qi,1),:])).astype(BF16)
                dv[...]+=nn(pT.astype(BF16),gt)
                dk[...]+=nn(dsT,qt)
                dq[pl.ds(q0,TILE),:]+=tn(dsT,kt)
            @pl.when(c==2)
            def _(): step(False)
            @pl.when(c==1)
            def _(): step(True)
            return 0
        lax.fori_loop(ki,n,qloop,0)
        sorted_out[pl.ds(k0,TILE),HD:2*HD]=(dk[...]*SCALE).astype(BF16)
        sorted_out[pl.ds(k0,TILE),2*HD:]=dv[...].astype(BF16)
        return 0
    lax.fori_loop(0,n,kloop,0)
    sorted_out[:,0:HD]=(dq[...]*SCALE).astype(BF16)
    for s in range(nsrc):
        for j in range(per):
            d=pl.multiple_of(place[t,s*per+j]*RUN,RUN)
            outs[s][0,j*RUN:(j+1)*RUN,:]=sorted_out[pl.ds(d,RUN),:]

def attention_bwd(tables,parts,oparts,gparts,lse):
    place,starts,path,code=tables
    nsrc=len(parts); T,local,_=parts[0].shape; rows=nsrc*local; n=rows//TILE
    bs=lambda w: pl.BlockSpec((1,local,w),lambda t,*_:(t,0,0))
    return pl.pallas_call(partial(bwd_kernel,nsrc),
        grid_spec=pltpu.PrefetchScalarGridSpec(num_scalar_prefetch=4,grid=(T,),
            in_specs=[bs(3*HD)]*nsrc+[bs(HD)]*(2*nsrc)+[pl.BlockSpec((1,n,TILE),lambda t,*_:(t,0,0))],
            out_specs=[bs(3*HD)]*nsrc,
            scratch_shapes=[pltpu.VMEM((rows,HD),BF16)]*5+[pltpu.VMEM((rows,HD),jnp.int32),pltpu.VMEM((n,TILE),jnp.int32),
               pltpu.VMEM((n,TILE),F32),pltpu.VMEM((rows,HD),F32),pltpu.VMEM((TILE,HD),F32),pltpu.VMEM((TILE,HD),F32),
               pltpu.VMEM((rows,3*HD),BF16)]),
        out_shape=[jax.ShapeDtypeStruct((T,local,3*HD),BF16)]*nsrc,
        cost_estimate=pl.CostEstimate(flops=T*rows*rows*HD*5,bytes_accessed=T*rows*HD*20,transcendentals=T*rows*rows//2),
        name="tree_attention_back")(place,starts,path,code,*parts,*oparts,*gparts,lse)


def tree_tables(place, starts, parent, rows):
    labels = jnp.arange(parent.shape[1], dtype=jnp.int32)
    second = jnp.sum(jnp.where(parent[:, :, None] == labels, parent[:, None, :], 0), axis=2)
    path = (1 << labels)[None] | (1 << parent) | (1 << second)
    tiles = rows // TILE
    first_row = jnp.arange(tiles, dtype=jnp.int32)[None, :, None] * TILE
    low = jnp.sum((first_row >= starts[:, None, :]).astype(jnp.int32), axis=2) - 1
    high = jnp.sum((first_row + TILE - 1 >= starts[:, None, :]).astype(jnp.int32), axis=2) - 1
    inside = (labels >= low[:, :, None]) & (labels <= high[:, :, None])
    see = ((path[:, :, None] >> labels) & 1) == 1
    pair = inside[:, :, None, :, None] & inside[:, None, :, None, :]
    some = jnp.any(pair & see[:, None, None], axis=(3, 4))
    every = jnp.all((~pair) | see[:, None, None], axis=(3, 4))
    query = jnp.arange(tiles)[:, None]
    key = jnp.arange(tiles)[None, :]
    code = jnp.where((key > query) | ~some, 0, jnp.where(every & (key < query), 2, 1))
    return (
        place.astype(jnp.int32),
        starts.astype(jnp.int32),
        path.astype(jnp.int32),
        code.astype(jnp.int32).reshape(-1, tiles * tiles),
    )


def hypercube(n):
    bits = n.bit_length() - 1
    order = [sum(((r >> b) & 1) << (bits - 1 - b) for b in range(bits)) for r in range(n)]
    return bits, order


def first_norm_kernel(pieces, quarter, chunk, x_ref, dy_ref, gain_ref, shift_ref, n_ref, x0_ref, dyr_ref):
    width = x_ref.shape[2]
    part = width // pieces
    x = x_ref[0].astype(F32)
    mean = jnp.mean(x, axis=1, keepdims=True)
    spread = jnp.mean((x - mean) * (x - mean), axis=1, keepdims=True)
    scale = lax.rsqrt(spread + EPS)
    for k in range(pieces):
        here = slice(k * part, (k + 1) * part)
        there = pl.ds(pl.multiple_of(chunk[k] * part, part), part)
        xk = x_ref[0, :, there]
        n_ref[0, :, here] = (
            (xk.astype(F32) - mean) * scale * gain_ref[:, here] + shift_ref[:, here]
        ).astype(BF16)
        dyr_ref[0, :, here] = dy_ref[0, :, there]

        @pl.when(pl.program_id(1) == 0)
        def _():
            x0_ref[0, :, here] = xk


def first_norm(quarter, chunk, tokens, cotangent, gain, shift):
    trees, rows, width = tokens.shape
    parts = quarter.shape[0]
    block = (1, rows // parts, width)
    come = pl.BlockSpec(block, lambda i, r, q, c: (i, q[r], 0))
    go = pl.BlockSpec(block, lambda i, r, q, c: (i, r, 0))
    row = pl.BlockSpec((1, width), lambda i, r, q, c: (0, 0))
    return pl.pallas_call(
        partial(first_norm_kernel, chunk.shape[0]),
        grid_spec=pltpu.PrefetchScalarGridSpec(
            num_scalar_prefetch=2,
            grid=(trees, parts),
            in_specs=[come, come, row, row],
            out_specs=[go, pl.BlockSpec(block, lambda i, r, q, c: (i, 0, 0)), go],
        ),
        out_shape=[
            jax.ShapeDtypeStruct((trees, rows, width), BF16),
            jax.ShapeDtypeStruct((trees, rows // parts, width), BF16),
            jax.ShapeDtypeStruct((trees, rows, width), BF16),
        ],
        cost_estimate=pl.CostEstimate(
            flops=10 * tokens.size, bytes_accessed=8 * tokens.size, transcendentals=0
        ),
        name="first_norm",
    )(quarter, chunk, tokens, cotangent, gain, shift)


def replace_kernel(pieces, quarter, chunk, x_ref, o_ref):
    part = x_ref.shape[1] // pieces
    for k in range(pieces):
        there = pl.ds(pl.multiple_of(chunk[k] * part, part), part)
        o_ref[:, there] = x_ref[:, k * part : (k + 1) * part]


def replace(quarter, chunk, value):
    rows, width = value.shape
    parts = quarter.shape[0]
    block = (rows // parts, width)
    return pl.pallas_call(
        partial(replace_kernel, chunk.shape[0]),
        grid_spec=pltpu.PrefetchScalarGridSpec(
            num_scalar_prefetch=2,
            grid=(parts,),
            in_specs=[pl.BlockSpec(block, lambda r, q, c: (r, 0))],
            out_specs=pl.BlockSpec(block, lambda r, q, c: (q[r], 0)),
        ),
        out_shape=jax.ShapeDtypeStruct((rows, width), value.dtype),
        cost_estimate=pl.CostEstimate(flops=0, bytes_accessed=4 * value.size, transcendentals=0),
        name="replace",
    )(quarter, chunk, value)


def per_device(
    sizes,
    tokens,
    tree_position,
    segment,
    parent_table,
    norm1_gain,
    norm1_shift,
    query_weight,
    query_bias,
    key_weight,
    value_weight,
    value_bias,
    out_weight,
    out_bias,
    norm2_gain,
    norm2_shift,
    up_weight,
    up_bias,
    down_weight,
    down_bias,
    cotangent,
):
    n_f, n_c, n_t = sizes["fsdp"], sizes["ctx"], sizes["tp"]
    f, c, t = (lax.axis_index(name) for name in ("fsdp", "ctx", "tp"))
    trees, rows, width = tokens.shape
    part = width // n_f
    local_width = query_weight.shape[1]
    heads = local_width // HD
    mine = heads // n_c
    bits, order = hypercube(n_t)
    quarter_rows = rows // n_t

    def shift_f(v, k):
        return lax.ppermute(v, "fsdp", [(i, (i + k) % n_f) for i in range(n_f)])

    def shift_c(v, k):
        return lax.ppermute(v, "ctx", [(i, (i + k) % n_c) for i in range(n_c)])

    def flip_t(v, b):
        return lax.ppermute(v, "tp", [(i, i ^ (1 << b)) for i in range(n_t)])

    def pieces_of(v):
        return [v] + [shift_f(v, -k) for k in range(1, n_f)]

    def sum_rows(v):
        for b in range(bits):
            half = v.shape[0] // 2
            come = flip_t(v[half:].astype(BF16), b)
            v = v[:half].astype(F32) + come.astype(F32)
        return v

    def all_rows(v):
        for b in reversed(range(bits)):
            v = jnp.concatenate([v, flip_t(v, b)], axis=0)
        return v

    quarter = jnp.stack([t ^ r for r in order]).astype(jnp.int32)
    chunk = jnp.stack([(f + k) % n_f for k in range(n_f)]).astype(jnp.int32)

    def roll_in(v):
        return jnp.concatenate(
            [lax.dynamic_slice_in_dim(v, chunk[k] * part, part, axis=-1) for k in range(n_f)], axis=-1
        )

    vectors = roll_in(
        jnp.stack([norm1_gain, norm1_shift, norm2_gain, norm2_shift, out_bias, down_bias])
    )
    gain1, shift1, gain2, shift2, bias_out, bias_down = (vectors[i : i + 1] for i in range(6))

    def by_head(q, k, v):
        stacked = jnp.stack([a.reshape(a.shape[0], heads, HD) for a in (q, k, v)], axis=2)
        doubled = jnp.concatenate([stacked, stacked], axis=1)
        turned = lax.dynamic_slice_in_dim(doubled, c * mine, heads, axis=1)
        return turned.reshape(q.shape[0], heads * 3 * HD)

    w_qkv = pieces_of(by_head(query_weight, key_weight, value_weight))
    w_out = jnp.concatenate([out_weight, out_weight], axis=0)
    w_out = pieces_of(lax.dynamic_slice_in_dim(w_out, c * mine * HD, local_width, axis=0))
    w_up = pieces_of(up_weight)
    w_down = pieces_of(down_weight)
    bias_qkv = by_head(query_bias[None], jnp.zeros_like(query_bias)[None], value_bias[None])

    n_seg = parent_table.shape[1]

    def relative(v):
        blocks = v.reshape(trees, n_t, quarter_rows)
        return jnp.concatenate(
            [lax.dynamic_slice_in_dim(blocks, quarter[r], 1, axis=1) for r in range(n_t)], axis=1
        ).reshape(trees, rows)

    places = relative(tree_position)[:, ::RUN] // RUN
    ahead = jnp.sum(
        (segment[:, None, :] < jnp.arange(n_seg, dtype=jnp.int32)[None, :, None]).astype(jnp.int32), axis=2
    )
    info = jnp.concatenate([places, ahead], axis=1)
    infos = [info] + [shift_c(info, k) for k in range(1, n_c)]
    runs = places.shape[1]
    place = jnp.concatenate([v[:, :runs] for v in infos], axis=1)
    starts = sum(v[:, runs:] for v in infos)
    tables = tree_tables(place, starts, parent_table, n_c * rows)

    normed, inputs0, dy = first_norm(quarter, chunk, tokens, cotangent, gain1, shift1)

    def cols(v, k):
        return v[:, k * part : (k + 1) * part]

    def times(v, pieces):
        return sum(nn(cols(v, k), pieces[k]) for k in range(n_f))

    def times_back(v, pieces):
        return sum(nt(cols(v, k), pieces[k]) for k in range(n_f))

    def wide(v, pieces):
        return jnp.concatenate([nn(v, p) for p in pieces], axis=1)

    def wide_back(v, pieces):
        return jnp.concatenate([nt(v, p) for p in pieces], axis=1)

    def to_heads(v, width_each):
        span = mine * width_each
        return [v[:, :span]] + [shift_c(v[:, k * span : (k + 1) * span], k) for k in range(1, n_c)]

    def from_heads(parts):
        return [parts[0]] + [shift_c(parts[k], -k) for k in range(1, n_c)]

    def absolute(parts):
        doubled = jnp.stack(parts + parts)
        turned = lax.dynamic_slice_in_dim(doubled, (n_c - c) % n_c, n_c, axis=0)
        return jnp.concatenate([turned[k] for k in range(n_c)], axis=1)

    kept = []
    for i in range(trees):
        table = tuple(v[i : i + 1] for v in tables)
        qkv = (times(normed[i], w_qkv) + bias_qkv).astype(BF16)
        parts = to_heads(qkv, 3 * HD)
        parts = [v[None] for v in parts]
        *attended_parts, lse = attention_fwd(table, parts)
        attended = from_heads([v[0] for v in attended_parts])
        attended_here = jnp.concatenate(attended, axis=1)
        x0 = inputs0[i].astype(F32)
        middle = x0 + sum_rows(wide(attended_here, w_out)) + bias_out
        mean = jnp.mean(middle, axis=1, keepdims=True)
        spread = jnp.mean((middle - mean) * (middle - mean), axis=1, keepdims=True)
        rstd = lax.rsqrt(spread + EPS)
        unit = (middle - mean) * rstd
        normed_mid = all_rows((unit * gain2 + shift2).astype(BF16))
        kept.append((table, parts, attended_parts, lse, attended, x0, middle, unit, rstd, normed_mid))

    results = []
    back = []
    for i in range(trees):
        table, parts, attended_parts, lse, attended, x0, middle, unit, rstd, normed_mid = kept[i]
        hidden = times(normed_mid, w_up) + up_bias[None]
        cdf = 0.5 * (1.0 + lax.erf(hidden * math.sqrt(0.5)))
        slope = cdf + hidden * (jnp.exp(-0.5 * hidden * hidden) * (1.0 / math.sqrt(2.0 * math.pi)))
        active = (hidden * cdf).astype(BF16)
        grad_hidden = (times_back(dy[i], w_down) * slope).astype(BF16)
        grad_mid = sum_rows(wide_back(grad_hidden, w_up))
        g = grad_mid * gain2
        moved = rstd * (
            g - jnp.mean(g, axis=1, keepdims=True) - unit * jnp.mean(g * unit, axis=1, keepdims=True)
        )
        grad_middle = dy[i, :quarter_rows].astype(F32) + moved
        branch0 = grad_middle.astype(BF16)
        branch = all_rows(branch0)
        result = middle + sum_rows(wide(active, w_down)) + bias_down
        results.append(all_rows(result.astype(BF16)))
        back.append(
            dict(
                active=active,
                grad_hidden=grad_hidden,
                normed_mid=normed_mid,
                branch=branch,
                grad_middle=grad_middle,
                gain2=jnp.sum(grad_mid * unit, axis=0),
                shift2=jnp.sum(grad_mid, axis=0),
                out_bias=jnp.sum(branch0.astype(F32), axis=0),
                down_bias=jnp.sum(dy[i, :quarter_rows].astype(F32), axis=0),
                up_bias=jnp.sum(grad_hidden.astype(F32), axis=0),
            )
        )

    def whole(name):
        return jnp.concatenate([b[name] for b in back], axis=0)

    def scatter(parts, axis):
        total = parts[0].astype(F32)
        for k in range(1, n_f):
            total = total + shift_f(parts[k].astype(BF16), k).astype(F32)
        return lax.psum_scatter(
            total.astype(BF16), "ctx", scatter_dimension=axis, tiled=True
        ).astype(F32)

    dys = dy.reshape(trees * rows, width)
    active, grad_hidden, normed_mid = whole("active"), whole("grad_hidden"), whole("normed_mid")
    g_down = scatter([tn(active, cols(dys, k)) for k in range(n_f)], 1)
    g_up = scatter([tn(cols(normed_mid, k), grad_hidden) for k in range(n_f)], 0)

    heads_back = []
    for i in range(trees):
        table, parts, attended_parts, lse, attended, x0 = kept[i][:6]
        grad_attended = times_back(back[i]["branch"], w_out).astype(BF16)
        grad_parts = [v[None] for v in to_heads(grad_attended, HD)]
        back_parts = attention_bwd(table, parts, attended_parts, grad_parts, lse)
        heads_back.append(from_heads([v[0] for v in back_parts]))

    branch = whole("branch")
    attended_abs = jnp.concatenate([absolute(k[4]) for k in kept], axis=0)
    g_out = scatter([tn(attended_abs, cols(branch, k)) for k in range(n_f)], 1)

    grads = []
    for i in range(trees):
        x0, grad_middle = kept[i][5], back[i]["grad_middle"]
        g = sum_rows(wide_back(jnp.concatenate(heads_back[i], axis=1), w_qkv))
        mean = jnp.mean(x0, axis=1, keepdims=True)
        spread = jnp.mean((x0 - mean) * (x0 - mean), axis=1, keepdims=True)
        rstd = lax.rsqrt(spread + EPS)
        unit = (x0 - mean) * rstd
        back[i]["gain1"] = jnp.sum(g * unit, axis=0)
        back[i]["shift1"] = jnp.sum(g, axis=0)
        g = g * gain1
        moved = rstd * (
            g - jnp.mean(g, axis=1, keepdims=True) - unit * jnp.mean(g * unit, axis=1, keepdims=True)
        )
        grads.append(all_rows((grad_middle + moved).astype(BF16)))

    dqkv = jnp.concatenate([absolute(v) for v in heads_back], axis=0)
    normed_all = normed.reshape(trees * rows, width)
    g_qkv = scatter([tn(cols(normed_all, k), dqkv) for k in range(n_f)], 0)
    bias_sums = jnp.sum(dqkv.astype(F32), axis=0)

    def split_heads(v):
        apart = v.reshape(v.shape[0], heads, 3, HD)
        return [apart[:, :, k].reshape(v.shape[0], heads * HD) for k in range(3)]

    g_query, g_key, g_value = split_heads(g_qkv)
    query_sum, _, value_sum = split_heads(bias_sums[None])
    names = ("gain1", "shift1", "out_bias", "gain2", "shift2", "down_bias")
    rolled = jnp.stack([sum(b[name] for b in back) for name in names])
    turned = jnp.concatenate(
        [
            lax.dynamic_slice_in_dim(rolled, ((n_f + k - f) % n_f) * part, part, axis=1)
            for k in range(n_f)
        ],
        axis=1,
    )
    turned = lax.psum(turned, ("fsdp", "ctx", "tp"))
    span = part // n_c
    own = lax.dynamic_slice_in_dim(turned, f * part + c * span, span, axis=1)
    unit_sums = jnp.concatenate(
        [query_sum[0], value_sum[0], sum(b["up_bias"] for b in back)], axis=0
    )
    unit_sums = lax.psum(unit_sums, ("fsdp", "ctx"))
    return (
        jnp.stack([replace(quarter, chunk, v) for v in results]),
        jnp.stack([replace(quarter, chunk, v) for v in grads]),
        own[0],
        own[1],
        g_query,
        unit_sums[:local_width],
        g_key,
        g_value,
        unit_sums[local_width : 2 * local_width],
        g_out,
        own[2],
        own[3],
        own[4],
        g_up,
        unit_sums[2 * local_width :],
        g_down,
        own[5],
    )


def solution(mesh):
    in_specs = (
        P("fsdp", "ctx", None),
        P("fsdp", "ctx"),
        P("fsdp", "ctx"),
        P("fsdp", None),
        P(),
        P(),
        P("fsdp", "tp"),
        P("tp"),
        P("fsdp", "tp"),
        P("fsdp", "tp"),
        P("tp"),
        P("tp", "fsdp"),
        P(),
        P(),
        P(),
        P("fsdp", "tp"),
        P("tp"),
        P("tp", "fsdp"),
        P(),
        P("fsdp", "ctx", None),
    )
    out_specs = (
        P("fsdp", "ctx", None),
        P("fsdp", "ctx", None),
        P(("fsdp", "ctx")),
        P(("fsdp", "ctx")),
        P(("fsdp", "ctx"), "tp"),
        P("tp"),
        P(("fsdp", "ctx"), "tp"),
        P(("fsdp", "ctx"), "tp"),
        P("tp"),
        P("tp", ("fsdp", "ctx")),
        P(("fsdp", "ctx")),
        P(("fsdp", "ctx")),
        P(("fsdp", "ctx")),
        P(("fsdp", "ctx"), "tp"),
        P("tp"),
        P("tp", ("fsdp", "ctx")),
        P(("fsdp", "ctx")),
    )
    return jax.shard_map(
        partial(per_device, dict(mesh.shape)), mesh=mesh, in_specs=in_specs, out_specs=out_specs, check_vma=False
    )
```

time: 1770 us -> 1230 us (0.69)
  waiting for transfers between devices: 1180 us -> 542 us
  Pallas kernels: 0 us -> 118 us
  starting transfers between devices: 2.77 us -> 100 us
  matrix products: 317 us -> 221 us
  blocking collectives: 102 us -> 71.6 us
  other arithmetic: 126 us -> 96 us
  local copies, waits for them, and re-layouts: 21.5 us -> 50.6 us
    ppermute x0 -> x67, waiting for transfers between devices: none -> 542 us  [the longest x8 286 us: shift_f(): return lax.ppermute(v, 'fsdp', [(i, (i + k) % n_f) for i in range(n_f)])]
    reduce_scatter x10 -> x4, waiting for transfers between devices: 449 us -> 0.01 us  [scatter(): lax.psum_scatter(total.astype(BF16), 'ctx', scatter_dimension=axis, tiled...]
    all_gather x10 -> x0, waiting for transfers between devices: 388 us -> none  [the longest x1 99.3 us: per_device(): lax.all_gather(up_weight, 'fsdp', axis=0, tiled=True)]
    psum x4 -> x0, waiting for transfers between devices: 338 us -> none  [the longest x1 153 us: per_device(): lax.psum(jnp.dot(active, w_down, preferred_element_type=jnp.float32).asty...]
    pallas_call x0 -> x9, Pallas kernels: none -> 118 us  [the longest x2 47.8 us: attention_bwd(): pl.pallas_call(partial(bwd_kernel, nsrc), grid_spec=pltpu.PrefetchScalarG...]
    ppermute x0 -> x67, starting transfers between devices: none -> 100 us  [the longest x27 71.1 us: shift_c(): return lax.ppermute(v, 'ctx', [(i, (i + k) % n_c) for i in range(n_c)])]
    dot_general x48 -> x40, matrix products: 317 us -> 221 us  [the longest x8 84.7 us: tn(): lax.dot_general(a, b, (((0,), (0,)), ((), ())), preferred_element_type=F32)]
    unnamed x1 -> x0, blocking collectives: 40.6 us -> none
  transfers between devices with their start and end apart: 24 -> 71, of which waited for: 21 -> 27; matrix products, arithmetic and copies ran while one was open for 20% -> 28% of each run, Pallas kernels for 0% -> 10%
where the time goes in v1:
time: 1230 us; the launch traced here: 1220 us
  waiting for transfers between devices  542 us (44%)
  matrix products  221 us (18%)
  Pallas kernels  118 us (10%)
  starting transfers between devices  100 us (8%)
  other arithmetic  96 us (8%)
  blocking collectives  71.6 us (6%)
  local copies, waits for them, and re-layouts  50.6 us (4%)
  between operations  16.6 us (1%)
    ppermute x8, waiting for transfers between devices, shift_f(): return lax.ppermute(v, 'fsdp', [(i, (i + k) % n_f) for i in range(n_f)])  286 us
    ppermute x27, waiting for transfers between devices, shift_c(): return lax.ppermute(v, 'ctx', [(i, (i + k) % n_c) for i in range(n_c)])  160 us
    ppermute x32, waiting for transfers between devices, flip_t(): return lax.ppermute(v, 'tp', [(i, i ^ 1 << b) for i in range(n_t)])  95.5 us
    dot_general x8, matrix products, tn(): lax.dot_general(a, b, (((0,), (0,)), ((), ())), preferred_element_type=F32)  84.7 us
    dot_general x16, matrix products, nt(): lax.dot_general(a, b, (((1,), (1,)), ((), ())), preferred_element_type=F32)  74.8 us
    ppermute x27, starting transfers between devices, shift_c(): return lax.ppermute(v, 'ctx', [(i, (i + k) % n_c) for i in range(n_c)])  71.1 us
    dot_general x16, matrix products, nn(): lax.dot_general(a, b, (((1,), (0,)), ((), ())), preferred_element_type=F32)  61.8 us
    pallas_call x2, Pallas kernels, attention_bwd(): pl.pallas_call(partial(bwd_kernel, nsrc), grid_spec=pltpu.PrefetchScalarG...  47.8 us
  transfers between devices with their start and end apart: 71, of which 27 were waited for; matrix products, arithmetic and copies ran while one was open for 28% of the time, Pallas kernels for 10%

profile of v1, /device:TPU:0, one launch (start us, length us, event | category | flops | bytes accessed | tf_op | source)
XLA Modules:
  0.0 1216.1 jit_solution(6803603078534049741)
XLA Ops:
  9.3 5.1 collective-permute-start.2
  30.6 11.5 first_norm.1
  46.8 6.1 fusion.127
  53.0 5.4 fusion.118
  59.4 50.7 %collective-permute-done.3 = bf16[1024,1536]{0,1:T(8,128)(2,1)} collective-permute-done((bf16[1024,1536]{0,1:T(8,128)(2,1)}, bf16[1024,1536]{0,1:T(8,128)(2,1)}, u32[]{:S(2)}, u32[]{:S(2)}) %collective-permute-start.3) | collective-permute-done | bytes 3145760 | tf_op jit(solution)/shard_map/ppermute | solution.py:327
  110.1 5.0 fusion.19
  128.7 17.4 %collective-permute-start.22 = (bf16[512,384]{1,0:T(8,128)(2,1)S(1)}, bf16[512,384]{1,0:T(8,128)(2,1)S(1)}, u32[]{:S(2)}, u32[]{:S(2)}) collective-permute-start(bf16[512,384]{1,0:T(8,128)(2,1)S(1)} %get-tuple-element.152), channel_id=1, source_target_pairs={{0,8},{4,12},{8,0},{12,4},{1,9},{5,13},{9,1},{13,5},{2,10},{6,14},... | collective-permute-start | bytes 1179656 | tf_op jit(solution)/shard_map/ppermute | solution.py:330
  146.2 21.7 %collective-permute-done.5 = bf16[512,384]{1,0:T(8,128)(2,1)S(1)} collective-permute-done((bf16[512,384]{1,0:T(8,128)(2,1)S(1)}, bf16[512,384]{1,0:T(8,128)(2,1)S(1)}, u32[]{:S(2)}, u32[]{:S(2)}) %collective-permute-start.5) | collective-permute-done | bytes 393248 | tf_op jit(solution)/shard_map/ppermute | solution.py:330
  169.2 20.1 %tree_attention.2 = (bf16[1,512,128]{2,1,0:T(8,128)(2,1)}, bf16[1,512,128]{2,1,0:T(8,128)(2,1)}, bf16[1,512,128]{2,1,0:T(8,128)(2,1)}, bf16[1,512,128]{2,1,0:T(8,128)(2,1)}, f32[1,8,256]{2,1,0:T(8,128)}) custom-call(s32[1,32]{1,0:T(1,128)} %get-tuple-element.213.place, s32[1,7]{1,0:T(1,128)} %get-tuple-element.211.starts, s32[1,7]{1,0:T(1,128)} %get-tuple-element.209.path, ...), custom_call_target="tpu_custom_call" | custom-call | flops 1073741824 | bytes 2097152 | tf_op jit(solution)/shard_map/tree_attention/pallas_call | solution.py:101
  197.0 20.1 %tree_attention.3 = (bf16[1,512,128]{2,1,0:T(8,128)(2,1)}, bf16[1,512,128]{2,1,0:T(8,128)(2,1)}, bf16[1,512,128]{2,1,0:T(8,128)(2,1)}, bf16[1,512,128]{2,1,0:T(8,128)(2,1)}, f32[1,8,256]{2,1,0:T(8,128)}) custom-call(s32[1,32]{1,0:T(1,128)} %get-tuple-element.214.place, s32[1,7]{1,0:T(1,128)} %get-tuple-element.212.starts, s32[1,7]{1,0:T(1,128)} %get-tuple-element.210.path, ...), custom_call_target="tpu_custom_call" | custom-call | flops 1073741824 | bytes 2097152 | tf_op jit(solution)/shard_map/tree_attention/pallas_call | solution.py:101
  239.0 4.4 fusion.103
  243.4 7.2 collective-permute-done.12
  250.6 8.8 collective-permute-done.28
  263.5 4.3 fusion.109
  267.9 5.7 collective-permute-done.13
  280.4 8.9 collective-permute-done.15
  289.3 4.5 fusion.123
  296.8 79.1 %collective-permute-done.16 = bf16[2048,1024]{1,0:T(8,128)(2,1)} collective-permute-done((bf16[2048,1024]{1,0:T(8,128)(2,1)}, bf16[2048,1024]{1,0:T(8,128)(2,1)}, u32[]{:S(2)}, u32[]{:S(2)}) %collective-permute-start.16) | collective-permute-done | bytes 4194336 | tf_op jit(solution)/shard_map/ppermute | solution.py:327
  376.0 15.7 %convert_reduce_fusion.2 = (f32[2048]{0:T(1024)}, bf16[512,2048]{1,0:T(8,128)(2,1)S(1)}) fusion(f32[512,2048]{1,0:T(8,128)S(1)} %get-tuple-element.216, f32[512,2048]{1,0:T(8,128)S(1)} %copy-done.126, bf16[2048,1024]{1,0:T(8,128)(2,1)} %collective-permute-done.16, bf16[512,2048]{1,0:T(8,128)(2,1)S(1)} %copy-done.29), kind=kOutput, calls=%fused_computation.45 | convolution fusion | flops 2161113088 | bytes 15736832 | tf_op jit(solution)/shard_map/dot_general | solution.py:27
  394.1 4.6 fusion.189
  403.4 4.6 fusion.185
  411.6 6.5 fusion.114
  418.1 5.9 multiply_convert_fusion
  424.1 8.5 convert_reduce_fusion.1
  432.5 4.1 fusion.190
  436.6 4.5 fusion.191
  445.2 4.5 fusion.187
  453.9 11.2 collective-permute-done.18
  465.2 11.2 collective-permute-done.50
  476.4 10.8 collective-permute-done.32
  492.2 12.9 %collective-permute-done.37 = bf16[128,2048]{1,0:T(8,128)(2,1)S(1)} collective-permute-done((bf16[128,2048]{1,0:T(8,128)(2,1)S(1)}, bf16[128,2048]{1,0:T(8,128)(2,1)S(1)}, u32[]{:S(2)}, u32[]{:S(2)}) %collective-permute-start.37) | collective-permute-done | bytes 524320 | tf_op jit(solution)/shard_map/ppermute | solution.py:333
  511.6 13.3 %collective-permute-done.51 = bf16[128,2048]{1,0:T(8,128)(2,1)S(1)} collective-permute-done((bf16[128,2048]{1,0:T(8,128)(2,1)S(1)}, bf16[128,2048]{1,0:T(8,128)(2,1)S(1)}, u32[]{:S(2)}, u32[]{:S(2)}) %collective-permute-start.51) | collective-permute-done | bytes 524320 | tf_op jit(solution)/shard_map/ppermute | solution.py:333
  525.1 6.2 convolution_convert_fusion.1
  535.0 111.9 %collective-permute-done.64 = bf16[512,1024]{1,0:T(8,128)(2,1)S(1)} collective-permute-done((bf16[512,1024]{1,0:T(8,128)(2,1)S(1)}, bf16[512,1024]{1,0:T(8,128)(2,1)S(1)}, u32[]{:S(2)}, u32[]{:S(2)}) %collective-permute-start.64) | collective-permute-done | bytes 1048608 | tf_op jit(solution)/shard_map/ppermute | solution.py:327
  649.3 10.9 add_convert_fusion
  664.4 9.0 convolution_convert_fusion.2
  682.7 9.0 collective-permute-done.41
  694.4 6.8 collective-permute-done.40
  702.2 23.9 %tree_attention_back.2 = (bf16[1,512,384]{2,1,0:T(8,128)(2,1)}, bf16[1,512,384]{2,1,0:T(8,128)(2,1)}, bf16[1,512,384]{2,1,0:T(8,128)(2,1)}, bf16[1,512,384]{2,1,0:T(8,128)(2,1)}) custom-call(s32[1,32]{1,0:T(1,128)} %get-tuple-element.213.place, s32[1,7]{1,0:T(1,128)} %get-tuple-element.211.starts, s32[1,7]{1,0:T(1,128)} %get-tuple-element.209.path, ...), custom_call_target="tpu_custom_call" | custom-call | flops 2684354560 | bytes 5242880 | tf_op jit(solution)/shard_map/tree_attention_back/pallas_call | solution.py:178
  729.7 4.7 collective-permute-start.43
  735.8 19.3 %collective-permute-done.42 = bf16[512,384]{1,0:T(8,128)(2,1)S(1)} collective-permute-done((bf16[512,384]{1,0:T(8,128)(2,1)}, bf16[512,384]{1,0:T(8,128)(2,1)S(1)}, u32[]{:S(2)}, u32[]{:S(2)}) %collective-permute-start.42) | collective-permute-done | bytes 393248 | tf_op jit(solution)/shard_map/ppermute | solution.py:330
  755.1 16.2 %collective-permute-start.44 = (bf16[512,384]{1,0:T(8,128)(2,1)S(1)}, bf16[512,384]{1,0:T(8,128)(2,1)S(1)}, u32[]{:S(2)}, u32[]{:S(2)}) collective-permute-start(bf16[512,384]{1,0:T(8,128)(2,1)S(1)} %bitcast.354), channel_id=1, source_target_pairs={{0,4},{4,8},{8,12},{12,0},{1,5},{5,9},{9,13},{13,1},{2,6},{6,10},{... | collective-permute-start | bytes 1179656 | tf_op jit(solution)/shard_map/ppermute | solution.py:330
  771.4 21.9 %collective-permute-done.43 = bf16[512,384]{1,0:T(8,128)(2,1)S(1)} collective-permute-done((bf16[512,384]{1,0:T(8,128)(2,1)}, bf16[512,384]{1,0:T(8,128)(2,1)S(1)}, u32[]{:S(2)}, u32[]{:S(2)}) %collective-permute-start.43) | collective-permute-done | bytes 393248 | tf_op jit(solution)/shard_map/ppermute | solution.py:330
  799.0 5.8 fusion.135
  804.9 7.8 add_convert_fusion.1
  824.1 5.6 collective-permute-done.55
  829.7 18.9 %collective-permute-done.54 = bf16[512,128]{1,0:T(8,128)(2,1)S(1)} collective-permute-done((bf16[512,128]{1,0:T(8,128)(2,1)S(1)}, bf16[512,128]{1,0:T(8,128)(2,1)S(1)}, u32[]{:S(2)}, u32[]{:S(2)}) %collective-permute-start.54) | collective-permute-done | bytes 131104 | tf_op jit(solution)/shard_map/ppermute | solution.py:330
  849.3 23.9 %tree_attention_back.3 = (bf16[1,512,384]{2,1,0:T(8,128)(2,1)}, bf16[1,512,384]{2,1,0:T(8,128)(2,1)}, bf16[1,512,384]{2,1,0:T(8,128)(2,1)}, bf16[1,512,384]{2,1,0:T(8,128)(2,1)}) custom-call(s32[1,32]{1,0:T(1,128)} %get-tuple-element.214.place, s32[1,7]{1,0:T(1,128)} %get-tuple-element.212.starts, s32[1,7]{1,0:T(1,128)} %get-tuple-element.210.path, ...), custom_call_target="tpu_custom_call" | custom-call | flops 2684354560 | bytes 5242880 | tf_op jit(solution)/shard_map/tree_attention_back/pallas_call | solution.py:178
  878.8 20.3 %collective-permute-done.56 = bf16[512,384]{1,0:T(8,128)(2,1)S(1)} collective-permute-done((bf16[512,384]{1,0:T(8,128)(2,1)}, bf16[512,384]{1,0:T(8,128)(2,1)S(1)}, u32[]{:S(2)}, u32[]{:S(2)}) %collective-permute-start.56) | collective-permute-done | bytes 393248 | tf_op jit(solution)/shard_map/ppermute | solution.py:330
  899.2 32.8 %collective-permute-done.57 = bf16[512,384]{1,0:T(8,128)(2,1)S(1)} collective-permute-done((bf16[512,384]{1,0:T(8,128)(2,1)}, bf16[512,384]{1,0:T(8,128)(2,1)S(1)}, u32[]{:S(2)}, u32[]{:S(2)}) %collective-permute-start.57) | collective-permute-done | bytes 393248 | tf_op jit(solution)/shard_map/ppermute | solution.py:330
  935.0 23.0 %convolution_convert_fusion = bf16[1024,1536]{1,0:T(8,128)(2,1)} fusion(bf16[1024,2048]{1,0:T(8,128)(2,1)S(1)} %bitcast.293, bf16[512,384]{1,0:T(8,128)(2,1)S(1)} %get-tuple-element.143, bf16[512,384]{1,0:T(8,128)(2,1)S(1)} %get-tuple-element.141, bf16[512,384]{1,0:T(8,128)(2,1)S(1)} %get-tuple-element.142, bf16[512,384]{1,0:T(8,128)(2,1)S(1)} %get-tuple-element.140, ...), kind=kOutput, calls=%fused_computation.52 | convolution fusion | flops 3247964160 | bytes 8388608 | tf_op jit(solution)/shard_map/dot_general | solution.py:31
  966.6 4.7 replace.4
  974.1 4.5 replace.5
  986.9 4.5 fusion.133
  993.3 35.3 %collective-permute-done.63 = bf16[1024,1536]{1,0:T(8,128)(2,1)} collective-permute-done((bf16[1024,1536]{1,0:T(8,128)(2,1)}, bf16[1024,1536]{1,0:T(8,128)(2,1)}, u32[]{:S(2)}, u32[]{:S(2)}) %collective-permute-start.63) | collective-permute-done | bytes 3145760 | tf_op jit(solution)/shard_map/ppermute | solution.py:327
  1028.7 24.3 %add_convert_fusion.2 = bf16[1024,1536]{1,0:T(8,128)(2,1)} fusion(bf16[1024,1536]{1,0:T(8,128)(2,1)} %collective-permute-done.63, bf16[1024,2048]{1,0:T(8,128)(2,1)S(1)} %bitcast.294, bf16[512,384]{1,0:T(8,128)(2,1)S(1)} %copy-done.66, bf16[512,384]{1,0:T(8,128)(2,1)S(1)} %copy-done.60, bf16[512,384]{1,0:T(8,128)(2,1)S(1)} %copy-done.63, ...), kind=kOutput, calls=%fused_computation.9 | convolution fusion | flops 3251109888 | bytes 11534336 | tf_op jit(solution)/shard_map/dot_general | solution.py:31
  1053.7 4.8 pad_maximum_fusion
  1063.4 11.5 collective-permute-done.60
  1080.4 20.1 %convert_reduce_fusion = f32[1536]{0:T(1024)S(1)} fusion(bf16[512,384]{1,0:T(8,128)(2,1)S(1)} %copy-done.67, bf16[512,384]{1,0:T(8,128)(2,1)S(1)} %copy-done.61, bf16[512,384]{1,0:T(8,128)(2,1)S(1)} %copy-done.64, bf16[512,384]{1,0:T(8,128)(2,1)S(1)} %copy-done.58, bf16[512,384]{1,0:T(8,128)(2,1)S(1)} %copy-done.55, bf16[512,384]{1,0:T(8,128)(2,1)S(1)} %copy-done.49, ...), kind=kLoop, calls=%fused_computation.8 | loop fusion | flops 26737152 | bytes 3151872 | tf_op jit(solution)/shard_map/reduce_sum | solution.py:523
  1103.0 33.6 %psum.15 = f32[3072]{0:T(1024)S(1)} all-reduce(f32[3072]{0:T(1024)S(1)} %pad_maximum_fusion.47), channel_id=1, replica_groups=mesh['fsdp'=2,'ctx'=4,'tp'=4] {'fsdp','ctx'}, use_global_device_ids=true, to_apply=%region_39.40 | all-reduce | flops 3072 | bytes 24576 | tf_op jit(solution)/shard_map/psum | solution.py:546
  1140.1 38.0 %psum.14 = f32[6,2048]{1,0:T(8,128)S(1)} all-reduce(f32[6,2048]{1,0:T(8,128)S(1)} %pad_maximum_fusion.46), channel_id=1, replica_groups=mesh['fsdp'=2,'ctx'=4,'tp'=4] {'fsdp','ctx','tp'}, use_global_device_ids=true, to_apply=%region_34.35 | all-reduce | flops 12288 | bytes 98304 | tf_op jit(solution)/shard_map/psum | solution.py:540
  1183.3 4.5 replace.6
  1190.5 4.6 replace.7
  1195.1 4.0 pad_maximum_fusion.1
  (596 shorter events, 222.7 us)
Async XLA Ops:
  7.2 1171.6 %reduce-scatter.7.cloned.1.call-start = ((), (), s32[]{:S(2)}) async-start(), calls=%async_computation.5 | async-start | bytes 1310720 | tf_op jit(solution)/shard_map/reduce_scatter | solution.py:483
  9.3 49.1 %collective-permute-start.2 = (s32[2,15]{1,0:T(2,128)S(1)}, s32[2,15]{1,0:T(2,128)S(1)}, u32[]{:S(2)}, u32[]{:S(2)}) collective-permute-start(s32[2,15]{1,0:T(2,128)S(1)} %pad_add_fusion), channel_id=1, source_target_pairs={{0,12},{4,0},{8,4},{12,8},{1,13},{5,1},{9,5},{13,9},{2,14},{6,2},{... | collective-permute-start | bytes 368 | tf_op jit(solution)/shard_map/ppermute | solution.py:330
  14.4 44.0 %collective-permute-start.1 = (s32[2,15]{1,0:T(2,128)S(1)}, s32[2,15]{1,0:T(2,128)S(1)}, u32[]{:S(2)}, u32[]{:S(2)}) collective-permute-start(s32[2,15]{1,0:T(2,128)S(1)} %pad_add_fusion), channel_id=1, source_target_pairs={{0,8},{4,12},{8,0},{12,4},{1,9},{5,13},{9,1},{13,5},{2,10},{6,14},... | collective-permute-start | bytes 368 | tf_op jit(solution)/shard_map/ppermute | solution.py:330
  14.4 44.0 %collective-permute-start = (s32[2,15]{1,0:T(2,128)S(1)}, s32[2,15]{1,0:T(2,128)S(1)}, u32[]{:S(2)}, u32[]{:S(2)}) collective-permute-start(s32[2,15]{1,0:T(2,128)S(1)} %pad_add_fusion), channel_id=1, source_target_pairs={{0,4},{4,8},{8,12},{12,0},{1,5},{5,9},{9,13},{13,1},{2,6},{6,10},{... | collective-permute-start | bytes 368 | tf_op jit(solution)/shard_map/ppermute | solution.py:330
  18.4 201.8 %collective-permute-start.10 = (bf16[512,1024]{1,0:T(8,128)(2,1)}, bf16[512,1024]{1,0:T(8,128)(2,1)}, u32[]{:S(2)}, u32[]{:S(2)}) collective-permute-start(bf16[512,1024]{1,0:T(8,128)(2,1)} %fusion.98), channel_id=1, source_target_pairs={{0,16},{16,0},{1,17},{17,1},{2,18},{18,2},{3,19},{19,3},{4,20},{20... | collective-permute-start | bytes 3145736 | tf_op jit(solution)/shard_map/ppermute | solution.py:327
  27.0 83.2 %collective-permute-start.3 = (bf16[1024,1536]{0,1:T(8,128)(2,1)}, bf16[1024,1536]{0,1:T(8,128)(2,1)}, u32[]{:S(2)}, u32[]{:S(2)}) collective-permute-start(bf16[1024,1536]{0,1:T(8,128)(2,1)} %bitcast.17), channel_id=1, source_target_pairs={{0,16},{16,0},{1,17},{17,1},{2,18},{18,2},{3,19},{19,3},{4,20},{20... | collective-permute-start | bytes 9437192 | tf_op jit(solution)/shard_map/ppermute | solution.py:327
  116.1 12.6 %collective-permute-start.6 = (bf16[512,384]{1,0:T(8,128)(2,1)S(1)}, bf16[512,384]{1,0:T(8,128)(2,1)S(1)}, u32[]{:S(2)}, u32[]{:S(2)}) collective-permute-start(bf16[512,384]{1,0:T(8,128)(2,1)S(1)} %get-tuple-element.147), channel_id=1, source_target_pairs={{0,12},{4,0},{8,4},{12,8},{1,13},{5,1},{9,5},{13,9},{2,14},{6,2},{... | collective-permute-start | bytes 1179656 | tf_op jit(solution)/shard_map/ppermute | solution.py:330
  119.1 48.7 %collective-permute-start.5 = (bf16[512,384]{1,0:T(8,128)(2,1)S(1)}, bf16[512,384]{1,0:T(8,128)(2,1)S(1)}, u32[]{:S(2)}, u32[]{:S(2)}) collective-permute-start(bf16[512,384]{1,0:T(8,128)(2,1)S(1)} %get-tuple-element.148), channel_id=1, source_target_pairs={{0,8},{4,12},{8,0},{12,4},{1,9},{5,13},{9,1},{13,5},{2,10},{6,14},... | collective-permute-start | bytes 1179656 | tf_op jit(solution)/shard_map/ppermute | solution.py:330
  120.0 49.3 %collective-permute-start.4 = (bf16[512,384]{1,0:T(8,128)(2,1)S(1)}, bf16[512,384]{1,0:T(8,128)(2,1)}, u32[]{:S(2)}, u32[]{:S(2)}) collective-permute-start(bf16[512,384]{1,0:T(8,128)(2,1)S(1)} %get-tuple-element.149), channel_id=1, source_target_pairs={{0,4},{4,8},{8,12},{12,0},{1,5},{5,9},{9,13},{13,1},{2,6},{6,10},{... | collective-permute-start | bytes 1179656 | tf_op jit(solution)/shard_map/ppermute | solution.py:330
  125.2 64.8 %collective-permute-start.23 = (bf16[512,384]{1,0:T(8,128)(2,1)S(1)}, bf16[512,384]{1,0:T(8,128)(2,1)S(1)}, u32[]{:S(2)}, u32[]{:S(2)}) collective-permute-start(bf16[512,384]{1,0:T(8,128)(2,1)S(1)} %get-tuple-element.151), channel_id=1, source_target_pairs={{0,12},{4,0},{8,4},{12,8},{1,13},{5,1},{9,5},{13,9},{2,14},{6,2},{... | collective-permute-start | bytes 1179656 | tf_op jit(solution)/shard_map/ppermute | solution.py:330
  128.7 64.8 %collective-permute-start.22 = (bf16[512,384]{1,0:T(8,128)(2,1)S(1)}, bf16[512,384]{1,0:T(8,128)(2,1)S(1)}, u32[]{:S(2)}, u32[]{:S(2)}) collective-permute-start(bf16[512,384]{1,0:T(8,128)(2,1)S(1)} %get-tuple-element.152), channel_id=1, source_target_pairs={{0,8},{4,12},{8,0},{12,4},{1,9},{5,13},{9,1},{13,5},{2,10},{6,14},... | collective-permute-start | bytes 1179656 | tf_op jit(solution)/shard_map/ppermute | solution.py:330
  167.9 27.6 %collective-permute-start.21 = (bf16[512,384]{1,0:T(8,128)(2,1)S(1)}, bf16[512,384]{1,0:T(8,128)(2,1)S(1)}, u32[]{:S(2)}, u32[]{:S(2)}) collective-permute-start(bf16[512,384]{1,0:T(8,128)(2,1)S(1)} %get-tuple-element.153), channel_id=1, source_target_pairs={{0,4},{4,8},{8,12},{12,0},{1,5},{5,9},{9,13},{13,1},{2,6},{6,10},{... | collective-permute-start | bytes 1179656 | tf_op jit(solution)/shard_map/ppermute | solution.py:330
  189.3 27.8 %collective-permute-start.9 = (bf16[512,128]{1,0:T(8,128)(2,1)}, bf16[512,128]{1,0:T(8,128)(2,1)S(1)}, u32[]{:S(2)}, u32[]{:S(2)}) collective-permute-start(bf16[512,128]{1,0:T(8,128)(2,1)} %bitcast.365), channel_id=1, source_target_pairs={{0,4},{4,8},{8,12},{12,0},{1,5},{5,9},{9,13},{13,1},{2,6},{6,10},{... | collective-permute-start | bytes 393224 | tf_op jit(solution)/shard_map/ppermute | solution.py:330
  190.0 27.6 %collective-permute-start.8 = (bf16[512,128]{1,0:T(8,128)(2,1)}, bf16[512,128]{1,0:T(8,128)(2,1)S(1)}, u32[]{:S(2)}, u32[]{:S(2)}) collective-permute-start(bf16[512,128]{1,0:T(8,128)(2,1)} %bitcast.364), channel_id=1, source_target_pairs={{0,8},{4,12},{8,0},{12,4},{1,9},{5,13},{9,1},{13,5},{2,10},{6,14},... | collective-permute-start | bytes 393224 | tf_op jit(solution)/shard_map/ppermute | solution.py:330
  193.5 24.6 %collective-permute-start.7 = (bf16[512,128]{1,0:T(8,128)(2,1)}, bf16[512,128]{1,0:T(8,128)(2,1)S(1)}, u32[]{:S(2)}, u32[]{:S(2)}) collective-permute-start(bf16[512,128]{1,0:T(8,128)(2,1)} %bitcast.363), channel_id=1, source_target_pairs={{0,12},{4,0},{8,4},{12,8},{1,13},{5,1},{9,5},{13,9},{2,14},{6,2},{... | collective-permute-start | bytes 393224 | tf_op jit(solution)/shard_map/ppermute | solution.py:330
  195.5 93.8 %collective-permute-start.15 = (bf16[1024,2048]{1,0:T(8,128)(2,1)}, bf16[1024,2048]{1,0:T(8,128)(2,1)}, u32[]{:S(2)}, u32[]{:S(2)}) collective-permute-start(bf16[1024,2048]{1,0:T(8,128)(2,1)} %param.35), channel_id=1, source_target_pairs={{0,16},{16,0},{1,17},{17,1},{2,18},{18,2},{3,19},{19,3},{4,20},{20... | collective-permute-start | bytes 12582920 | tf_op jit(solution)/shard_map/ppermute | solution.py:327
  217.1 158.8 %collective-permute-start.16 = (bf16[2048,1024]{1,0:T(8,128)(2,1)}, bf16[2048,1024]{1,0:T(8,128)(2,1)}, u32[]{:S(2)}, u32[]{:S(2)}) collective-permute-start(bf16[2048,1024]{1,0:T(8,128)(2,1)} %param.37), channel_id=1, source_target_pairs={{0,16},{16,0},{1,17},{17,1},{2,18},{18,2},{3,19},{19,3},{4,20},{20... | collective-permute-start | bytes 12582920 | tf_op jit(solution)/shard_map/ppermute | solution.py:327
  218.2 10.3 collective-permute-start.25
  220.2 8.3 collective-permute-start.24
  225.6 9.7 collective-permute-start.11
  235.7 14.9 %collective-permute-start.12 = (bf16[128,2048]{1,0:T(8,128)(2,1)S(1)}, bf16[128,2048]{1,0:T(8,128)(2,1)S(1)}, u32[]{:S(2)}, u32[]{:S(2)}) collective-permute-start(bf16[128,2048]{1,0:T(8,128)(2,1)S(1)} %slice.856), channel_id=1, source_target_pairs={{0,2},{1,3},{2,0},{3,1},{4,6},{5,7},{6,4},{7,5},{8,10},{9,11},{10,... | collective-permute-start | bytes 1572872 | tf_op jit(solution)/shard_map/ppermute | solution.py:333
  237.7 21.7 %collective-permute-start.28 = (bf16[128,2048]{1,0:T(8,128)(2,1)S(1)}, bf16[128,2048]{1,0:T(8,128)(2,1)S(1)}, u32[]{:S(2)}, u32[]{:S(2)}) collective-permute-start(bf16[128,2048]{1,0:T(8,128)(2,1)S(1)} %slice.854), channel_id=1, source_target_pairs={{0,2},{1,3},{2,0},{3,1},{4,6},{5,7},{6,4},{7,5},{8,10},{9,11},{10,... | collective-permute-start | bytes 1572872 | tf_op jit(solution)/shard_map/ppermute | solution.py:333
  262.0 11.6 collective-permute-start.13
  278.6 124.6 %collective-permute-start.29 = (bf16[128,2048]{1,0:T(8,128)(2,1)S(1)}, bf16[128,2048]{1,0:T(8,128)(2,1)S(1)}, u32[]{:S(2)}, u32[]{:S(2)}) collective-permute-start(bf16[128,2048]{1,0:T(8,128)(2,1)S(1)} %get-tuple-element.119), channel_id=1, source_target_pairs={{0,2},{1,3},{2,0},{3,1},{4,6},{5,7},{6,4},{7,5},{8,10},{9,11},{10,... | collective-permute-start | bytes 1572872 | tf_op jit(solution)/shard_map/ppermute | solution.py:333
  398.8 9.9 collective-permute-start.35
  408.1 41.8 %collective-permute-start.17 = (bf16[256,2048]{1,0:T(8,128)(2,1)S(1)}, bf16[256,2048]{1,0:T(8,128)(2,1)S(1)}, u32[]{:S(2)}, u32[]{:S(2)}) collective-permute-start(bf16[256,2048]{1,0:T(8,128)(2,1)S(1)} %fusion.57), channel_id=1, source_target_pairs={{0,1},{1,0},{2,3},{3,2},{4,5},{5,4},{6,7},{7,6},{8,9},{9,8},{10,11... | collective-permute-start | bytes 3145736 | tf_op jit(solution)/shard_map/ppermute | solution.py:333
  409.1 44.9 %collective-permute-start.36 = (bf16[128,2048]{1,0:T(8,128)(2,1)S(1)}, bf16[128,2048]{1,0:T(8,128)(2,1)S(1)}, u32[]{:S(2)}, u32[]{:S(2)}) collective-permute-start(bf16[128,2048]{1,0:T(8,128)(2,1)S(1)} %slice.852), channel_id=1, source_target_pairs={{0,2},{1,3},{2,0},{3,1},{4,6},{5,7},{6,4},{7,5},{8,10},{9,11},{10,... | collective-permute-start | bytes 1572872 | tf_op jit(solution)/shard_map/ppermute | solution.py:333
  441.4 9.5 collective-permute-start.49
  450.3 14.9 %collective-permute-start.18 = (bf16[128,2048]{1,0:T(8,128)(2,1)S(1)}, bf16[128,2048]{1,0:T(8,128)(2,1)S(1)}, u32[]{:S(2)}, u32[]{:S(2)}) collective-permute-start(bf16[128,2048]{1,0:T(8,128)(2,1)S(1)} %slice.855), channel_id=1, source_target_pairs={{0,2},{1,3},{2,0},{3,1},{4,6},{5,7},{6,4},{7,5},{8,10},{9,11},{10,... | collective-permute-start | bytes 1572872 | tf_op jit(solution)/shard_map/ppermute | solution.py:333
  451.3 25.1 %collective-permute-start.50 = (bf16[128,2048]{1,0:T(8,128)(2,1)S(1)}, bf16[128,2048]{1,0:T(8,128)(2,1)S(1)}, u32[]{:S(2)}, u32[]{:S(2)}) collective-permute-start(bf16[128,2048]{1,0:T(8,128)(2,1)S(1)} %slice.850), channel_id=1, source_target_pairs={{0,2},{1,3},{2,0},{3,1},{4,6},{5,7},{6,4},{7,5},{8,10},{9,11},{10,... | collective-permute-start | bytes 1572872 | tf_op jit(solution)/shard_map/ppermute | solution.py:333
  453.3 33.9 %collective-permute-start.32 = (bf16[128,2048]{1,0:T(8,128)(2,1)S(1)}, bf16[128,2048]{1,0:T(8,128)(2,1)S(1)}, u32[]{:S(2)}, u32[]{:S(2)}) collective-permute-start(bf16[128,2048]{1,0:T(8,128)(2,1)S(1)} %slice.853), channel_id=1, source_target_pairs={{0,2},{1,3},{2,0},{3,1},{4,6},{5,7},{6,4},{7,5},{8,10},{9,11},{10,... | collective-permute-start | bytes 1572872 | tf_op jit(solution)/shard_map/ppermute | solution.py:333
  491.7 13.5 %collective-permute-start.37 = (bf16[128,2048]{1,0:T(8,128)(2,1)S(1)}, bf16[128,2048]{1,0:T(8,128)(2,1)S(1)}, u32[]{:S(2)}, u32[]{:S(2)}) collective-permute-start(bf16[128,2048]{1,0:T(8,128)(2,1)S(1)} %get-tuple-element.126), channel_id=1, source_target_pairs={{0,2},{1,3},{2,0},{3,1},{4,6},{5,7},{6,4},{7,5},{8,10},{9,11},{10,... | collective-permute-start | bytes 1572872 | tf_op jit(solution)/shard_map/ppermute | solution.py:333
  510.6 14.4 %collective-permute-start.51 = (bf16[128,2048]{1,0:T(8,128)(2,1)S(1)}, bf16[128,2048]{1,0:T(8,128)(2,1)S(1)}, u32[]{:S(2)}, u32[]{:S(2)}) collective-permute-start(bf16[128,2048]{1,0:T(8,128)(2,1)S(1)} %get-tuple-element.123), channel_id=1, source_target_pairs={{0,2},{1,3},{2,0},{3,1},{4,6},{5,7},{6,4},{7,5},{8,10},{9,11},{10,... | collective-permute-start | bytes 1572872 | tf_op jit(solution)/shard_map/ppermute | solution.py:333
  531.4 118.0 %collective-permute-start.66 = (bf16[2048,1024]{1,0:T(8,128)(2,1)}, bf16[2048,1024]{1,0:T(8,128)(2,1)}, u32[]{:S(2)}, u32[]{:S(2)}) collective-permute-start(bf16[2048,1024]{1,0:T(8,128)(2,1)} %convolution_convert_fusion.1), channel_id=1, source_target_pairs={{0,16},{16,0},{1,17},{17,1},{2,18},{18,2},{3,19},{19,3},{4,20},{20... | collective-permute-start | bytes 12582920 | tf_op jit(solution)/shard_map/ppermute | solution.py:327
  534.5 112.5 %collective-permute-start.64 = (bf16[512,1024]{1,0:T(8,128)(2,1)S(1)}, bf16[512,1024]{1,0:T(8,128)(2,1)S(1)}, u32[]{:S(2)}, u32[]{:S(2)}) collective-permute-start(bf16[512,1024]{1,0:T(8,128)(2,1)S(1)} %fusion.61), channel_id=1, source_target_pairs={{0,16},{16,0},{1,17},{17,1},{2,18},{18,2},{3,19},{19,3},{4,20},{20... | collective-permute-start | bytes 3145736 | tf_op jit(solution)/shard_map/ppermute | solution.py:327
  649.3 549.9 %reduce-scatter.11.cloned.1.call-start = ((), (), s32[]{:S(2)}) async-start(), calls=%async_computation.7 | async-start | bytes 5242880 | tf_op jit(solution)/shard_map/reduce_scatter | solution.py:483
  660.2 541.6 %reduce-scatter.9.cloned.1.call-start = ((), (), s32[]{:S(2)}) async-start(), calls=%async_computation.6 | async-start | bytes 5242880 | tf_op jit(solution)/shard_map/reduce_scatter | solution.py:483
  673.4 131.5 %collective-permute-start.65 = (bf16[1024,2048]{1,0:T(8,128)(2,1)}, bf16[1024,2048]{1,0:T(8,128)(2,1)}, u32[]{:S(2)}, u32[]{:S(2)}) collective-permute-start(bf16[1024,2048]{1,0:T(8,128)(2,1)} %convolution_convert_fusion.2), channel_id=1, source_target_pairs={{0,16},{16,0},{1,17},{17,1},{2,18},{18,2},{3,19},{19,3},{4,20},{20... | collective-permute-start | bytes 12582920 | tf_op jit(solution)/shard_map/ppermute | solution.py:327
  679.9 11.8 collective-permute-start.41
  680.1 48.6 %collective-permute-start.19 = (bf16[128,2048]{1,0:T(8,128)(2,1)S(1)}, bf16[128,2048]{1,0:T(8,128)(2,1)S(1)}, u32[]{:S(2)}, u32[]{:S(2)}) collective-permute-start(bf16[128,2048]{1,0:T(8,128)(2,1)S(1)} %copy-done.13), channel_id=1, source_target_pairs={{0,2},{1,3},{2,0},{3,1},{4,6},{5,7},{6,4},{7,5},{8,10},{9,11},{10,... | collective-permute-start | bytes 1572872 | tf_op jit(solution)/shard_map/ppermute | solution.py:333
  680.6 53.9 %collective-permute-start.33 = (bf16[128,2048]{1,0:T(8,128)(2,1)S(1)}, bf16[128,2048]{1,0:T(8,128)(2,1)S(1)}, u32[]{:S(2)}, u32[]{:S(2)}) collective-permute-start(bf16[128,2048]{1,0:T(8,128)(2,1)S(1)} %copy-done.11), channel_id=1, source_target_pairs={{0,2},{1,3},{2,0},{3,1},{4,6},{5,7},{6,4},{7,5},{8,10},{9,11},{10,... | collective-permute-start | bytes 1572872 | tf_op jit(solution)/shard_map/ppermute | solution.py:333
  682.1 19.2 %collective-permute-start.40 = (bf16[512,128]{1,0:T(8,128)(2,1)S(1)}, bf16[512,128]{1,0:T(8,128)(2,1)}, u32[]{:S(2)}, u32[]{:S(2)}) collective-permute-start(bf16[512,128]{1,0:T(8,128)(2,1)S(1)} %get-tuple-element.175), channel_id=1, source_target_pairs={{0,8},{4,12},{8,0},{12,4},{1,9},{5,13},{9,1},{13,5},{2,10},{6,14},... | collective-permute-start | bytes 393224 | tf_op jit(solution)/shard_map/ppermute | solution.py:330
  692.4 9.8 collective-permute-start.39
  726.1 29.0 %collective-permute-start.42 = (bf16[512,384]{1,0:T(8,128)(2,1)}, bf16[512,384]{1,0:T(8,128)(2,1)S(1)}, u32[]{:S(2)}, u32[]{:S(2)}) collective-permute-start(bf16[512,384]{1,0:T(8,128)(2,1)} %bitcast.358), channel_id=1, source_target_pairs={{0,12},{4,0},{8,4},{12,8},{1,13},{5,1},{9,5},{13,9},{2,14},{6,2},{... | collective-permute-start | bytes 1179656 | tf_op jit(solution)/shard_map/ppermute | solution.py:330
  729.7 234.0 %collective-permute-start.20 = (bf16[256,2048]{1,0:T(8,128)(2,1)}, bf16[256,2048]{1,0:T(8,128)(2,1)}, u32[]{:S(2)}, u32[]{:S(2)}) collective-permute-start(bf16[256,2048]{1,0:T(8,128)(2,1)} %pad_maximum_fusion.29), channel_id=1, source_target_pairs={{0,1},{1,0},{2,3},{3,2},{4,5},{5,4},{6,7},{7,6},{8,9},{9,8},{10,11... | collective-permute-start | bytes 3145736 | tf_op jit(solution)/shard_map/ppermute | solution.py:333
  729.7 63.5 %collective-permute-start.43 = (bf16[512,384]{1,0:T(8,128)(2,1)}, bf16[512,384]{1,0:T(8,128)(2,1)S(1)}, u32[]{:S(2)}, u32[]{:S(2)}) collective-permute-start(bf16[512,384]{1,0:T(8,128)(2,1)} %bitcast.355), channel_id=1, source_target_pairs={{0,8},{4,12},{8,0},{12,4},{1,9},{5,13},{9,1},{13,5},{2,10},{6,14},... | collective-permute-start | bytes 1179656 | tf_op jit(solution)/shard_map/ppermute | solution.py:330
  735.6 235.7 %collective-permute-start.34 = (bf16[256,2048]{1,0:T(8,128)(2,1)}, bf16[256,2048]{1,0:T(8,128)(2,1)}, u32[]{:S(2)}, u32[]{:S(2)}) collective-permute-start(bf16[256,2048]{1,0:T(8,128)(2,1)} %pad_maximum_fusion.31), channel_id=1, source_target_pairs={{0,1},{1,0},{2,3},{3,2},{4,5},{5,4},{6,7},{7,6},{8,9},{9,8},{10,11... | collective-permute-start | bytes 3145736 | tf_op jit(solution)/shard_map/ppermute | solution.py:333
  755.1 38.2 %collective-permute-start.44 = (bf16[512,384]{1,0:T(8,128)(2,1)S(1)}, bf16[512,384]{1,0:T(8,128)(2,1)S(1)}, u32[]{:S(2)}, u32[]{:S(2)}) collective-permute-start(bf16[512,384]{1,0:T(8,128)(2,1)S(1)} %bitcast.354), channel_id=1, source_target_pairs={{0,4},{4,8},{8,12},{12,0},{1,5},{5,9},{9,13},{13,1},{2,6},{6,10},{... | collective-permute-start | bytes 1179656 | tf_op jit(solution)/shard_map/ppermute | solution.py:330
  812.7 391.9 %reduce-scatter.5.cloned.1.call-start = ((), (), s32[]{:S(2)}) async-start(), calls=%async_computation.4 | async-start | bytes 3932160 | tf_op jit(solution)/shard_map/reduce_scatter | solution.py:483
  819.4 10.4 collective-permute-start.55
  819.4 29.2 %collective-permute-start.54 = (bf16[512,128]{1,0:T(8,128)(2,1)S(1)}, bf16[512,128]{1,0:T(8,128)(2,1)S(1)}, u32[]{:S(2)}, u32[]{:S(2)}) collective-permute-start(bf16[512,128]{1,0:T(8,128)(2,1)S(1)} %get-tuple-element.171), channel_id=1, source_target_pairs={{0,8},{4,12},{8,0},{12,4},{1,9},{5,13},{9,1},{13,5},{2,10},{6,14},... | collective-permute-start | bytes 393224 | tf_op jit(solution)/shard_map/ppermute | solution.py:330
  821.3 27.3 %collective-permute-start.53 = (bf16[512,128]{1,0:T(8,128)(2,1)S(1)}, bf16[512,128]{1,0:T(8,128)(2,1)S(1)}, u32[]{:S(2)}, u32[]{:S(2)}) collective-permute-start(bf16[512,128]{1,0:T(8,128)(2,1)S(1)} %get-tuple-element.172), channel_id=1, source_target_pairs={{0,4},{4,8},{8,12},{12,0},{1,5},{5,9},{9,13},{13,1},{2,6},{6,10},{... | collective-permute-start | bytes 393224 | tf_op jit(solution)/shard_map/ppermute | solution.py:330
  873.2 25.9 %collective-permute-start.56 = (bf16[512,384]{1,0:T(8,128)(2,1)}, bf16[512,384]{1,0:T(8,128)(2,1)S(1)}, u32[]{:S(2)}, u32[]{:S(2)}) collective-permute-start(bf16[512,384]{1,0:T(8,128)(2,1)} %bitcast.359), channel_id=1, source_target_pairs={{0,12},{4,0},{8,4},{12,8},{1,13},{5,1},{9,5},{13,9},{2,14},{6,2},{... | collective-permute-start | bytes 1179656 | tf_op jit(solution)/shard_map/ppermute | solution.py:330
  875.2 56.8 %collective-permute-start.57 = (bf16[512,384]{1,0:T(8,128)(2,1)}, bf16[512,384]{1,0:T(8,128)(2,1)S(1)}, u32[]{:S(2)}, u32[]{:S(2)}) collective-permute-start(bf16[512,384]{1,0:T(8,128)(2,1)} %bitcast.357), channel_id=1, source_target_pairs={{0,8},{4,12},{8,0},{12,4},{1,9},{5,13},{9,1},{13,5},{2,10},{6,14},... | collective-permute-start | bytes 1179656 | tf_op jit(solution)/shard_map/ppermute | solution.py:330
  876.7 55.3 %collective-permute-start.58 = (bf16[512,384]{1,0:T(8,128)(2,1)S(1)}, bf16[512,384]{1,0:T(8,128)(2,1)S(1)}, u32[]{:S(2)}, u32[]{:S(2)}) collective-permute-start(bf16[512,384]{1,0:T(8,128)(2,1)S(1)} %bitcast.356), channel_id=1, source_target_pairs={{0,4},{4,8},{8,12},{12,0},{1,5},{5,9},{9,13},{13,1},{2,6},{6,10},{... | collective-permute-start | bytes 1179656 | tf_op jit(solution)/shard_map/ppermute | solution.py:330
  958.1 70.5 %collective-permute-start.63 = (bf16[1024,1536]{1,0:T(8,128)(2,1)}, bf16[1024,1536]{1,0:T(8,128)(2,1)}, u32[]{:S(2)}, u32[]{:S(2)}) collective-permute-start(bf16[1024,1536]{1,0:T(8,128)(2,1)} %convolution_convert_fusion), channel_id=1, source_target_pairs={{0,16},{16,0},{1,17},{17,1},{2,18},{18,2},{3,19},{19,3},{4,20},{20... | collective-permute-start | bytes 9437192 | tf_op jit(solution)/shard_map/ppermute | solution.py:327
  960.8 17.8 %collective-permute-start.45 = (bf16[256,2048]{1,0:T(8,128)(2,1)}, bf16[256,2048]{1,0:T(8,128)(2,1)}, u32[]{:S(2)}, u32[]{:S(2)}) collective-permute-start(bf16[256,2048]{1,0:T(8,128)(2,1)} %fusion.53), channel_id=1, source_target_pairs={{0,1},{1,0},{2,3},{3,2},{4,5},{5,4},{6,7},{7,6},{8,9},{9,8},{10,11... | collective-permute-start | bytes 3145736 | tf_op jit(solution)/shard_map/ppermute | solution.py:333
  981.6 76.8 %collective-permute-start.46 = (bf16[128,2048]{1,0:T(8,128)(2,1)}, bf16[128,2048]{1,0:T(8,128)(2,1)S(1)}, u32[]{:S(2)}, u32[]{:S(2)}) collective-permute-start(bf16[128,2048]{1,0:T(8,128)(2,1)} %slice.851), channel_id=1, source_target_pairs={{0,2},{1,3},{2,0},{3,1},{4,6},{5,7},{6,4},{7,5},{8,10},{9,11},{10,... | collective-permute-start | bytes 1572872 | tf_op jit(solution)/shard_map/ppermute | solution.py:333
  993.1 66.2 %collective-permute-start.59 = (bf16[256,2048]{1,0:T(8,128)(2,1)}, bf16[256,2048]{1,0:T(8,128)(2,1)}, u32[]{:S(2)}, u32[]{:S(2)}) collective-permute-start(bf16[256,2048]{1,0:T(8,128)(2,1)} %fusion.51), channel_id=1, source_target_pairs={{0,1},{1,0},{2,3},{3,2},{4,5},{5,4},{6,7},{7,6},{8,9},{9,8},{10,11... | collective-permute-start | bytes 3145736 | tf_op jit(solution)/shard_map/ppermute | solution.py:333
  1061.9 13.1 %collective-permute-start.60 = (bf16[128,2048]{1,0:T(8,128)(2,1)S(1)}, bf16[128,2048]{1,0:T(8,128)(2,1)S(1)}, u32[]{:S(2)}, u32[]{:S(2)}) collective-permute-start(bf16[128,2048]{1,0:T(8,128)(2,1)S(1)} %slice.849), channel_id=1, source_target_pairs={{0,2},{1,3},{2,0},{3,1},{4,6},{5,7},{6,4},{7,5},{8,10},{9,11},{10,... | collective-permute-start | bytes 1572872 | tf_op jit(solution)/shard_map/ppermute | solution.py:333
  1078.3 22.3 %collective-permute-start.47 = (bf16[128,2048]{1,0:T(8,128)(2,1)S(1)}, bf16[128,2048]{1,0:T(8,128)(2,1)S(1)}, u32[]{:S(2)}, u32[]{:S(2)}) collective-permute-start(bf16[128,2048]{1,0:T(8,128)(2,1)S(1)} %get-tuple-element.155), channel_id=1, source_target_pairs={{0,2},{1,3},{2,0},{3,1},{4,6},{5,7},{6,4},{7,5},{8,10},{9,11},{10,... | collective-permute-start | bytes 1572872 | tf_op jit(solution)/shard_map/ppermute | solution.py:333
  1079.9 22.0 %collective-permute-start.61 = (bf16[128,2048]{1,0:T(8,128)(2,1)S(1)}, bf16[128,2048]{1,0:T(8,128)(2,1)S(1)}, u32[]{:S(2)}, u32[]{:S(2)}) collective-permute-start(bf16[128,2048]{1,0:T(8,128)(2,1)S(1)} %get-tuple-element.156), channel_id=1, source_target_pairs={{0,2},{1,3},{2,0},{3,1},{4,6},{5,7},{6,4},{7,5},{8,10},{9,11},{10,... | collective-permute-start | bytes 1572872 | tf_op jit(solution)/shard_map/ppermute | solution.py:333
  1101.6 78.9 %collective-permute-start.48 = (bf16[256,2048]{1,0:T(8,128)(2,1)}, bf16[256,2048]{1,0:T(8,128)(2,1)}, u32[]{:S(2)}, u32[]{:S(2)}) collective-permute-start(bf16[256,2048]{1,0:T(8,128)(2,1)} %pad_maximum_fusion.33), channel_id=1, source_target_pairs={{0,1},{1,0},{2,3},{3,2},{4,5},{5,4},{6,7},{7,6},{8,9},{9,8},{10,11... | collective-permute-start | bytes 3145736 | tf_op jit(solution)/shard_map/ppermute | solution.py:333
  1102.0 85.8 %collective-permute-start.62 = (bf16[256,2048]{1,0:T(8,128)(2,1)S(1)}, bf16[256,2048]{1,0:T(8,128)(2,1)}, u32[]{:S(2)}, u32[]{:S(2)}) collective-permute-start(bf16[256,2048]{1,0:T(8,128)(2,1)S(1)} %pad_maximum_fusion.35), channel_id=1, source_target_pairs={{0,1},{1,0},{2,3},{3,2},{4,5},{5,4},{6,7},{7,6},{8,9},{9,8},{10,11... | collective-permute-start | bytes 3145736 | tf_op jit(solution)/shard_map/ppermute | solution.py:333
  (142 other events, 2181.6 us)
Sparse Core Ops, SparseCore 0:
  649.4 24.5 reduce-scatter.6
  676.3 103.7 reduce-scatter.10
  812.8 101.2 reduce-scatter.8
  1053.1 58.4 reduce-scatter.4

commit v2 on v1

--- a/solution.py
+++ b/solution.py
@@ -41,15 +41,15 @@
     return p
 
 def fwd_kernel(nsrc,place,starts,path,code,*refs):
-    ins=refs[:nsrc]; outs=refs[nsrc:2*nsrc]; lse_ref=refs[2*nsrc]
-    qs,ks,vs,os,kbit,qpath,m_s,l_s,acc_s=refs[2*nsrc+1:]
+    qkv_ref=refs[0]; outs=refs[1:nsrc+1]; lse_ref=refs[nsrc+1]
+    qs,ks,vs,os,kbit,qpath,m_s,l_s,acc_s=refs[nsrc+2:]
     t=pl.program_id(0)
-    local=ins[0].shape[1]; per=local//RUN; rows=nsrc*local; n=rows//TILE
+    rows=qkv_ref.shape[1]; local=rows//nsrc; per=local//RUN; n=rows//TILE
     nseg=path.shape[1]
     for s in range(nsrc):
         for j in range(per):
             d=pl.multiple_of(place[t,s*per+j]*RUN,RUN)
-            blk=ins[s][0,j*RUN:(j+1)*RUN,:]
+            blk=qkv_ref[0,s*local+j*RUN:s*local+(j+1)*RUN,:]
             qs[pl.ds(d,RUN),:]=blk[:,0:HD]; ks[pl.ds(d,RUN),:]=blk[:,HD:2*HD]; vs[pl.ds(d,RUN),:]=blk[:,2*HD:]
     pos=lax.broadcasted_iota(jnp.int32,(rows,HD),0)
     kbit[...]=jnp.left_shift(1,seg_of(pos,starts,t,nseg))
@@ -94,31 +94,31 @@
             d=pl.multiple_of(place[t,s*per+j]*RUN,RUN)
             outs[s][0,j*RUN:(j+1)*RUN,:]=os[pl.ds(d,RUN),:]
 
-def attention_fwd(tables,parts):
+def attention_fwd(tables,nsrc,qkv):
     place,starts,path,code=tables
-    nsrc=len(parts); T,local,_=parts[0].shape; rows=nsrc*local; n=rows//TILE
+    T,rows,_=qkv.shape; local=rows//nsrc; n=rows//TILE
     bs=lambda w: pl.BlockSpec((1,local,w),lambda t,*_:(t,0,0))
     return pl.pallas_call(partial(fwd_kernel,nsrc),
         grid_spec=pltpu.PrefetchScalarGridSpec(num_scalar_prefetch=4,grid=(T,),
-            in_specs=[bs(3*HD)]*nsrc,
+            in_specs=[pl.BlockSpec((1,rows,3*HD),lambda t,*_:(t,0,0))],
             out_specs=[bs(HD)]*nsrc+[pl.BlockSpec((1,n,TILE),lambda t,*_:(t,0,0))],
             scratch_shapes=[pltpu.VMEM((rows,HD),BF16)]*4+[pltpu.VMEM((rows,HD),jnp.int32),pltpu.VMEM((n,TILE),jnp.int32),
                pltpu.VMEM((1,TILE),F32),pltpu.VMEM((1,TILE),F32),pltpu.VMEM((HD,TILE),F32)]),
         out_shape=[jax.ShapeDtypeStruct((T,local,HD),BF16)]*nsrc+[jax.ShapeDtypeStruct((T,n,TILE),F32)],
-        cost_estimate=pl.CostEstimate(flops=T*rows*rows*HD*2,bytes_accessed=T*rows*HD*8,transcendentals=T*rows*rows//2),
-        name="tree_attention")(place,starts,path,code,*parts)
+        cost_estimate=pl.CostEstimate(flops=T*rows*rows*HD*20,bytes_accessed=T*rows*HD*8,transcendentals=T*rows*rows//2),
+        name="tree_attention")(place,starts,path,code,qkv)
 
 def bwd_kernel(nsrc,place,starts,path,code,*refs):
-    ins=refs[:nsrc]; oin=refs[nsrc:2*nsrc]; gin=refs[2*nsrc:3*nsrc]; lse_ref=refs[3*nsrc]
-    outs=refs[3*nsrc+1:4*nsrc+1]
-    qs,ks,vs,gs,os,kbit,qpath,dsum,dq,dk,dv,sorted_out=refs[4*nsrc+1:]
+    qkv_ref=refs[0]; oin=refs[1:nsrc+1]; gin=refs[nsrc+1:2*nsrc+1]; lse_ref=refs[2*nsrc+1]
+    outs=refs[2*nsrc+2:3*nsrc+1]; whole_ref=refs[3*nsrc+1]
+    qs,ks,vs,gs,os,kbit,qpath,dsum,dq,dk,dv,sorted_out=refs[3*nsrc+2:]
     t=pl.program_id(0)
-    local=ins[0].shape[1]; per=local//RUN; rows=nsrc*local; n=rows//TILE
+    rows=qkv_ref.shape[1]; local=rows//nsrc; per=local//RUN; n=rows//TILE
     nseg=path.shape[1]
     for s in range(nsrc):
         for j in range(per):
             d=pl.multiple_of(place[t,s*per+j]*RUN,RUN)
-            blk=ins[s][0,j*RUN:(j+1)*RUN,:]
+            blk=qkv_ref[0,s*local+j*RUN:s*local+(j+1)*RUN,:]
             qs[pl.ds(d,RUN),:]=blk[:,0:HD]; ks[pl.ds(d,RUN),:]=blk[:,HD:2*HD]; vs[pl.ds(d,RUN),:]=blk[:,2*HD:]
             gs[pl.ds(d,RUN),:]=gin[s][0,j*RUN:(j+1)*RUN,:]; os[pl.ds(d,RUN),:]=oin[s][0,j*RUN:(j+1)*RUN,:]
     pos=lax.broadcasted_iota(jnp.int32,(rows,HD),0)
@@ -169,22 +169,24 @@
     for s in range(nsrc):
         for j in range(per):
             d=pl.multiple_of(place[t,s*per+j]*RUN,RUN)
-            outs[s][0,j*RUN:(j+1)*RUN,:]=sorted_out[pl.ds(d,RUN),:]
-
-def attention_bwd(tables,parts,oparts,gparts,lse):
+            blk=sorted_out[pl.ds(d,RUN),:]
+            whole_ref[0,s*local+j*RUN:s*local+(j+1)*RUN,:]=blk
+            if s: outs[s-1][0,j*RUN:(j+1)*RUN,:]=blk
+
+def attention_bwd(tables,qkv,oparts,gparts,lse):
     place,starts,path,code=tables
-    nsrc=len(parts); T,local,_=parts[0].shape; rows=nsrc*local; n=rows//TILE
+    nsrc=len(oparts); T,rows,_=qkv.shape; local=rows//nsrc; n=rows//TILE
     bs=lambda w: pl.BlockSpec((1,local,w),lambda t,*_:(t,0,0))
     return pl.pallas_call(partial(bwd_kernel,nsrc),
         grid_spec=pltpu.PrefetchScalarGridSpec(num_scalar_prefetch=4,grid=(T,),
-            in_specs=[bs(3*HD)]*nsrc+[bs(HD)]*(2*nsrc)+[pl.BlockSpec((1,n,TILE),lambda t,*_:(t,0,0))],
-            out_specs=[bs(3*HD)]*nsrc,
+            in_specs=[pl.BlockSpec((1,rows,3*HD),lambda t,*_:(t,0,0))]+[bs(HD)]*(2*nsrc)+[pl.BlockSpec((1,n,TILE),lambda t,*_:(t,0,0))],
+            out_specs=[bs(3*HD)]*(nsrc-1)+[pl.BlockSpec((1,rows,3*HD),lambda t,*_:(t,0,0))],
             scratch_shapes=[pltpu.VMEM((rows,HD),BF16)]*5+[pltpu.VMEM((rows,HD),jnp.int32),pltpu.VMEM((n,TILE),jnp.int32),
                pltpu.VMEM((n,TILE),F32),pltpu.VMEM((rows,HD),F32),pltpu.VMEM((TILE,HD),F32),pltpu.VMEM((TILE,HD),F32),
                pltpu.VMEM((rows,3*HD),BF16)]),
-        out_shape=[jax.ShapeDtypeStruct((T,local,3*HD),BF16)]*nsrc,
-        cost_estimate=pl.CostEstimate(flops=T*rows*rows*HD*5,bytes_accessed=T*rows*HD*20,transcendentals=T*rows*rows//2),
-        name="tree_attention_back")(place,starts,path,code,*parts,*oparts,*gparts,lse)
+        out_shape=[jax.ShapeDtypeStruct((T,local,3*HD),BF16)]*(nsrc-1)+[jax.ShapeDtypeStruct((T,rows,3*HD),BF16)],
+        cost_estimate=pl.CostEstimate(flops=T*rows*rows*HD*25,bytes_accessed=T*rows*HD*20,transcendentals=T*rows*rows//2),
+        name="tree_attention_back")(place,starts,path,code,qkv,*oparts,*gparts,lse)
 
 
 def tree_tables(place, starts, parent, rows):
@@ -238,10 +240,11 @@
             x0_ref[0, :, here] = xk
 
 
-def first_norm(quarter, chunk, tokens, cotangent, gain, shift):
-    trees, rows, width = tokens.shape
+def first_norm(quarter, chunk, tokens, cotangent, gain, shift, block_rows):
+    trees, _, width = tokens.shape
     parts = quarter.shape[0]
-    block = (1, rows // parts, width)
+    rows = parts * block_rows
+    block = (1, block_rows, width)
     come = pl.BlockSpec(block, lambda i, r, q, c: (i, q[r], 0))
     go = pl.BlockSpec(block, lambda i, r, q, c: (i, r, 0))
     row = pl.BlockSpec((1, width), lambda i, r, q, c: (0, 0))
@@ -265,29 +268,40 @@
     )(quarter, chunk, tokens, cotangent, gain, shift)
 
 
-def replace_kernel(pieces, quarter, chunk, x_ref, o_ref):
-    part = x_ref.shape[1] // pieces
-    for k in range(pieces):
-        there = pl.ds(pl.multiple_of(chunk[k] * part, part), part)
-        o_ref[:, there] = x_ref[:, k * part : (k + 1) * part]
-
-
-def replace(quarter, chunk, value):
-    rows, width = value.shape
-    parts = quarter.shape[0]
-    block = (rows // parts, width)
+def replace_kernel(pieces, trees, quarter, chunk, *refs):
+    o_ref = refs[2 * trees]
+    part = o_ref.shape[2] // pieces
+    step = pl.program_id(0)
+    for half in range(2):
+
+        @pl.when((step >= pl.num_programs(0) // 2) == (half == 1))
+        def _():
+            for i in range(trees):
+                for k in range(pieces):
+                    there = pl.ds(pl.multiple_of(chunk[k] * part, part), part)
+                    o_ref[i, :, there] = refs[2 * i + half][:, k * part : (k + 1) * part]
+
+
+def replace(quarter, chunk, values):
+    half_rows, width = values[0][0].shape
+    trees, parts = len(values), quarter.shape[0]
+    turn = parts // 2
+    block = (half_rows // turn, width)
+    first = pl.BlockSpec(block, lambda r, q, c: (jnp.minimum(r, turn - 1), 0))
+    second = pl.BlockSpec(block, lambda r, q, c: (jnp.maximum(r - turn, 0), 0))
+    flat = [half for value in values for half in value]
     return pl.pallas_call(
-        partial(replace_kernel, chunk.shape[0]),
+        partial(replace_kernel, chunk.shape[0], trees),
         grid_spec=pltpu.PrefetchScalarGridSpec(
             num_scalar_prefetch=2,
             grid=(parts,),
-            in_specs=[pl.BlockSpec(block, lambda r, q, c: (r, 0))],
-            out_specs=pl.BlockSpec(block, lambda r, q, c: (q[r], 0)),
+            in_specs=[first, second] * trees,
+            out_specs=pl.BlockSpec((trees,) + block, lambda r, q, c: (0, q[r], 0)),
         ),
-        out_shape=jax.ShapeDtypeStruct((rows, width), value.dtype),
-        cost_estimate=pl.CostEstimate(flops=0, bytes_accessed=4 * value.size, transcendentals=0),
+        out_shape=jax.ShapeDtypeStruct((trees, 2 * half_rows, width), values[0][0].dtype),
+        cost_estimate=pl.CostEstimate(flops=0, bytes_accessed=4 * trees * half_rows * width, transcendentals=0),
         name="replace",
-    )(quarter, chunk, value)
+    )(quarter, chunk, *flat)
 
 
 def per_device(
@@ -319,7 +333,8 @@
     part = width // n_f
     local_width = query_weight.shape[1]
     heads = local_width // HD
-    mine = heads // n_c
+    assert heads == n_c
+    span = 3 * HD
     bits, order = hypercube(n_t)
     quarter_rows = rows // n_t
 
@@ -331,6 +346,9 @@
 
     def flip_t(v, b):
         return lax.ppermute(v, "tp", [(i, i ^ (1 << b)) for i in range(n_t)])
+
+    def after(v, *others):
+        return lax.optimization_barrier((v,) + others)[0]
 
     def pieces_of(v):
         return [v] + [shift_f(v, -k) for k in range(1, n_f)]
@@ -347,6 +365,16 @@
             v = jnp.concatenate([v, flip_t(v, b)], axis=0)
         return v
 
+    def both_halves(v, axis=0):
+        for b in reversed(range(1, bits)):
+            v = jnp.concatenate([v, flip_t(v, b)], axis=axis)
+        return v, flip_t(v, 0)
+
+    both = jnp.concatenate(
+        [up_weight[:, k * part : (k + 1) * part] for k in range(up_weight.shape[1] // part)] + [down_weight], axis=0
+    )
+    every = lax.all_gather(both, "fsdp")
+
     quarter = jnp.stack([t ^ r for r in order]).astype(jnp.int32)
     chunk = jnp.stack([(f + k) % n_f for k in range(n_f)]).astype(jnp.int32)
 
@@ -360,18 +388,27 @@
     )
     gain1, shift1, gain2, shift2, bias_out, bias_down = (vectors[i : i + 1] for i in range(6))
 
+    def my_head(q, k, v):
+        return jnp.concatenate(
+            [lax.dynamic_slice_in_dim(a, c * HD, HD, axis=1) for a in (q, k, v)], axis=1
+        )
+
     def by_head(q, k, v):
         stacked = jnp.stack([a.reshape(a.shape[0], heads, HD) for a in (q, k, v)], axis=2)
         doubled = jnp.concatenate([stacked, stacked], axis=1)
-        turned = lax.dynamic_slice_in_dim(doubled, c * mine, heads, axis=1)
-        return turned.reshape(q.shape[0], heads * 3 * HD)
-
-    w_qkv = pieces_of(by_head(query_weight, key_weight, value_weight))
+        turned = lax.dynamic_slice_in_dim(doubled, c, heads, axis=1)
+        return turned.reshape(q.shape[0], heads * span)
+
+    w_own = pieces_of(my_head(query_weight, key_weight, value_weight))
     w_out = jnp.concatenate([out_weight, out_weight], axis=0)
-    w_out = pieces_of(lax.dynamic_slice_in_dim(w_out, c * mine * HD, local_width, axis=0))
-    w_up = pieces_of(up_weight)
-    w_down = pieces_of(down_weight)
-    bias_qkv = by_head(query_bias[None], jnp.zeros_like(query_bias)[None], value_bias[None])
+    w_out = pieces_of(lax.dynamic_slice_in_dim(w_out, c * HD, local_width, axis=0))
+    units = up_weight.shape[1]
+    w_up, w_down = [up_weight], [down_weight]
+    for k in range(1, n_f):
+        other = lax.dynamic_index_in_dim(every, chunk[k], 0, keepdims=False)
+        w_up.append(jnp.concatenate([other[j * part : (j + 1) * part] for j in range(units // part)], axis=1))
+        w_down.append(other[units:])
+    bias_own = my_head(query_bias[None], jnp.zeros_like(query_bias)[None], value_bias[None])
 
     n_seg = parent_table.shape[1]
 
@@ -387,13 +424,26 @@
     )
     info = jnp.concatenate([places, ahead], axis=1)
     infos = [info] + [shift_c(info, k) for k in range(1, n_c)]
+
+    tokens = after(tokens, both, *infos)
+    normed0, inputs0, dy0 = first_norm(
+        quarter[:1], chunk, tokens, cotangent, gain1, shift1, quarter_rows
+    )
+    rings = []
+    for i in range(trees):
+        ring = [normed0[i] if i == 0 else after(normed0[i], rings[-1][-1])]
+        for k in range(1, n_c):
+            ring.append(shift_c(ring[-1], 1))
+        rings.append(ring)
+    normed, _, dy = first_norm(quarter, chunk, after(tokens, normed0), cotangent, gain1, shift1, quarter_rows)
+    infos = lax.optimization_barrier((*infos, normed))[:n_c]
+    normed = after(normed, rings[0][min(2, n_c - 1)], *w_own[1:])
+
     runs = places.shape[1]
     place = jnp.concatenate([v[:, :runs] for v in infos], axis=1)
     starts = sum(v[:, runs:] for v in infos)
     tables = tree_tables(place, starts, parent_table, n_c * rows)
 
-    normed, inputs0, dy = first_norm(quarter, chunk, tokens, cotangent, gain1, shift1)
-
     def cols(v, k):
         return v[:, k * part : (k + 1) * part]
 
@@ -410,60 +460,82 @@
         return jnp.concatenate([nt(v, p) for p in pieces], axis=1)
 
     def to_heads(v, width_each):
-        span = mine * width_each
-        return [v[:, :span]] + [shift_c(v[:, k * span : (k + 1) * span], k) for k in range(1, n_c)]
+        return [v[:, :width_each]] + [
+            shift_c(v[:, k * width_each : (k + 1) * width_each], k) for k in range(1, n_c)
+        ]
 
     def from_heads(parts):
         return [parts[0]] + [shift_c(parts[k], -k) for k in range(1, n_c)]
 
-    def absolute(parts):
-        doubled = jnp.stack(parts + parts)
-        turned = lax.dynamic_slice_in_dim(doubled, (n_c - c) % n_c, n_c, axis=0)
-        return jnp.concatenate([turned[k] for k in range(n_c)], axis=1)
+    far = [[both_halves(ring[k]) for k in range(1, n_c)] for ring in rings]
+    w_qkv = [by_head(query_weight, key_weight, value_weight)]
+    w_far = [lax.all_gather(after(v, ring[-1]), "ctx") for v in w_own[1:]]
 
     kept = []
     for i in range(trees):
         table = tuple(v[i : i + 1] for v in tables)
-        qkv = (times(normed[i], w_qkv) + bias_qkv).astype(BF16)
-        parts = to_heads(qkv, 3 * HD)
-        parts = [v[None] for v in parts]
-        *attended_parts, lse = attention_fwd(table, parts)
-        attended = from_heads([v[0] for v in attended_parts])
-        attended_here = jnp.concatenate(attended, axis=1)
+        everyone = lax.pad(normed[i], jnp.zeros((), BF16), ((0, (n_c - 1) * rows, 0), (0, 0, 0)))
+        for k in range(1, n_c):
+            for r, half in enumerate(far[i][k - 1]):
+                everyone = lax.dynamic_update_slice(everyone, half, (k * rows + r * (rows // 2), 0))
+        qkv = (times(everyone, w_own) + bias_own).astype(BF16)[None]
+        *attended_parts, lse = attention_fwd(table, n_c, qkv)
+        attended = jnp.concatenate(from_heads([v[0] for v in attended_parts]), axis=1)
         x0 = inputs0[i].astype(F32)
-        middle = x0 + sum_rows(wide(attended_here, w_out)) + bias_out
+        middle = x0 + sum_rows(wide(attended, w_out)) + bias_out
         mean = jnp.mean(middle, axis=1, keepdims=True)
         spread = jnp.mean((middle - mean) * (middle - mean), axis=1, keepdims=True)
         rstd = lax.rsqrt(spread + EPS)
         unit = (middle - mean) * rstd
-        normed_mid = all_rows((unit * gain2 + shift2).astype(BF16))
-        kept.append((table, parts, attended_parts, lse, attended, x0, middle, unit, rstd, normed_mid))
-
-    results = []
-    back = []
+        normed_mid = (unit * gain2 + shift2).astype(BF16)
+        if i == 0:
+            normed_mid = after(normed_mid, w_qkv[0])
+        normed_mid = all_rows(normed_mid)
+        kept.append((table, qkv, attended_parts, lse, attended, x0, middle, unit, rstd, normed_mid, everyone))
+
+    for v in w_far:
+        w_qkv.append(
+            jnp.concatenate(
+                [lax.dynamic_index_in_dim(v, (c + j) % n_c, 0, keepdims=False) for j in range(n_c)], axis=1
+            )
+        )
+
+    inner = []
     for i in range(trees):
-        table, parts, attended_parts, lse, attended, x0, middle, unit, rstd, normed_mid = kept[i]
+        normed_mid = kept[i][9]
         hidden = times(normed_mid, w_up) + up_bias[None]
         cdf = 0.5 * (1.0 + lax.erf(hidden * math.sqrt(0.5)))
         slope = cdf + hidden * (jnp.exp(-0.5 * hidden * hidden) * (1.0 / math.sqrt(2.0 * math.pi)))
         active = (hidden * cdf).astype(BF16)
         grad_hidden = (times_back(dy[i], w_down) * slope).astype(BF16)
-        grad_mid = sum_rows(wide_back(grad_hidden, w_up))
+        inner.append((active, grad_hidden, wide_back(grad_hidden, w_up)))
+
+    dys = dy.reshape(trees * rows, width)
+    down_product = [tn(jnp.concatenate([v[0] for v in inner], axis=0), cols(dys, k)) for k in range(n_f)]
+    down_product[1:] = [v.astype(BF16) for v in down_product[1:]]
+
+    back = []
+    for i in range(trees):
+        x0, middle, unit, rstd, normed_mid = kept[i][5:10]
+        active, grad_hidden, grad_mid = inner[i]
+        grad_mid = sum_rows(grad_mid)
         g = grad_mid * gain2
         moved = rstd * (
             g - jnp.mean(g, axis=1, keepdims=True) - unit * jnp.mean(g * unit, axis=1, keepdims=True)
         )
         grad_middle = dy[i, :quarter_rows].astype(F32) + moved
         branch0 = grad_middle.astype(BF16)
+        if i == 0:
+            branch0 = after(branch0, *down_product[1:])
         branch = all_rows(branch0)
-        result = middle + sum_rows(wide(active, w_down)) + bias_down
-        results.append(all_rows(result.astype(BF16)))
         back.append(
             dict(
                 active=active,
                 grad_hidden=grad_hidden,
                 normed_mid=normed_mid,
+                attended=kept[i][4],
                 branch=branch,
+                branch0=branch0,
                 grad_middle=grad_middle,
                 gain2=jnp.sum(grad_mid * unit, axis=0),
                 shift2=jnp.sum(grad_mid, axis=0),
@@ -476,30 +548,72 @@
     def whole(name):
         return jnp.concatenate([b[name] for b in back], axis=0)
 
-    def scatter(parts, axis):
+    def in_order(v):
+        return jnp.concatenate(
+            [lax.dynamic_slice_in_dim(v, ((n_f + k - f) % n_f) * part, part, axis=1) for k in range(n_f)], axis=1
+        )
+
+    def sent(parts):
+        return [parts[0]] + [shift_f(parts[k].astype(BF16), k) for k in range(1, n_f)]
+
+    def joined(parts, *others):
         total = parts[0].astype(F32)
         for k in range(1, n_f):
-            total = total + shift_f(parts[k].astype(BF16), k).astype(F32)
-        return lax.psum_scatter(
-            total.astype(BF16), "ctx", scatter_dimension=axis, tiled=True
-        ).astype(F32)
-
-    dys = dy.reshape(trees * rows, width)
-    active, grad_hidden, normed_mid = whole("active"), whole("grad_hidden"), whole("normed_mid")
-    g_down = scatter([tn(active, cols(dys, k)) for k in range(n_f)], 1)
-    g_up = scatter([tn(cols(normed_mid, k), grad_hidden) for k in range(n_f)], 0)
+            total = total + after(parts[k], *others).astype(F32)
+        return total.astype(BF16)
+
+    def scatter(v, axis):
+        return lax.psum_scatter(v, "ctx", scatter_dimension=axis, tiled=True).astype(F32)
+
+    grad_hidden, normed_mid = whole("grad_hidden"), whole("normed_mid")
+    part_down = sent(down_product)
+    part_up = sent([tn(cols(normed_mid, k), grad_hidden) for k in range(n_f)])
+
+    grad_attended = jnp.stack([times_back(b["branch"], w_out).astype(BF16) for b in back])
+    grad_parts = [grad_attended[:, :, :HD]] + [
+        shift_c(grad_attended[:, :, k * HD : (k + 1) * HD], k) for k in range(1, n_c)
+    ]
+    grad_parts = [[v[i : i + 1] for v in grad_parts] for i in range(trees)]
 
     heads_back = []
+    own_back = []
     for i in range(trees):
-        table, parts, attended_parts, lse, attended, x0 = kept[i][:6]
-        grad_attended = times_back(back[i]["branch"], w_out).astype(BF16)
-        grad_parts = [v[None] for v in to_heads(grad_attended, HD)]
-        back_parts = attention_bwd(table, parts, attended_parts, grad_parts, lse)
-        heads_back.append(from_heads([v[0] for v in back_parts]))
-
-    branch = whole("branch")
-    attended_abs = jnp.concatenate([absolute(k[4]) for k in kept], axis=0)
-    g_out = scatter([tn(attended_abs, cols(branch, k)) for k in range(n_f)], 1)
+        table, qkv, attended_parts, lse = kept[i][:4]
+        if i == 0:
+            total_down = joined(part_down, *[v for parts in grad_parts for v in parts])
+            g_down = scatter(total_down, 1)
+            ahead = [total_down, *w_far]
+        else:
+            ahead = heads_back[0] + [sums]
+        *back_parts, own = attention_bwd(table, after(qkv, *ahead), attended_parts, grad_parts[i], lse)
+        own_back.append(own[0])
+        heads_back.append(from_heads([own[0, :rows]] + [v[0] for v in back_parts]))
+        if i == 0:
+            partial_sums = [
+                wide(after(b["active"], own_back[0]), w_down).reshape(n_t, quarter_rows, width) for b in back
+            ]
+            sums = sum_rows(jnp.concatenate(partial_sums, axis=1)).reshape(trees, quarter_rows, width)
+    results = both_halves(
+        jnp.stack([kept[i][6] + sums[i] + bias_down for i in range(trees)]).astype(BF16), 1
+    )
+    results = [[half[i] for half in results] for i in range(trees)]
+
+    total_up = joined(part_up, own_back[-1])
+    g_up = scatter(after(total_up, g_down), 0)
+
+    attended = after(whole("attended"), own_back[-1])
+    attended = lax.dynamic_slice_in_dim(
+        jnp.concatenate([attended, attended], axis=1), ((n_c - c) % n_c) * HD, local_width, axis=1
+    )
+    branch = after(whole("branch"), own_back[-1])
+    part_out = sent([tn(attended, cols(branch, k)) for k in range(n_f)])
+    own_back = [after(v, *(w for h in heads_back for w in h)) for v in own_back]
+    part_own = sent([sum(tn(cols(kept[i][10], k), own_back[i]) for i in range(trees)) for k in range(n_f)])
+    own_total = joined(part_own, total_up)
+    share = part // n_c
+
+    def own_rows(k):
+        return lax.dynamic_slice_in_dim(own_total, ((c + k) % n_c) * share, share, axis=0)
 
     grads = []
     for i in range(trees):
@@ -515,51 +629,62 @@
         moved = rstd * (
             g - jnp.mean(g, axis=1, keepdims=True) - unit * jnp.mean(g * unit, axis=1, keepdims=True)
         )
-        grads.append(all_rows((grad_middle + moved).astype(BF16)))
-
-    dqkv = jnp.concatenate([absolute(v) for v in heads_back], axis=0)
-    normed_all = normed.reshape(trees * rows, width)
-    g_qkv = scatter([tn(cols(normed_all, k), dqkv) for k in range(n_f)], 0)
-    bias_sums = jnp.sum(dqkv.astype(F32), axis=0)
-
-    def split_heads(v):
-        apart = v.reshape(v.shape[0], heads, 3, HD)
-        return [apart[:, :, k].reshape(v.shape[0], heads * HD) for k in range(3)]
-
-    g_query, g_key, g_value = split_heads(g_qkv)
-    query_sum, _, value_sum = split_heads(bias_sums[None])
+        grads.append(both_halves((grad_middle + moved).astype(BF16)))
+
+    come = [own_rows(0)] + [shift_c(own_rows(k), k) for k in range(1, n_c)]
+
+    def by_source(parts):
+        turned = jnp.stack([parts[(n_c - k) % n_c] for k in range(n_c)] * 2)
+        return lax.dynamic_slice_in_dim(turned, (n_c - c) % n_c, n_c, axis=0)
+
+    come = list(lax.optimization_barrier((*come, *[half for v in grads for half in v])))[:n_c]
+    come = by_source(come).astype(F32)
+    g_query, g_key, g_value = (
+        jnp.concatenate([come[h, :, k * HD : (k + 1) * HD] for h in range(heads)], axis=1) for k in range(3)
+    )
+
+    g_out = scatter(after(joined(part_out, back[-1]["shift1"]), g_up), 1)
+
     names = ("gain1", "shift1", "out_bias", "gain2", "shift2", "down_bias")
     rolled = jnp.stack([sum(b[name] for b in back) for name in names])
-    turned = jnp.concatenate(
-        [
-            lax.dynamic_slice_in_dim(rolled, ((n_f + k - f) % n_f) * part, part, axis=1)
-            for k in range(n_f)
-        ],
-        axis=1,
-    )
-    turned = lax.psum(turned, ("fsdp", "ctx", "tp"))
-    span = part // n_c
-    own = lax.dynamic_slice_in_dim(turned, f * part + c * span, span, axis=1)
-    unit_sums = jnp.concatenate(
-        [query_sum[0], value_sum[0], sum(b["up_bias"] for b in back)], axis=0
-    )
-    unit_sums = lax.psum(unit_sums, ("fsdp", "ctx"))
+    for b in range(bits):
+        rolled = rolled + flip_t(rolled, b)
+    mine_f = cols(rolled, 0)
+    for k in range(1, n_f):
+        mine_f = mine_f + shift_f(cols(rolled, k), k)
+
+    def own_share(k):
+        return lax.dynamic_slice_in_dim(mine_f, ((c + k) % n_c) * share, share, axis=1)
+
+    own = own_share(0)
+    for k in range(1, n_c):
+        own = own + shift_c(own_share(k), k)
+
+    head_sum = sum(jnp.sum(v.astype(F32), axis=0) for v in own_back)
+    head_sum = after(head_sum, grads[-1][0])
+    unit_sum = sum(b["up_bias"] for b in back)
+    sums = jnp.concatenate([head_sum, unit_sum], axis=0)[None]
+    for k in range(1, n_f):
+        sums = sums + shift_f(jnp.concatenate([head_sum, unit_sum], axis=0)[None], k)
+    all_sums = [sums] + [shift_c(sums, k) for k in range(1, n_c)]
+    g_up_bias = sum(v[0, span:] for v in all_sums)
+    by_head_sum = by_source([v[0, :span] for v in all_sums])
     return (
-        jnp.stack([replace(quarter, chunk, v) for v in results]),
-        jnp.stack([replace(quarter, chunk, v) for v in grads]),
+        replace(quarter, chunk, results),
+        replace(quarter, chunk, grads),
         own[0],
         own[1],
         g_query,
-        unit_sums[:local_width],
+        by_head_sum[:, :HD].reshape(local_width),
         g_key,
         g_value,
-        unit_sums[local_width : 2 * local_width],
+        by_head_sum[:, 2 * HD :].reshape(local_width),
         g_out,
         own[2],
         own[3],
         own[4],
         g_up,
-        unit_sums[2 * local_width :],
+        g_up_bias,
         g_down,
         own[5],
     )

time: 1230 us -> 857 us (0.70)
  waiting for transfers between devices: 542 us -> 304 us
  matrix products: 221 us -> 149 us
  blocking collectives: 71.6 us -> 0 us
  local copies, waits for them, and re-layouts: 50.6 us -> 103 us
  starting transfers between devices: 100 us -> 68 us
    ppermute x8, waiting for transfers between devices: 286 us -> 41.8 us  [shift_f(): return lax.ppermute(v, 'fsdp', [(i, (i + k) % n_f) for i in range(n_f)])]
    psum x2 -> x0, blocking collectives: 71.6 us -> none  [the longest x1 38 us: per_device(): turned = lax.psum(turned, ('fsdp', 'ctx', 'tp'))]
    ppermute x32 -> x42, waiting for transfers between devices: 95.5 us -> 142 us  [flip_t(): return lax.ppermute(v, 'tp', [(i, i ^ 1 << b) for i in range(n_t)])]
    ppermute x27 -> x33, waiting for transfers between devices: 160 us -> 117 us  [shift_c(): return lax.ppermute(v, 'ctx', [(i, (i + k) % n_c) for i in range(n_c)])]
    dot_general x8 -> x10, matrix products: 84.7 us -> 47 us  [tn(): lax.dot_general(a, b, (((0,), (0,)), ((), ())), preferred_element_type=F32)]
    ppermute x27 -> x33, starting transfers between devices: 71.1 us -> 38.1 us  [shift_c(): return lax.ppermute(v, 'ctx', [(i, (i + k) % n_c) for i in range(n_c)])]
    dot_general x16, matrix products: 74.8 us -> 51.1 us  [nt(): lax.dot_general(a, b, (((1,), (1,)), ((), ())), preferred_element_type=F32)]
    reduce_sum x1 -> x2, other arithmetic: 20.1 us -> 0.78 us  [per_device(): head_sum = sum((jnp.sum(v.astype(F32), axis=0) for v in own_back))]
  transfers between devices with their start and end apart: 71 -> 88, of which waited for: 27 -> 37; matrix products, arithmetic and copies ran while one was open for 28% -> 37% of each run, Pallas kernels for 10% -> 14%
where the time goes in v2:
time: 857 us; the launch traced here: 844 us
  waiting for transfers between devices  304 us (35%)
  matrix products  149 us (17%)
  Pallas kernels  117 us (14%)
  local copies, waits for them, and re-layouts  103 us (12%)
  other arithmetic  85.8 us (10%)
  starting transfers between devices  68 us (8%)
  between operations  16.5 us (2%)
    ppermute x42, waiting for transfers between devices, flip_t(): return lax.ppermute(v, 'tp', [(i, i ^ 1 << b) for i in range(n_t)])  142 us
    ppermute x33, waiting for transfers between devices, shift_c(): return lax.ppermute(v, 'ctx', [(i, (i + k) % n_c) for i in range(n_c)])  117 us
    dot_general x16, matrix products, nn(): lax.dot_general(a, b, (((1,), (0,)), ((), ())), preferred_element_type=F32)  51.3 us
    dot_general x16, matrix products, nt(): lax.dot_general(a, b, (((1,), (1,)), ((), ())), preferred_element_type=F32)  51.1 us
    pallas_call x2, Pallas kernels, attention_bwd(): pl.pallas_call(partial(bwd_kernel, nsrc), grid_spec=pltpu.PrefetchScalarG...  48.4 us
    dot_general x10, matrix products, tn(): lax.dot_general(a, b, (((0,), (0,)), ((), ())), preferred_element_type=F32)  47 us
    unnamed x310, local copies, waits for them, and re-layouts  43.6 us
    ppermute x8, waiting for transfers between devices, shift_f(): return lax.ppermute(v, 'fsdp', [(i, (i + k) % n_f) for i in range(n_f)])  41.8 us
  transfers between devices with their start and end apart: 88, of which 37 were waited for; matrix products, arithmetic and copies ran while one was open for 37% of the time, Pallas kernels for 14%

profile of v2, /device:TPU:0, one launch (start us, length us, event | category | flops | bytes accessed | tf_op | source)
XLA Modules:
  0.0 844.3 jit_solution(5986840361409541024)
XLA Ops:
  25.8 4.2 pad_maximum_fusion
  34.2 4.9 first_norm.2
  42.0 11.9 %first_norm.3 = (bf16[2,512,2048]{2,1,0:T(8,128)(2,1)}, bf16[2,128,2048]{2,1,0:T(8,128)(2,1)}, bf16[2,512,2048]{2,1,0:T(8,128)(2,1)}) custom-call(s32[4]{0:T(128)} %pad_add_fusion.2.quarter, s32[2]{0:T(128)} %pad_add_fusion.3.chunk, bf16[2,512,2048]{2,1,0:T(8,128)(2,1)} %x_ref.1, bf16[2,512,2048]{2,1,0:T(8,128)(2,1)} %dy_ref.3, ...), custom_call_target="tpu_custom_call" | custom-call | flops 20971520 | bytes 16777216 | tf_op jit(solution)/shard_map/first_norm/pallas_call | solution.py:251
  59.8 8.8 %collective-permute-done.4 = bf16[128,2048]{1,0:T(8,128)(2,1)} collective-permute-done((bf16[128,2048]{1,0:T(8,128)(2,1)S(1)}, bf16[128,2048]{1,0:T(8,128)(2,1)}, u32[]{:S(2)}, u32[]{:S(2)}) %collective-permute-start.4) | collective-permute-done | bytes 524320 | tf_op jit(solution)/shard_map/ppermute | solution.py:345
  76.7 4.5 collective-permute-done.10
  88.2 5.0 collective-permute-done.11
  100.7 8.1 collective-permute-done.22
  109.6 3.8 collective-permute-done.24
  120.5 3.6 fusion.43.refs_0_
  124.1 20.2 %tree_attention.2 = (bf16[1,512,128]{2,1,0:T(8,128)(2,1)}, bf16[1,512,128]{2,1,0:T(8,128)(2,1)}, bf16[1,512,128]{2,1,0:T(8,128)(2,1)}, bf16[1,512,128]{2,1,0:T(8,128)(2,1)}, f32[1,8,256]{2,1,0:T(8,128)}) custom-call(s32[1,32]{1,0:T(1,128)} %get-tuple-element.252.place, s32[1,7]{1,0:T(1,128)} %get-tuple-element.271.starts, s32[1,7]{1,0:T(1,128)} %get-tuple-element.248.path, ...), custom_call_target="tpu_custom_call" | custom-call | flops 10737418240 | bytes 2097152 | tf_op jit(solution)/shard_map/tree_attention/pallas_call | solution.py:101
  144.3 3.8 collective-permute-start.13
  152.8 4.7 collective-permute-done.14
  161.2 3.3 fusion.155
  170.3 3.5 fusion.46.refs_0_
  173.9 19.7 %tree_attention.3 = (bf16[1,512,128]{2,1,0:T(8,128)(2,1)}, bf16[1,512,128]{2,1,0:T(8,128)(2,1)}, bf16[1,512,128]{2,1,0:T(8,128)(2,1)}, bf16[1,512,128]{2,1,0:T(8,128)(2,1)}, f32[1,8,256]{2,1,0:T(8,128)}) custom-call(s32[1,32]{1,0:T(1,128)} %get-tuple-element.253.place, s32[1,7]{1,0:T(1,128)} %get-tuple-element.270.starts, s32[1,7]{1,0:T(1,128)} %get-tuple-element.249.path, ...), custom_call_target="tpu_custom_call" | custom-call | flops 10737418240 | bytes 2097152 | tf_op jit(solution)/shard_map/tree_attention/pallas_call | solution.py:101
  193.6 3.5 collective-permute-start.30
  201.6 9.6 %collective-permute-done.31 = bf16[512,128]{1,0:T(8,128)(2,1)S(1)} collective-permute-done((bf16[512,128]{1,0:T(8,128)(2,1)}, bf16[512,128]{1,0:T(8,128)(2,1)S(1)}, u32[]{:S(2)}, u32[]{:S(2)}) %collective-permute-start.31) | collective-permute-done | bytes 131104 | tf_op jit(solution)/shard_map/ppermute | solution.py:345
  230.4 3.5 fusion.33
  234.6 6.8 collective-permute-done.18
  241.4 10.8 %collective-permute-done.34 = bf16[128,2048]{1,0:T(8,128)(2,1)S(1)} collective-permute-done((bf16[128,2048]{1,0:T(8,128)(2,1)S(1)}, bf16[128,2048]{1,0:T(8,128)(2,1)S(1)}, u32[]{:S(2)}, u32[]{:S(2)}) %collective-permute-start.34) | collective-permute-done | bytes 524320 | tf_op jit(solution)/shard_map/ppermute | solution.py:348
  254.9 12.6 %collective-permute-done.19 = bf16[128,2048]{1,0:T(8,128)(2,1)S(1)} collective-permute-done((bf16[128,2048]{1,0:T(8,128)(2,1)S(1)}, bf16[128,2048]{1,0:T(8,128)(2,1)S(1)}, u32[]{:S(2)}, u32[]{:S(2)}) %collective-permute-start.19) | collective-permute-done | bytes 524320 | tf_op jit(solution)/shard_map/ppermute | solution.py:348
  274.0 10.9 %collective-permute-done.35 = bf16[128,2048]{1,0:T(8,128)(2,1)S(1)} collective-permute-done((bf16[128,2048]{1,0:T(8,128)(2,1)S(1)}, bf16[128,2048]{1,0:T(8,128)(2,1)S(1)}, u32[]{:S(2)}, u32[]{:S(2)}) %collective-permute-start.35) | collective-permute-done | bytes 524320 | tf_op jit(solution)/shard_map/ppermute | solution.py:348
  285.9 4.3 fusion.136
  290.3 4.4 fusion.130
  303.4 4.2 multiply_convert_fusion.1
  307.6 5.5 convert_reduce_fusion.1
  321.9 4.3 multiply_convert_fusion
  326.1 6.3 convert_reduce_fusion
  344.8 6.6 convolution_convert_fusion.1
  351.4 5.7 collective-permute-done.39
  357.1 10.8 %collective-permute-done.43 = bf16[128,2048]{1,0:T(8,128)(2,1)S(1)} collective-permute-done((bf16[128,2048]{1,0:T(8,128)(2,1)S(1)}, bf16[128,2048]{1,0:T(8,128)(2,1)S(1)}, u32[]{:S(2)}, u32[]{:S(2)}) %collective-permute-start.43) | collective-permute-done | bytes 524320 | tf_op jit(solution)/shard_map/ppermute | solution.py:348
  372.0 3.7 dynamic-slice_bitcast_fusion.10
  375.7 8.3 collective-permute-done.40
  392.5 6.2 convolution_convert_fusion
  398.7 7.1 collective-permute-done.44
  406.0 6.4 fusion.40
  430.0 4.2 collective-permute-done.48
  434.9 13.8 %collective-permute-done.47 = bf16[2,512,128]{2,1,0:T(8,128)(2,1)S(1)} collective-permute-done((bf16[2,512,128]{2,1,0:T(8,128)(2,1)S(1)}, bf16[2,512,128]{2,1,0:T(8,128)(2,1)S(1)}, u32[]{:S(2)}, u32[]{:S(2)}) %collective-permute-start.47) | collective-permute-done | bytes 262176 | tf_op jit(solution)/shard_map/ppermute | solution.py:345
  450.2 29.3 %collective-permute-done.37 = bf16[2048,1024]{1,0:T(8,128)(2,1)} collective-permute-done((bf16[2048,1024]{1,0:T(8,128)(2,1)}, bf16[2048,1024]{1,0:T(8,128)(2,1)}, u32[]{:S(2)}, u32[]{:S(2)}) %collective-permute-start.37) | collective-permute-done | bytes 4194336 | tf_op jit(solution)/shard_map/ppermute | solution.py:342
  479.4 5.8 add_convert_fusion.1
  485.3 24.5 %tree_attention_back.2 = (bf16[1,512,384]{2,1,0:T(8,128)(2,1)}, bf16[1,512,384]{2,1,0:T(8,128)(2,1)}, bf16[1,512,384]{2,1,0:T(8,128)(2,1)}, bf16[1,2048,384]{2,1,0:T(8,128)(2,1)}) custom-call(s32[1,32]{1,0:T(1,128)} %get-tuple-element.252.place, s32[1,7]{1,0:T(1,128)} %get-tuple-element.271.starts, s32[1,7]{1,0:T(1,128)} %get-tuple-element.248.path, ...), custom_call_target="tpu_custom_call" | custom-call | flops 13421772800 | bytes 5242880 | tf_op jit(solution)/shard_map/tree_attention_back/pallas_call | solution.py:180
  509.8 4.5 fusion.211
  514.4 4.7 fusion.41
  522.2 4.5 fusion.42
  535.5 9.6 %collective-permute-done.53 = bf16[512,384]{1,0:T(8,128)(2,1)S(1)} collective-permute-done((bf16[512,384]{1,0:T(8,128)(2,1)S(1)}, bf16[512,384]{1,0:T(8,128)(2,1)S(1)}, u32[]{:S(2)}, u32[]{:S(2)}) %collective-permute-start.53) | collective-permute-done | bytes 393248 | tf_op jit(solution)/shard_map/ppermute | solution.py:345
  545.1 45.4 %collective-permute-done.54 = bf16[512,384]{1,0:T(8,128)(2,1)S(1)} collective-permute-done((bf16[512,384]{1,0:T(8,128)(2,1)S(1)}, bf16[512,384]{1,0:T(8,128)(2,1)S(1)}, u32[]{:S(2)}, u32[]{:S(2)}) %collective-permute-start.54) | collective-permute-done | bytes 393248 | tf_op jit(solution)/shard_map/ppermute | solution.py:345
  590.5 23.9 %tree_attention_back.3 = (bf16[1,512,384]{2,1,0:T(8,128)(2,1)}, bf16[1,512,384]{2,1,0:T(8,128)(2,1)}, bf16[1,512,384]{2,1,0:T(8,128)(2,1)}, bf16[1,2048,384]{2,1,0:T(8,128)(2,1)}) custom-call(s32[1,32]{1,0:T(1,128)} %get-tuple-element.253.place, s32[1,7]{1,0:T(1,128)} %get-tuple-element.270.starts, s32[1,7]{1,0:T(1,128)} %get-tuple-element.249.path, ...), custom_call_target="tpu_custom_call" | custom-call | flops 13421772800 | bytes 5242880 | tf_op jit(solution)/shard_map/tree_attention_back/pallas_call | solution.py:180
  618.7 3.8 fusion.152
  629.1 8.1 add_convert_fusion
  638.3 4.4 fusion.75
  643.6 7.9 collective-permute-done.61
  651.6 4.6 fusion.15
  659.0 3.2 fusion.151
  662.2 3.2 fusion.144
  674.4 9.7 %collective-permute-done.73 = bf16[1024,384]{1,0:T(8,128)(2,1)S(1)} collective-permute-done((bf16[1024,384]{1,0:T(8,128)(2,1)S(1)}, bf16[1024,384]{1,0:T(8,128)(2,1)S(1)}, u32[]{:S(2)}, u32[]{:S(2)}) %collective-permute-start.73) | collective-permute-done | bytes 786464 | tf_op jit(solution)/shard_map/ppermute | solution.py:342
  694.9 3.5 fusion.13
  715.4 4.2 fusion.104
  724.5 3.5 add_convert_fusion.4
  730.1 4.5 collective-permute-done.65
  741.0 25.4 %collective-permute-done.58 = bf16[128,2048]{1,0:T(8,128)(2,1)S(1)} collective-permute-done((bf16[128,2048]{1,0:T(8,128)(2,1)S(1)}, bf16[128,2048]{1,0:T(8,128)(2,1)S(1)}, u32[]{:S(2)}, u32[]{:S(2)}) %collective-permute-start.58) | collective-permute-done | bytes 524320 | tf_op jit(solution)/shard_map/ppermute | solution.py:348
  786.2 18.6 %collective-permute-done.51 = bf16[2,128,2048]{2,1,0:T(8,128)(2,1)S(1)} collective-permute-done((bf16[2,128,2048]{2,1,0:T(8,128)(2,1)S(1)}, bf16[2,128,2048]{2,1,0:T(8,128)(2,1)S(1)}, u32[]{:S(2)}, u32[]{:S(2)}) %collective-permute-start.51) | collective-permute-done | bytes 1048608 | tf_op jit(solution)/shard_map/ppermute | solution.py:348
  811.8 5.9 replace.3
  823.7 3.2 slice_bitcast_fusion.4
  826.9 5.9 replace.2
  (668 shorter events, 286.3 us)
Async XLA Ops:
  7.2 290.5 %all-gather.5.cloned.1.call-start = ((), (), s32[]{:S(2)}) async-start(), calls=%async_computation.6 | async-start | bytes 25165824 | tf_op jit(solution)/shard_map/all_gather | solution.py:376
  9.3 24.9 %collective-permute-start = (s32[2,15]{1,0:T(2,128)S(1)}, s32[2,15]{1,0:T(2,128)S(1)}, u32[]{:S(2)}, u32[]{:S(2)}) collective-permute-start(s32[2,15]{1,0:T(2,128)S(1)} %pad_add_fusion), channel_id=1, source_target_pairs={{0,4},{4,8},{8,12},{12,0},{1,5},{5,9},{9,13},{13,1},{2,6},{6,10},{... | collective-permute-start | bytes 368 | tf_op jit(solution)/shard_map/ppermute | solution.py:345
  12.3 21.8 %collective-permute-start.1 = (s32[2,15]{1,0:T(2,128)S(1)}, s32[2,15]{1,0:T(2,128)S(1)}, u32[]{:S(2)}, u32[]{:S(2)}) collective-permute-start(s32[2,15]{1,0:T(2,128)S(1)} %pad_add_fusion), channel_id=1, source_target_pairs={{0,8},{4,12},{8,0},{12,4},{1,9},{5,13},{9,1},{13,5},{2,10},{6,14},... | collective-permute-start | bytes 368 | tf_op jit(solution)/shard_map/ppermute | solution.py:345
  14.9 19.2 %collective-permute-start.2 = (s32[2,15]{1,0:T(2,128)S(1)}, s32[2,15]{1,0:T(2,128)S(1)}, u32[]{:S(2)}, u32[]{:S(2)}) collective-permute-start(s32[2,15]{1,0:T(2,128)S(1)} %pad_add_fusion), channel_id=1, source_target_pairs={{0,12},{4,0},{8,4},{12,8},{1,13},{5,1},{9,5},{13,9},{2,14},{6,2},{... | collective-permute-start | bytes 368 | tf_op jit(solution)/shard_map/ppermute | solution.py:345
  18.5 41.4 %collective-permute-start.5 = (bf16[1024,384]{1,0:T(8,128)(2,1)S(1)}, bf16[1024,384]{1,0:T(8,128)(2,1)S(1)}, u32[]{:S(2)}, u32[]{:S(2)}) collective-permute-start(bf16[1024,384]{1,0:T(8,128)(2,1)S(1)} %pad_maximum_fusion.30), channel_id=1, source_target_pairs={{0,16},{16,0},{1,17},{17,1},{2,18},{18,2},{3,19},{19,3},{4,20},{20... | collective-permute-start | bytes 2359304 | tf_op jit(solution)/shard_map/ppermute | solution.py:342
  22.3 138.9 %collective-permute-start.16 = (bf16[512,1024]{1,0:T(8,128)(2,1)}, bf16[512,1024]{1,0:T(8,128)(2,1)}, u32[]{:S(2)}, u32[]{:S(2)}) collective-permute-start(bf16[512,1024]{1,0:T(8,128)(2,1)} %fusion.119), channel_id=1, source_target_pairs={{0,16},{16,0},{1,17},{17,1},{2,18},{18,2},{3,19},{19,3},{4,20},{20... | collective-permute-start | bytes 3145736 | tf_op jit(solution)/shard_map/ppermute | solution.py:342
  30.1 341.9 %all-gather.7.cloned.1.call-start = ((), (), s32[]{:S(2)}) async-start(), calls=%async_computation.7 | async-start | bytes 3932160 | tf_op jit(solution)/shard_map/all_gather | solution.py:472
  41.4 14.0 %collective-permute-start.3 = (bf16[128,2048]{1,0:T(8,128)(2,1)S(1)}, bf16[128,2048]{1,0:T(8,128)(2,1)S(1)}, u32[]{:S(2)}, u32[]{:S(2)}) collective-permute-start(bf16[128,2048]{1,0:T(8,128)(2,1)S(1)} %get-tuple-element.200), channel_id=1, source_target_pairs={{0,4},{4,8},{8,12},{12,0},{1,5},{5,9},{9,13},{13,1},{2,6},{6,10},{... | collective-permute-start | bytes 1572872 | tf_op jit(solution)/shard_map/ppermute | solution.py:345
  55.4 13.2 %collective-permute-start.4 = (bf16[128,2048]{1,0:T(8,128)(2,1)S(1)}, bf16[128,2048]{1,0:T(8,128)(2,1)}, u32[]{:S(2)}, u32[]{:S(2)}) collective-permute-start(bf16[128,2048]{1,0:T(8,128)(2,1)S(1)} %collective-permute-done.3), channel_id=1, source_target_pairs={{0,4},{4,8},{8,12},{12,0},{1,5},{5,9},{9,13},{13,1},{2,6},{6,10},{... | collective-permute-start | bytes 1572872 | tf_op jit(solution)/shard_map/ppermute | solution.py:345
  57.7 14.7 %collective-permute-start.6 = (bf16[128,2048]{1,0:T(8,128)(2,1)S(1)}, bf16[128,2048]{1,0:T(8,128)(2,1)}, u32[]{:S(2)}, u32[]{:S(2)}) collective-permute-start(bf16[128,2048]{1,0:T(8,128)(2,1)S(1)} %collective-permute-done.3), channel_id=1, source_target_pairs={{0,2},{1,3},{2,0},{3,1},{4,6},{5,7},{6,4},{7,5},{8,10},{9,11},{10,... | collective-permute-start | bytes 1572872 | tf_op jit(solution)/shard_map/ppermute | solution.py:348
  68.7 12.6 %collective-permute-start.10 = (bf16[128,2048]{1,0:T(8,128)(2,1)}, bf16[128,2048]{1,0:T(8,128)(2,1)}, u32[]{:S(2)}, u32[]{:S(2)}) collective-permute-start(bf16[128,2048]{1,0:T(8,128)(2,1)} %collective-permute-done.4), channel_id=1, source_target_pairs={{0,4},{4,8},{8,12},{12,0},{1,5},{5,9},{9,13},{13,1},{2,6},{6,10},{... | collective-permute-start | bytes 1572872 | tf_op jit(solution)/shard_map/ppermute | solution.py:345
  71.2 14.0 %collective-permute-start.8 = (bf16[128,2048]{1,0:T(8,128)(2,1)}, bf16[128,2048]{1,0:T(8,128)(2,1)}, u32[]{:S(2)}, u32[]{:S(2)}) collective-permute-start(bf16[128,2048]{1,0:T(8,128)(2,1)} %collective-permute-done.4), channel_id=1, source_target_pairs={{0,2},{1,3},{2,0},{3,1},{4,6},{5,7},{6,4},{7,5},{8,10},{9,11},{10,... | collective-permute-start | bytes 1572872 | tf_op jit(solution)/shard_map/ppermute | solution.py:348
  74.2 24.0 %collective-permute-start.7 = (bf16[256,2048]{1,0:T(8,128)(2,1)}, bf16[256,2048]{1,0:T(8,128)(2,1)}, u32[]{:S(2)}, u32[]{:S(2)}) collective-permute-start(bf16[256,2048]{1,0:T(8,128)(2,1)} %constant_dynamic-update-slice_fusion), channel_id=1, source_target_pairs={{0,1},{1,0},{2,3},{3,2},{4,5},{5,4},{6,7},{7,6},{8,9},{9,8},{10,11... | collective-permute-start | bytes 3145736 | tf_op jit(solution)/shard_map/ppermute | solution.py:348
  81.2 12.0 %collective-permute-start.11 = (bf16[128,2048]{1,0:T(8,128)(2,1)}, bf16[128,2048]{1,0:T(8,128)(2,1)}, u32[]{:S(2)}, u32[]{:S(2)}) collective-permute-start(bf16[128,2048]{1,0:T(8,128)(2,1)} %collective-permute-done.10), channel_id=1, source_target_pairs={{0,2},{1,3},{2,0},{3,1},{4,6},{5,7},{6,4},{7,5},{8,10},{9,11},{10,... | collective-permute-start | bytes 1572872 | tf_op jit(solution)/shard_map/ppermute | solution.py:348
  85.1 12.0 %collective-permute-start.21 = (bf16[128,2048]{1,0:T(8,128)(2,1)}, bf16[128,2048]{1,0:T(8,128)(2,1)S(1)}, u32[]{:S(2)}, u32[]{:S(2)}) collective-permute-start(bf16[128,2048]{1,0:T(8,128)(2,1)} %get-tuple-element.84), channel_id=1, source_target_pairs={{0,4},{4,8},{8,12},{12,0},{1,5},{5,9},{9,13},{13,1},{2,6},{6,10},{... | collective-permute-start | bytes 1572872 | tf_op jit(solution)/shard_map/ppermute | solution.py:345
  87.1 13.4 %collective-permute-start.9 = (bf16[256,2048]{1,0:T(8,128)(2,1)}, bf16[256,2048]{1,0:T(8,128)(2,1)S(1)}, u32[]{:S(2)}, u32[]{:S(2)}) collective-permute-start(bf16[256,2048]{1,0:T(8,128)(2,1)} %constant_dynamic-update-slice_fusion.2), channel_id=1, source_target_pairs={{0,1},{1,0},{2,3},{3,2},{4,5},{5,4},{6,7},{7,6},{8,9},{9,8},{10,11... | collective-permute-start | bytes 3145736 | tf_op jit(solution)/shard_map/ppermute | solution.py:348
  94.4 22.9 %collective-permute-start.12 = (bf16[256,2048]{1,0:T(8,128)(2,1)S(1)}, bf16[256,2048]{1,0:T(8,128)(2,1)S(1)}, u32[]{:S(2)}, u32[]{:S(2)}) collective-permute-start(bf16[256,2048]{1,0:T(8,128)(2,1)S(1)} %constant_dynamic-update-slice_fusion.4), channel_id=1, source_target_pairs={{0,1},{1,0},{2,3},{3,2},{4,5},{5,4},{6,7},{7,6},{8,9},{9,8},{10,11... | collective-permute-start | bytes 3145736 | tf_op jit(solution)/shard_map/ppermute | solution.py:348
  97.1 11.6 %collective-permute-start.22 = (bf16[128,2048]{1,0:T(8,128)(2,1)S(1)}, bf16[128,2048]{1,0:T(8,128)(2,1)S(1)}, u32[]{:S(2)}, u32[]{:S(2)}) collective-permute-start(bf16[128,2048]{1,0:T(8,128)(2,1)S(1)} %collective-permute-done.21), channel_id=1, source_target_pairs={{0,2},{1,3},{2,0},{3,1},{4,6},{5,7},{6,4},{7,5},{8,10},{9,11},{10,... | collective-permute-start | bytes 1572872 | tf_op jit(solution)/shard_map/ppermute | solution.py:348
  100.5 13.0 %collective-permute-start.24 = (bf16[128,2048]{1,0:T(8,128)(2,1)S(1)}, bf16[128,2048]{1,0:T(8,128)(2,1)}, u32[]{:S(2)}, u32[]{:S(2)}) collective-permute-start(bf16[128,2048]{1,0:T(8,128)(2,1)S(1)} %collective-permute-done.21), channel_id=1, source_target_pairs={{0,4},{4,8},{8,12},{12,0},{1,5},{5,9},{9,13},{13,1},{2,6},{6,10},{... | collective-permute-start | bytes 1572872 | tf_op jit(solution)/shard_map/ppermute | solution.py:345
  109.6 54.9 %collective-permute-start.23 = (bf16[256,2048]{1,0:T(8,128)(2,1)}, bf16[256,2048]{1,0:T(8,128)(2,1)}, u32[]{:S(2)}, u32[]{:S(2)}) collective-permute-start(bf16[256,2048]{1,0:T(8,128)(2,1)} %constant_dynamic-update-slice_fusion.9), channel_id=1, source_target_pairs={{0,1},{1,0},{2,3},{3,2},{4,5},{5,4},{6,7},{7,6},{8,9},{9,8},{10,11... | collective-permute-start | bytes 3145736 | tf_op jit(solution)/shard_map/ppermute | solution.py:348
  113.4 35.7 %collective-permute-start.25 = (bf16[128,2048]{1,0:T(8,128)(2,1)}, bf16[128,2048]{1,0:T(8,128)(2,1)}, u32[]{:S(2)}, u32[]{:S(2)}) collective-permute-start(bf16[128,2048]{1,0:T(8,128)(2,1)} %collective-permute-done.24), channel_id=1, source_target_pairs={{0,2},{1,3},{2,0},{3,1},{4,6},{5,7},{6,4},{7,5},{8,10},{9,11},{10,... | collective-permute-start | bytes 1572872 | tf_op jit(solution)/shard_map/ppermute | solution.py:348
  114.6 33.4 %collective-permute-start.27 = (bf16[128,2048]{1,0:T(8,128)(2,1)}, bf16[128,2048]{1,0:T(8,128)(2,1)}, u32[]{:S(2)}, u32[]{:S(2)}) collective-permute-start(bf16[128,2048]{1,0:T(8,128)(2,1)} %collective-permute-done.24), channel_id=1, source_target_pairs={{0,4},{4,8},{8,12},{12,0},{1,5},{5,9},{9,13},{13,1},{2,6},{6,10},{... | collective-permute-start | bytes 1572872 | tf_op jit(solution)/shard_map/ppermute | solution.py:345
  197.1 14.1 %collective-permute-start.31 = (bf16[512,128]{1,0:T(8,128)(2,1)}, bf16[512,128]{1,0:T(8,128)(2,1)S(1)}, u32[]{:S(2)}, u32[]{:S(2)}) collective-permute-start(bf16[512,128]{1,0:T(8,128)(2,1)} %bitcast.373), channel_id=1, source_target_pairs={{0,8},{4,12},{8,0},{12,4},{1,9},{5,13},{9,1},{13,5},{2,10},{6,14},... | collective-permute-start | bytes 393224 | tf_op jit(solution)/shard_map/ppermute | solution.py:345
  198.7 12.5 %collective-permute-start.32 = (bf16[512,128]{1,0:T(8,128)(2,1)}, bf16[512,128]{1,0:T(8,128)(2,1)S(1)}, u32[]{:S(2)}, u32[]{:S(2)}) collective-permute-start(bf16[512,128]{1,0:T(8,128)(2,1)} %bitcast.374), channel_id=1, source_target_pairs={{0,4},{4,8},{8,12},{12,0},{1,5},{5,9},{9,13},{13,1},{2,6},{6,10},{... | collective-permute-start | bytes 393224 | tf_op jit(solution)/shard_map/ppermute | solution.py:345
  201.5 23.0 %collective-permute-start.17 = (bf16[256,2048]{1,0:T(8,128)(2,1)}, bf16[256,2048]{1,0:T(8,128)(2,1)}, u32[]{:S(2)}, u32[]{:S(2)}) collective-permute-start(bf16[256,2048]{1,0:T(8,128)(2,1)} %fusion.70), channel_id=1, source_target_pairs={{0,1},{1,0},{2,3},{3,2},{4,5},{5,4},{6,7},{7,6},{8,9},{9,8},{10,11... | collective-permute-start | bytes 3145736 | tf_op jit(solution)/shard_map/ppermute | solution.py:348
  226.5 14.9 %collective-permute-start.18 = (bf16[128,2048]{1,0:T(8,128)(2,1)S(1)}, bf16[128,2048]{1,0:T(8,128)(2,1)S(1)}, u32[]{:S(2)}, u32[]{:S(2)}) collective-permute-start(bf16[128,2048]{1,0:T(8,128)(2,1)S(1)} %slice.944), channel_id=1, source_target_pairs={{0,2},{1,3},{2,0},{3,1},{4,6},{5,7},{6,4},{7,5},{8,10},{9,11},{10,... | collective-permute-start | bytes 1572872 | tf_op jit(solution)/shard_map/ppermute | solution.py:348
  229.2 23.0 %collective-permute-start.34 = (bf16[128,2048]{1,0:T(8,128)(2,1)S(1)}, bf16[128,2048]{1,0:T(8,128)(2,1)S(1)}, u32[]{:S(2)}, u32[]{:S(2)}) collective-permute-start(bf16[128,2048]{1,0:T(8,128)(2,1)S(1)} %slice.943), channel_id=1, source_target_pairs={{0,2},{1,3},{2,0},{3,1},{4,6},{5,7},{6,4},{7,5},{8,10},{9,11},{10,... | collective-permute-start | bytes 1572872 | tf_op jit(solution)/shard_map/ppermute | solution.py:348
  254.0 13.5 %collective-permute-start.19 = (bf16[128,2048]{1,0:T(8,128)(2,1)S(1)}, bf16[128,2048]{1,0:T(8,128)(2,1)S(1)}, u32[]{:S(2)}, u32[]{:S(2)}) collective-permute-start(bf16[128,2048]{1,0:T(8,128)(2,1)S(1)} %add_convert_fusion.8), channel_id=1, source_target_pairs={{0,2},{1,3},{2,0},{3,1},{4,6},{5,7},{6,4},{7,5},{8,10},{9,11},{10,... | collective-permute-start | bytes 1572872 | tf_op jit(solution)/shard_map/ppermute | solution.py:348
  270.9 14.0 %collective-permute-start.35 = (bf16[128,2048]{1,0:T(8,128)(2,1)S(1)}, bf16[128,2048]{1,0:T(8,128)(2,1)S(1)}, u32[]{:S(2)}, u32[]{:S(2)}) collective-permute-start(bf16[128,2048]{1,0:T(8,128)(2,1)S(1)} %get-tuple-element.150), channel_id=1, source_target_pairs={{0,2},{1,3},{2,0},{3,1},{4,6},{5,7},{6,4},{7,5},{8,10},{9,11},{10,... | collective-permute-start | bytes 1572872 | tf_op jit(solution)/shard_map/ppermute | solution.py:348
  294.7 395.1 %reduce-scatter.4.cloned.1.call-start = ((), (), s32[]{:S(2)}) async-start(), calls=%async_computation.3 | async-start | bytes 5242880 | tf_op jit(solution)/shard_map/reduce_scatter | solution.py:566
  318.0 23.8 %collective-permute-start.38 = (bf16[256,2048]{1,0:T(8,128)(2,1)S(1)}, bf16[256,2048]{1,0:T(8,128)(2,1)S(1)}, u32[]{:S(2)}, u32[]{:S(2)}) collective-permute-start(bf16[256,2048]{1,0:T(8,128)(2,1)S(1)} %fusion.66), channel_id=1, source_target_pairs={{0,1},{1,0},{2,3},{3,2},{4,5},{5,4},{6,7},{7,6},{8,9},{9,8},{10,11... | collective-permute-start | bytes 3145736 | tf_op jit(solution)/shard_map/ppermute | solution.py:348
  342.2 14.9 %collective-permute-start.39 = (bf16[128,2048]{1,0:T(8,128)(2,1)S(1)}, bf16[128,2048]{1,0:T(8,128)(2,1)S(1)}, u32[]{:S(2)}, u32[]{:S(2)}) collective-permute-start(bf16[128,2048]{1,0:T(8,128)(2,1)S(1)} %slice.942), channel_id=1, source_target_pairs={{0,2},{1,3},{2,0},{3,1},{4,6},{5,7},{6,4},{7,5},{8,10},{9,11},{10,... | collective-permute-start | bytes 1572872 | tf_op jit(solution)/shard_map/ppermute | solution.py:348
  343.5 24.4 %collective-permute-start.43 = (bf16[128,2048]{1,0:T(8,128)(2,1)S(1)}, bf16[128,2048]{1,0:T(8,128)(2,1)S(1)}, u32[]{:S(2)}, u32[]{:S(2)}) collective-permute-start(bf16[128,2048]{1,0:T(8,128)(2,1)S(1)} %slice.941), channel_id=1, source_target_pairs={{0,2},{1,3},{2,0},{3,1},{4,6},{5,7},{6,4},{7,5},{8,10},{9,11},{10,... | collective-permute-start | bytes 1572872 | tf_op jit(solution)/shard_map/ppermute | solution.py:348
  370.6 13.5 %collective-permute-start.40 = (bf16[128,2048]{1,0:T(8,128)(2,1)S(1)}, bf16[128,2048]{1,0:T(8,128)(2,1)S(1)}, u32[]{:S(2)}, u32[]{:S(2)}) collective-permute-start(bf16[128,2048]{1,0:T(8,128)(2,1)S(1)} %get-tuple-element.90), channel_id=1, source_target_pairs={{0,2},{1,3},{2,0},{3,1},{4,6},{5,7},{6,4},{7,5},{8,10},{9,11},{10,... | collective-permute-start | bytes 1572872 | tf_op jit(solution)/shard_map/ppermute | solution.py:348
  385.6 93.8 %collective-permute-start.37 = (bf16[2048,1024]{1,0:T(8,128)(2,1)}, bf16[2048,1024]{1,0:T(8,128)(2,1)}, u32[]{:S(2)}, u32[]{:S(2)}) collective-permute-start(bf16[2048,1024]{1,0:T(8,128)(2,1)} %convolution_convert_fusion.1), channel_id=1, source_target_pairs={{0,16},{16,0},{1,17},{17,1},{2,18},{18,2},{3,19},{19,3},{4,20},{20... | collective-permute-start | bytes 12582920 | tf_op jit(solution)/shard_map/ppermute | solution.py:342
  391.5 14.3 %collective-permute-start.44 = (bf16[128,2048]{1,0:T(8,128)(2,1)S(1)}, bf16[128,2048]{1,0:T(8,128)(2,1)S(1)}, u32[]{:S(2)}, u32[]{:S(2)}) collective-permute-start(bf16[128,2048]{1,0:T(8,128)(2,1)S(1)} %get-tuple-element.147), channel_id=1, source_target_pairs={{0,2},{1,3},{2,0},{3,1},{4,6},{5,7},{6,4},{7,5},{8,10},{9,11},{10,... | collective-permute-start | bytes 1572872 | tf_op jit(solution)/shard_map/ppermute | solution.py:348
  406.0 14.1 %collective-permute-start.45 = (bf16[256,2048]{1,0:T(8,128)(2,1)S(1)}, bf16[256,2048]{1,0:T(8,128)(2,1)S(1)}, u32[]{:S(2)}, u32[]{:S(2)}) collective-permute-start(bf16[256,2048]{1,0:T(8,128)(2,1)S(1)} %pad_maximum_fusion.26), channel_id=1, source_target_pairs={{0,1},{1,0},{2,3},{3,2},{4,5},{5,4},{6,7},{7,6},{8,9},{9,8},{10,11... | collective-permute-start | bytes 3145736 | tf_op jit(solution)/shard_map/ppermute | solution.py:348
  412.4 214.6 %collective-permute-start.74 = (bf16[1024,2048]{1,0:T(8,128)(2,1)}, bf16[1024,2048]{1,0:T(8,128)(2,1)}, u32[]{:S(2)}, u32[]{:S(2)}) collective-permute-start(bf16[1024,2048]{1,0:T(8,128)(2,1)} %convolution_convert_fusion), channel_id=1, source_target_pairs={{0,16},{16,0},{1,17},{17,1},{2,18},{18,2},{3,19},{19,3},{4,20},{20... | collective-permute-start | bytes 12582920 | tf_op jit(solution)/shard_map/ppermute | solution.py:342
  425.3 23.4 %collective-permute-start.47 = (bf16[2,512,128]{2,1,0:T(8,128)(2,1)S(1)}, bf16[2,512,128]{2,1,0:T(8,128)(2,1)S(1)}, u32[]{:S(2)}, u32[]{:S(2)}) collective-permute-start(bf16[2,512,128]{2,1,0:T(8,128)(2,1)S(1)} %get-tuple-element.193), channel_id=1, source_target_pairs={{0,8},{4,12},{8,0},{12,4},{1,9},{5,13},{9,1},{13,5},{2,10},{6,14},... | collective-permute-start | bytes 786440 | tf_op jit(solution)/shard_map/ppermute | solution.py:345
  427.8 21.7 %collective-permute-start.46 = (bf16[2,512,128]{2,1,0:T(8,128)(2,1)S(1)}, bf16[2,512,128]{2,1,0:T(8,128)(2,1)S(1)}, u32[]{:S(2)}, u32[]{:S(2)}) collective-permute-start(bf16[2,512,128]{2,1,0:T(8,128)(2,1)S(1)} %get-tuple-element.194), channel_id=1, source_target_pairs={{0,4},{4,8},{8,12},{12,0},{1,5},{5,9},{9,13},{13,1},{2,6},{6,10},{... | collective-permute-start | bytes 786440 | tf_op jit(solution)/shard_map/ppermute | solution.py:345
  485.3 322.1 %reduce-scatter.6.cloned.1.call-start = ((), (), s32[]{:S(2)}) async-start(), calls=%async_computation.4 | async-start | bytes 5242880 | tf_op jit(solution)/shard_map/reduce_scatter | solution.py:566
  519.1 26.0 %collective-permute-start.53 = (bf16[512,384]{1,0:T(8,128)(2,1)S(1)}, bf16[512,384]{1,0:T(8,128)(2,1)S(1)}, u32[]{:S(2)}, u32[]{:S(2)}) collective-permute-start(bf16[512,384]{1,0:T(8,128)(2,1)S(1)} %bitcast.368), channel_id=1, source_target_pairs={{0,12},{4,0},{8,4},{12,8},{1,13},{5,1},{9,5},{13,9},{2,14},{6,2},{... | collective-permute-start | bytes 1179656 | tf_op jit(solution)/shard_map/ppermute | solution.py:345
  519.2 71.3 %collective-permute-start.54 = (bf16[512,384]{1,0:T(8,128)(2,1)S(1)}, bf16[512,384]{1,0:T(8,128)(2,1)S(1)}, u32[]{:S(2)}, u32[]{:S(2)}) collective-permute-start(bf16[512,384]{1,0:T(8,128)(2,1)S(1)} %bitcast.367), channel_id=1, source_target_pairs={{0,8},{4,12},{8,0},{12,4},{1,9},{5,13},{9,1},{13,5},{2,10},{6,14},... | collective-permute-start | bytes 1179656 | tf_op jit(solution)/shard_map/ppermute | solution.py:345
  520.1 70.4 %collective-permute-start.55 = (bf16[512,384]{1,0:T(8,128)(2,1)S(1)}, bf16[512,384]{1,0:T(8,128)(2,1)}, u32[]{:S(2)}, u32[]{:S(2)}) collective-permute-start(bf16[512,384]{1,0:T(8,128)(2,1)S(1)} %bitcast.365), channel_id=1, source_target_pairs={{0,4},{4,8},{8,12},{12,0},{1,5},{5,9},{9,13},{13,1},{2,6},{6,10},{... | collective-permute-start | bytes 1179656 | tf_op jit(solution)/shard_map/ppermute | solution.py:345
  534.4 160.5 %collective-permute-start.49 = (bf16[2,256,2048]{2,1,0:T(8,128)(2,1)}, bf16[2,256,2048]{2,1,0:T(8,128)(2,1)}, u32[]{:S(2)}, u32[]{:S(2)}) collective-permute-start(bf16[2,256,2048]{2,1,0:T(8,128)(2,1)} %fusion.14), channel_id=1, source_target_pairs={{0,1},{1,0},{2,3},{3,2},{4,5},{5,4},{6,7},{7,6},{8,9},{9,8},{10,11... | collective-permute-start | bytes 6291464 | tf_op jit(solution)/shard_map/ppermute | solution.py:348
  614.4 28.3 %collective-permute-start.60 = (bf16[512,384]{1,0:T(8,128)(2,1)}, bf16[512,384]{1,0:T(8,128)(2,1)}, u32[]{:S(2)}, u32[]{:S(2)}) collective-permute-start(bf16[512,384]{1,0:T(8,128)(2,1)} %bitcast.366), channel_id=1, source_target_pairs={{0,12},{4,0},{8,4},{12,8},{1,13},{5,1},{9,5},{13,9},{2,14},{6,2},{... | collective-permute-start | bytes 1179656 | tf_op jit(solution)/shard_map/ppermute | solution.py:345
  614.4 37.2 %collective-permute-start.61 = (bf16[512,384]{1,0:T(8,128)(2,1)}, bf16[512,384]{1,0:T(8,128)(2,1)}, u32[]{:S(2)}, u32[]{:S(2)}) collective-permute-start(bf16[512,384]{1,0:T(8,128)(2,1)} %bitcast.364), channel_id=1, source_target_pairs={{0,8},{4,12},{8,0},{12,4},{1,9},{5,13},{9,1},{13,5},{2,10},{6,14},... | collective-permute-start | bytes 1179656 | tf_op jit(solution)/shard_map/ppermute | solution.py:345
  616.7 34.9 %collective-permute-start.62 = (bf16[512,384]{1,0:T(8,128)(2,1)}, bf16[512,384]{1,0:T(8,128)(2,1)}, u32[]{:S(2)}, u32[]{:S(2)}) collective-permute-start(bf16[512,384]{1,0:T(8,128)(2,1)} %bitcast.363), channel_id=1, source_target_pairs={{0,4},{4,8},{8,12},{12,0},{1,5},{5,9},{9,13},{13,1},{2,6},{6,10},{... | collective-permute-start | bytes 1179656 | tf_op jit(solution)/shard_map/ppermute | solution.py:345
  627.1 44.7 %collective-permute-start.56 = (bf16[256,2048]{1,0:T(8,128)(2,1)S(1)}, bf16[256,2048]{1,0:T(8,128)(2,1)}, u32[]{:S(2)}, u32[]{:S(2)}) collective-permute-start(bf16[256,2048]{1,0:T(8,128)(2,1)S(1)} %fusion.64), channel_id=1, source_target_pairs={{0,1},{1,0},{2,3},{3,2},{4,5},{5,4},{6,7},{7,6},{8,9},{9,8},{10,11... | collective-permute-start | bytes 3145736 | tf_op jit(solution)/shard_map/ppermute | solution.py:348
  642.6 77.8 %collective-permute-start.82 = (bf16[512,1024]{1,0:T(8,128)(2,1)}, bf16[512,1024]{1,0:T(8,128)(2,1)}, u32[]{:S(2)}, u32[]{:S(2)}) collective-permute-start(bf16[512,1024]{1,0:T(8,128)(2,1)} %fusion.75), channel_id=1, source_target_pairs={{0,16},{16,0},{1,17},{17,1},{2,18},{18,2},{3,19},{19,3},{4,20},{20... | collective-permute-start | bytes 3145736 | tf_op jit(solution)/shard_map/ppermute | solution.py:342
  658.7 25.4 %collective-permute-start.73 = (bf16[1024,384]{1,0:T(8,128)(2,1)S(1)}, bf16[1024,384]{1,0:T(8,128)(2,1)S(1)}, u32[]{:S(2)}, u32[]{:S(2)}) collective-permute-start(bf16[1024,384]{1,0:T(8,128)(2,1)S(1)} %add_convert_fusion.6), channel_id=1, source_target_pairs={{0,16},{16,0},{1,17},{17,1},{2,18},{18,2},{3,19},{19,3},{4,20},{20... | collective-permute-start | bytes 2359304 | tf_op jit(solution)/shard_map/ppermute | solution.py:342
  670.7 15.1 %collective-permute-start.63 = (bf16[256,2048]{1,0:T(8,128)(2,1)S(1)}, bf16[256,2048]{1,0:T(8,128)(2,1)S(1)}, u32[]{:S(2)}, u32[]{:S(2)}) collective-permute-start(bf16[256,2048]{1,0:T(8,128)(2,1)S(1)} %fusion.63), channel_id=1, source_target_pairs={{0,1},{1,0},{2,3},{3,2},{4,5},{5,4},{6,7},{7,6},{8,9},{9,8},{10,11... | collective-permute-start | bytes 3145736 | tf_op jit(solution)/shard_map/ppermute | solution.py:348
  673.6 14.3 %collective-permute-start.57 = (bf16[128,2048]{1,0:T(8,128)(2,1)S(1)}, bf16[128,2048]{1,0:T(8,128)(2,1)S(1)}, u32[]{:S(2)}, u32[]{:S(2)}) collective-permute-start(bf16[128,2048]{1,0:T(8,128)(2,1)S(1)} %slice.940), channel_id=1, source_target_pairs={{0,2},{1,3},{2,0},{3,1},{4,6},{5,7},{6,4},{7,5},{8,10},{9,11},{10,... | collective-permute-start | bytes 1572872 | tf_op jit(solution)/shard_map/ppermute | solution.py:348
  685.3 93.9 %collective-permute-start.75 = (bf16[256,384]{1,0:T(8,128)(2,1)}, bf16[256,384]{1,0:T(8,128)(2,1)S(1)}, u32[]{:S(2)}, u32[]{:S(2)}) collective-permute-start(bf16[256,384]{1,0:T(8,128)(2,1)} %get-tuple-element.203), channel_id=1, source_target_pairs={{0,4},{4,8},{8,12},{12,0},{1,5},{5,9},{9,13},{13,1},{2,6},{6,10},{... | collective-permute-start | bytes 589832 | tf_op jit(solution)/shard_map/ppermute | solution.py:345
  686.9 14.6 %collective-permute-start.64 = (bf16[128,2048]{1,0:T(8,128)(2,1)}, bf16[128,2048]{1,0:T(8,128)(2,1)}, u32[]{:S(2)}, u32[]{:S(2)}) collective-permute-start(bf16[128,2048]{1,0:T(8,128)(2,1)} %slice.939), channel_id=1, source_target_pairs={{0,2},{1,3},{2,0},{3,1},{4,6},{5,7},{6,4},{7,5},{8,10},{9,11},{10,... | collective-permute-start | bytes 1572872 | tf_op jit(solution)/shard_map/ppermute | solution.py:348
  692.5 143.3 %reduce-scatter.8.cloned.1.call-start = ((), (), s32[]{:S(2)}) async-start(), calls=%async_computation.5 | async-start | bytes 1310720 | tf_op jit(solution)/shard_map/reduce_scatter | solution.py:566
  719.6 15.0 %collective-permute-start.65 = (bf16[128,2048]{1,0:T(8,128)(2,1)}, bf16[128,2048]{1,0:T(8,128)(2,1)S(1)}, u32[]{:S(2)}, u32[]{:S(2)}) collective-permute-start(bf16[128,2048]{1,0:T(8,128)(2,1)} %get-tuple-element.187), channel_id=1, source_target_pairs={{0,2},{1,3},{2,0},{3,1},{4,6},{5,7},{6,4},{7,5},{8,10},{9,11},{10,... | collective-permute-start | bytes 1572872 | tf_op jit(solution)/shard_map/ppermute | solution.py:348
  728.0 48.5 %collective-permute-start.50 = (bf16[1,256,2048]{2,1,0:T(8,128)(2,1)}, bf16[1,256,2048]{2,1,0:T(8,128)(2,1)}, u32[]{:S(2)}, u32[]{:S(2)}) collective-permute-start(bf16[1,256,2048]{2,1,0:T(8,128)(2,1)} %slice.938), channel_id=1, source_target_pairs={{0,2},{1,3},{2,0},{3,1},{4,6},{5,7},{6,4},{7,5},{8,10},{9,11},{10,... | collective-permute-start | bytes 3145736 | tf_op jit(solution)/shard_map/ppermute | solution.py:348
  729.2 37.3 %collective-permute-start.58 = (bf16[128,2048]{1,0:T(8,128)(2,1)S(1)}, bf16[128,2048]{1,0:T(8,128)(2,1)S(1)}, u32[]{:S(2)}, u32[]{:S(2)}) collective-permute-start(bf16[128,2048]{1,0:T(8,128)(2,1)S(1)} %copy-done.44), channel_id=1, source_target_pairs={{0,2},{1,3},{2,0},{3,1},{4,6},{5,7},{6,4},{7,5},{8,10},{9,11},{10,... | collective-permute-start | bytes 1572872 | tf_op jit(solution)/shard_map/ppermute | solution.py:348
  739.5 28.0 %collective-permute-start.79 = (f32[1,2432]{1,0:T(1,128)S(1)}, f32[1,2432]{1,0:T(1,128)S(1)}, u32[]{:S(2)}, u32[]{:S(2)}) collective-permute-start(f32[1,2432]{1,0:T(1,128)S(1)} %reshape_add_fusion), channel_id=1, source_target_pairs={{0,12},{4,0},{8,4},{12,8},{1,13},{5,1},{9,5},{13,9},{2,14},{6,2},{... | collective-permute-start | bytes 29192 | tf_op jit(solution)/shard_map/ppermute | solution.py:345
  741.0 29.1 %collective-permute-start.80 = (f32[1,2432]{1,0:T(1,128)S(1)}, f32[1,2432]{1,0:T(1,128)S(1)}, u32[]{:S(2)}, u32[]{:S(2)}) collective-permute-start(f32[1,2432]{1,0:T(1,128)S(1)} %reshape_add_fusion), channel_id=1, source_target_pairs={{0,8},{4,12},{8,0},{12,4},{1,9},{5,13},{9,1},{13,5},{2,10},{6,14},... | collective-permute-start | bytes 29192 | tf_op jit(solution)/shard_map/ppermute | solution.py:345
  767.5 13.9 %collective-permute-start.76 = (bf16[256,384]{1,0:T(8,128)(2,1)}, bf16[256,384]{1,0:T(8,128)(2,1)}, u32[]{:S(2)}, u32[]{:S(2)}) collective-permute-start(bf16[256,384]{1,0:T(8,128)(2,1)} %get-tuple-element.202), channel_id=1, source_target_pairs={{0,8},{4,12},{8,0},{12,4},{1,9},{5,13},{9,1},{13,5},{2,10},{6,14},... | collective-permute-start | bytes 589832 | tf_op jit(solution)/shard_map/ppermute | solution.py:345
  779.2 25.6 %collective-permute-start.51 = (bf16[2,128,2048]{2,1,0:T(8,128)(2,1)S(1)}, bf16[2,128,2048]{2,1,0:T(8,128)(2,1)S(1)}, u32[]{:S(2)}, u32[]{:S(2)}) collective-permute-start(bf16[2,128,2048]{2,1,0:T(8,128)(2,1)S(1)} %pad_maximum_fusion.27), channel_id=1, source_target_pairs={{0,2},{1,3},{2,0},{3,1},{4,6},{5,7},{6,4},{7,5},{8,10},{9,11},{10,... | collective-permute-start | bytes 3145736 | tf_op jit(solution)/shard_map/ppermute | solution.py:348
  804.9 18.8 %collective-permute-start.52 = (bf16[2,256,2048]{2,1,0:T(8,128)(2,1)S(1)}, bf16[2,256,2048]{2,1,0:T(8,128)(2,1)}, u32[]{:S(2)}, u32[]{:S(2)}) collective-permute-start(bf16[2,256,2048]{2,1,0:T(8,128)(2,1)S(1)} %pad_maximum_fusion.20), channel_id=1, source_target_pairs={{0,1},{1,0},{2,3},{3,2},{4,5},{5,4},{6,7},{7,6},{8,9},{9,8},{10,11... | collective-permute-start | bytes 6291464 | tf_op jit(solution)/shard_map/ppermute | solution.py:348
  (166 other events, 1450.2 us)
Sparse Core Ops, SparseCore 0:
  30.2 209.1 all-gather.4
  294.8 60.4 all-gather.6
  485.4 98.4 reduce-scatter.3
  692.6 77.3 reduce-scatter.5
  810.3 25.5 reduce-scatter.7

commit v3 on v2

--- a/solution.py
+++ b/solution.py
@@ -353,8 +353,8 @@
     def pieces_of(v):
         return [v] + [shift_f(v, -k) for k in range(1, n_f)]
 
-    def sum_rows(v):
-        for b in range(bits):
+    def sum_rows(v, first=0, last=bits):
+        for b in range(first, last):
             half = v.shape[0] // 2
             come = flip_t(v[half:].astype(BF16), b)
             v = v[:half].astype(F32) + come.astype(F32)
@@ -479,6 +479,10 @@
             for r, half in enumerate(far[i][k - 1]):
                 everyone = lax.dynamic_update_slice(everyone, half, (k * rows + r * (rows // 2), 0))
         qkv = (times(everyone, w_own) + bias_own).astype(BF16)[None]
+        if i:
+            held = list(kept[-1])
+            qkv, held[6] = lax.optimization_barrier((qkv, held[6]))
+            kept[-1] = tuple(held)
         *attended_parts, lse = attention_fwd(table, n_c, qkv)
         attended = jnp.concatenate(from_heads([v[0] for v in attended_parts]), axis=1)
         x0 = inputs0[i].astype(F32)
@@ -584,7 +588,7 @@
             g_down = scatter(total_down, 1)
             ahead = [total_down, *w_far]
         else:
-            ahead = heads_back[0] + [sums]
+            ahead = heads_back[0]
         *back_parts, own = attention_bwd(table, after(qkv, *ahead), attended_parts, grad_parts[i], lse)
         own_back.append(own[0])
         heads_back.append(from_heads([own[0, :rows]] + [v[0] for v in back_parts]))
@@ -593,6 +597,7 @@
                 wide(after(b["active"], own_back[0]), w_down).reshape(n_t, quarter_rows, width) for b in back
             ]
             sums = sum_rows(jnp.concatenate(partial_sums, axis=1)).reshape(trees, quarter_rows, width)
+    *heads_back[-1], sums, g_down = lax.optimization_barrier((*heads_back[-1], sums, g_down))
     results = both_halves(
         jnp.stack([kept[i][6] + sums[i] + bias_down for i in range(trees)]).astype(BF16), 1
     )
@@ -618,7 +623,11 @@
     grads = []
     for i in range(trees):
         x0, grad_middle = kept[i][5], back[i]["grad_middle"]
-        g = sum_rows(wide_back(jnp.concatenate(heads_back[i], axis=1), w_qkv))
+        g = sum_rows(wide_back(jnp.concatenate(heads_back[i], axis=1), w_qkv), 0, bits - 1)
+        if i == trees - 1:
+            g, g_up = lax.optimization_barrier((g, g_up))
+            g_out = scatter(after(joined(part_out, *heads_back[-1]), g_up), 1)
+        g = sum_rows(g, bits - 1)
         mean = jnp.mean(x0, axis=1, keepdims=True)
         spread = jnp.mean((x0 - mean) * (x0 - mean), axis=1, keepdims=True)
         rstd = lax.rsqrt(spread + EPS)
@@ -629,7 +638,11 @@
         moved = rstd * (
             g - jnp.mean(g, axis=1, keepdims=True) - unit * jnp.mean(g * unit, axis=1, keepdims=True)
         )
-        grads.append(both_halves((grad_middle + moved).astype(BF16)))
+        moved = (grad_middle + moved).astype(BF16)
+        if i == trees - 1:
+            moved = after(moved, *[v[0] for v in results], grads[0][0])
+            moved, g_out = lax.optimization_barrier((moved, g_out))
+        grads.append(both_halves(moved))
 
     come = [own_rows(0)] + [shift_c(own_rows(k), k) for k in range(1, n_c)]
 
@@ -637,13 +650,12 @@
         turned = jnp.stack([parts[(n_c - k) % n_c] for k in range(n_c)] * 2)
         return lax.dynamic_slice_in_dim(turned, (n_c - c) % n_c, n_c, axis=0)
 
-    come = list(lax.optimization_barrier((*come, *[half for v in grads for half in v])))[:n_c]
+    come = list(lax.optimization_barrier((*come, moved)))[:n_c]
     come = by_source(come).astype(F32)
     g_query, g_key, g_value = (
         jnp.concatenate([come[h, :, k * HD : (k + 1) * HD] for h in range(heads)], axis=1) for k in range(3)
     )
 
-    g_out = scatter(after(joined(part_out, back[-1]["shift1"]), g_up), 1)
 
     names = ("gain1", "shift1", "out_bias", "gain2", "shift2", "down_bias")
     rolled = jnp.stack([sum(b[name] for b in back) for name in names])

time: 857 us -> 831 us (0.970)
  waiting for transfers between devices: 304 us -> 275 us
  local copies, waits for them, and re-layouts: 103 us -> 89.9 us
  other arithmetic: 85.8 us -> 96.6 us
    ppermute x42, waiting for transfers between devices: 142 us -> 103 us  [flip_t(): return lax.ppermute(v, 'tp', [(i, i ^ 1 << b) for i in range(n_t)])]
    unnamed x310 -> x300, local copies, waits for them, and re-layouts: 43.6 us -> 27.2 us
    ppermute x8, waiting for transfers between devices: 41.8 us -> 31.7 us  [shift_f(): return lax.ppermute(v, 'fsdp', [(i, (i + k) % n_f) for i in range(n_f)])]
    all_gather x1, waiting for transfers between devices: 0.01 us -> 10 us  [per_device(): w_far = [lax.all_gather(after(v, ring[-1]), 'ctx') for v in w_own[1:]]]
    reduce_scatter x3, waiting for transfers between devices: 3.04 us -> 12.7 us  [scatter(): lax.psum_scatter(v, 'ctx', scatter_dimension=axis, tiled=True).astype(F32)]
  transfers between devices with their start and end apart: 88 -> 88, of which waited for: 37 -> 37; matrix products, arithmetic and copies ran while one was open for 37% -> 40% of each run, Pallas kernels for 14% -> 14%
where the time goes in v3:
time: 831 us; the launch traced here: 821 us
  waiting for transfers between devices  275 us (33%)
  matrix products  152 us (18%)
  Pallas kernels  117 us (14%)
  other arithmetic  96.6 us (12%)
  local copies, waits for them, and re-layouts  89.9 us (11%)
  starting transfers between devices  72.4 us (9%)
  between operations  16.7 us (2%)
    ppermute x33, waiting for transfers between devices, shift_c(): return lax.ppermute(v, 'ctx', [(i, (i + k) % n_c) for i in range(n_c)])  117 us
    ppermute x42, waiting for transfers between devices, flip_t(): return lax.ppermute(v, 'tp', [(i, i ^ 1 << b) for i in range(n_t)])  103 us
    dot_general x16, matrix products, nn(): lax.dot_general(a, b, (((1,), (0,)), ((), ())), preferred_element_type=F32)  58.1 us
    dot_general x16, matrix products, nt(): lax.dot_general(a, b, (((1,), (1,)), ((), ())), preferred_element_type=F32)  49.6 us
    pallas_call x2, Pallas kernels, attention_bwd(): pl.pallas_call(partial(bwd_kernel, nsrc), grid_spec=pltpu.PrefetchScalarG...  49 us
    dot_general x10, matrix products, tn(): lax.dot_general(a, b, (((0,), (0,)), ((), ())), preferred_element_type=F32)  44.5 us
    pallas_call x2, Pallas kernels, attention_fwd(): pl.pallas_call(partial(fwd_kernel, nsrc), grid_spec=pltpu.PrefetchScalarG...  40.4 us
    ppermute x33, starting transfers between devices, shift_c(): return lax.ppermute(v, 'ctx', [(i, (i + k) % n_c) for i in range(n_c)])  37.5 us
  transfers between devices with their start and end apart: 88, of which 37 were waited for; matrix products, arithmetic and copies ran while one was open for 40% of the time, Pallas kernels for 14%

profile of v3, /device:TPU:0, one launch (start us, length us, event | category | flops | bytes accessed | tf_op | source)
XLA Modules:
  0.0 820.6 jit_solution(1595089661810269437)
XLA Ops:
  26.6 4.2 pad_maximum_fusion
  38.3 3.4 fusion.33
  41.7 4.1 first_norm.2
  48.9 11.8 %first_norm.3 = (bf16[2,512,2048]{2,1,0:T(8,128)(2,1)}, bf16[2,128,2048]{2,1,0:T(8,128)(2,1)}, bf16[2,512,2048]{2,1,0:T(8,128)(2,1)}) custom-call(s32[4]{0:T(128)} %pad_add_fusion.2.quarter, s32[2]{0:T(128)} %pad_add_fusion.3.chunk, bf16[2,512,2048]{2,1,0:T(8,128)(2,1)} %x_ref.1, bf16[2,512,2048]{2,1,0:T(8,128)(2,1)} %dy_ref.3, ...), custom_call_target="tpu_custom_call" | custom-call | flops 20971520 | bytes 16777216 | tf_op jit(solution)/shard_map/first_norm/pallas_call | solution.py:251
  61.6 4.8 slice_bitcast_fusion
  72.5 9.2 %collective-permute-done.4 = bf16[128,2048]{1,0:T(8,128)(2,1)} collective-permute-done((bf16[128,2048]{1,0:T(8,128)(2,1)S(1)}, bf16[128,2048]{1,0:T(8,128)(2,1)}, u32[]{:S(2)}, u32[]{:S(2)}) %collective-permute-start.4) | collective-permute-done | bytes 524320 | tf_op jit(solution)/shard_map/ppermute | solution.py:345
  90.1 5.1 collective-permute-done.6
  102.8 4.4 collective-permute-done.20
  108.4 3.6 collective-permute-done.7
  114.2 8.6 %collective-permute-done.8 = bf16[128,2048]{1,0:T(8,128)(2,1)S(1)} collective-permute-done((bf16[128,2048]{1,0:T(8,128)(2,1)S(1)}, bf16[128,2048]{1,0:T(8,128)(2,1)S(1)}, u32[]{:S(2)}, u32[]{:S(2)}) %collective-permute-start.8) | collective-permute-done | bytes 524320 | tf_op jit(solution)/shard_map/ppermute | solution.py:348
  128.3 4.2 fusion.17
  132.5 3.6 fusion.46.refs_0_
  136.1 20.2 %tree_attention.2 = (bf16[1,512,128]{2,1,0:T(8,128)(2,1)}, bf16[1,512,128]{2,1,0:T(8,128)(2,1)}, bf16[1,512,128]{2,1,0:T(8,128)(2,1)}, bf16[1,512,128]{2,1,0:T(8,128)(2,1)}, f32[1,8,256]{2,1,0:T(8,128)}) custom-call(s32[1,32]{1,0:T(1,128)} %get-tuple-element.278.place, s32[1,7]{1,0:T(1,128)} %get-tuple-element.297.starts, s32[1,7]{1,0:T(1,128)} %get-tuple-element.274.path, ...), custom_call_target="tpu_custom_call" | custom-call | flops 10737418240 | bytes 2097152 | tf_op jit(solution)/shard_map/tree_attention/pallas_call | solution.py:101
  156.3 3.3 collective-permute-start.22
  163.7 8.1 collective-permute-done.23
  176.8 8.0 collective-permute-done.14
  187.7 4.2 fusion.25
  192.0 3.5 fusion.43.refs_0_
  195.5 5.8 collective-permute-done.27
  201.6 20.2 %tree_attention.3 = (bf16[1,512,128]{2,1,0:T(8,128)(2,1)}, bf16[1,512,128]{2,1,0:T(8,128)(2,1)}, bf16[1,512,128]{2,1,0:T(8,128)(2,1)}, bf16[1,512,128]{2,1,0:T(8,128)(2,1)}, f32[1,8,256]{2,1,0:T(8,128)}) custom-call(s32[1,32]{1,0:T(1,128)} %get-tuple-element.279.place, s32[1,7]{1,0:T(1,128)} %get-tuple-element.296.starts, s32[1,7]{1,0:T(1,128)} %get-tuple-element.275.path, ...), custom_call_target="tpu_custom_call" | custom-call | flops 10737418240 | bytes 2097152 | tf_op jit(solution)/shard_map/tree_attention/pallas_call | solution.py:101
  227.6 7.9 collective-permute-done.31
  246.1 10.8 %collective-permute-done.34 = bf16[128,2048]{1,0:T(8,128)(2,1)S(1)} collective-permute-done((bf16[128,2048]{1,0:T(8,128)(2,1)S(1)}, bf16[128,2048]{1,0:T(8,128)(2,1)S(1)}, u32[]{:S(2)}, u32[]{:S(2)}) %collective-permute-start.34) | collective-permute-done | bytes 524320 | tf_op jit(solution)/shard_map/ppermute | solution.py:348
  259.7 4.3 fusion.130
  264.1 8.2 %collective-permute-done.35 = bf16[128,2048]{1,0:T(8,128)(2,1)S(1)} collective-permute-done((bf16[128,2048]{1,0:T(8,128)(2,1)S(1)}, bf16[128,2048]{1,0:T(8,128)(2,1)S(1)}, u32[]{:S(2)}, u32[]{:S(2)}) %collective-permute-start.35) | collective-permute-done | bytes 524320 | tf_op jit(solution)/shard_map/ppermute | solution.py:348
  275.3 4.4 fusion.124
  288.3 3.8 fusion.135
  292.1 5.7 multiply_convert_fusion.1
  297.8 5.5 convert_reduce_fusion.1
  313.2 4.2 multiply_convert_fusion
  317.4 5.9 convert_reduce_fusion
  331.1 10.0 %all-gather.7.cloned.1.call-done = bf16[4096,384]{1,0:T(8,128)(2,1)} async-done(((bf16[1024,384]{1,0:T(8,128)(2,1)}), bf16[4096,384]{1,0:T(8,128)(2,1)}) %all-gather.7.cloned.1.call-update) | async-done | bytes 3145744 | tf_op jit(solution)/shard_map/all_gather | solution.py:472
  341.1 3.5 dynamic-slice_bitcast_fusion.10
  353.2 6.2 convolution_convert_fusion.1
  363.8 9.9 %collective-permute-done.43 = bf16[128,2048]{1,0:T(8,128)(2,1)S(1)} collective-permute-done((bf16[128,2048]{1,0:T(8,128)(2,1)S(1)}, bf16[128,2048]{1,0:T(8,128)(2,1)S(1)}, u32[]{:S(2)}, u32[]{:S(2)}) %collective-permute-start.43) | collective-permute-done | bytes 524320 | tf_op jit(solution)/shard_map/ppermute | solution.py:348
  379.2 7.9 convolution_convert_fusion
  387.1 4.8 collective-permute-done.44
  392.1 9.0 %collective-permute-done.40 = bf16[128,2048]{1,0:T(8,128)(2,1)S(1)} collective-permute-done((bf16[128,2048]{1,0:T(8,128)(2,1)S(1)}, bf16[128,2048]{1,0:T(8,128)(2,1)S(1)}, u32[]{:S(2)}, u32[]{:S(2)}) %collective-permute-start.40) | collective-permute-done | bytes 524320 | tf_op jit(solution)/shard_map/ppermute | solution.py:348
  401.3 4.7 fusion.40
  423.4 4.4 collective-permute-done.48
  428.5 14.4 %collective-permute-done.47 = bf16[2,512,128]{2,1,0:T(8,128)(2,1)S(1)} collective-permute-done((bf16[2,512,128]{2,1,0:T(8,128)(2,1)S(1)}, bf16[2,512,128]{2,1,0:T(8,128)(2,1)S(1)}, u32[]{:S(2)}, u32[]{:S(2)}) %collective-permute-start.47) | collective-permute-done | bytes 262176 | tf_op jit(solution)/shard_map/ppermute | solution.py:345
  444.3 8.9 %collective-permute-done.37 = bf16[2048,1024]{1,0:T(8,128)(2,1)} collective-permute-done((bf16[2048,1024]{1,0:T(8,128)(2,1)}, bf16[2048,1024]{1,0:T(8,128)(2,1)}, u32[]{:S(2)}, u32[]{:S(2)}) %collective-permute-start.37) | collective-permute-done | bytes 4194336 | tf_op jit(solution)/shard_map/ppermute | solution.py:342
  453.2 5.9 add_convert_fusion.1
  459.1 24.6 %tree_attention_back.2 = (bf16[1,512,384]{2,1,0:T(8,128)(2,1)}, bf16[1,512,384]{2,1,0:T(8,128)(2,1)}, bf16[1,512,384]{2,1,0:T(8,128)(2,1)}, bf16[1,2048,384]{2,1,0:T(8,128)(2,1)}) custom-call(s32[1,32]{1,0:T(1,128)} %get-tuple-element.278.place, s32[1,7]{1,0:T(1,128)} %get-tuple-element.297.starts, s32[1,7]{1,0:T(1,128)} %get-tuple-element.274.path, ...), custom_call_target="tpu_custom_call" | custom-call | flops 13421772800 | bytes 5242880 | tf_op jit(solution)/shard_map/tree_attention_back/pallas_call | solution.py:180
  483.8 5.4 fusion.207
  492.3 4.5 fusion.41
  498.4 6.1 fusion.42
  513.9 49.6 %collective-permute-done.50 = bf16[512,384]{1,0:T(8,128)(2,1)} collective-permute-done((bf16[512,384]{1,0:T(8,128)(2,1)S(1)}, bf16[512,384]{1,0:T(8,128)(2,1)}, u32[]{:S(2)}, u32[]{:S(2)}) %collective-permute-start.50) | collective-permute-done | bytes 393248 | tf_op jit(solution)/shard_map/ppermute | solution.py:345
  563.5 24.4 %tree_attention_back.3 = (bf16[1,512,384]{2,1,0:T(8,128)(2,1)}, bf16[1,512,384]{2,1,0:T(8,128)(2,1)}, bf16[1,512,384]{2,1,0:T(8,128)(2,1)}, bf16[1,2048,384]{2,1,0:T(8,128)(2,1)}) custom-call(s32[1,32]{1,0:T(1,128)} %get-tuple-element.279.place, s32[1,7]{1,0:T(1,128)} %get-tuple-element.296.starts, s32[1,7]{1,0:T(1,128)} %get-tuple-element.275.path, ...), custom_call_target="tpu_custom_call" | custom-call | flops 13421772800 | bytes 5242880 | tf_op jit(solution)/shard_map/tree_attention_back/pallas_call | solution.py:180
  592.2 4.2 fusion.149
  596.4 3.8 fusion.143
  611.0 8.5 %add_convert_fusion = bf16[1024,2048]{1,0:T(8,128)(2,1)} fusion(bf16[1024,2048]{1,0:T(8,128)(2,1)} %collective-permute-done.64, bf16[512,2048]{1,0:T(8,128)(2,1)S(1)} %copy-done.128, bf16[512,2048]{1,0:T(8,128)(2,1)S(1)} %copy-done.125, bf16[1024,2048]{1,0:T(8,128)(2,1)} %constant_dynamic-update-slice_fusion.22), kind=kOutput, calls=%fused_computation.3 | convolution fusion | flops 4309647360 | bytes 14680064 | tf_op jit(solution)/shard_map/dot_general | solution.py:31
  625.3 10.6 %collective-permute-done.56 = bf16[1,256,2048]{2,1,0:T(8,128)(2,1)} collective-permute-done((bf16[1,256,2048]{2,1,0:T(8,128)(2,1)}, bf16[1,256,2048]{2,1,0:T(8,128)(2,1)}, u32[]{:S(2)}, u32[]{:S(2)}) %collective-permute-start.56) | collective-permute-done | bytes 1048608 | tf_op jit(solution)/shard_map/ppermute | solution.py:348
  641.6 3.4 fusion.75
  651.4 13.0 %collective-permute-done.66 = bf16[512,1024]{1,0:T(8,128)(2,1)S(1)} collective-permute-done((bf16[512,1024]{1,0:T(8,128)(2,1)S(1)}, bf16[512,1024]{1,0:T(8,128)(2,1)S(1)}, u32[]{:S(2)}, u32[]{:S(2)}) %collective-permute-start.66) | collective-permute-done | bytes 1048608 | tf_op jit(solution)/shard_map/ppermute | solution.py:342
  679.9 3.3 add_convert_fusion.6
  687.1 3.5 fusion.19
  694.1 7.6 collective-permute-done.75
  709.4 12.7 %reduce-scatter.6.cloned.1.call-done = bf16[256,2048]{1,0:T(8,128)(2,1)} async-done(((bf16[1024,2048]{1,0:T(8,128)(2,1)}), bf16[256,2048]{1,0:T(8,128)(2,1)}) %reduce-scatter.6.cloned.1.call-update) | async-done | bytes 1048592 | tf_op jit(solution)/shard_map/reduce_scatter | solution.py:570
  730.3 9.1 %collective-permute-done.65 = bf16[128,2048]{1,0:T(8,128)(2,1)} collective-permute-done((bf16[128,2048]{1,0:T(8,128)(2,1)}, bf16[128,2048]{1,0:T(8,128)(2,1)}, u32[]{:S(2)}, u32[]{:S(2)}) %collective-permute-start.65) | collective-permute-done | bytes 524320 | tf_op jit(solution)/shard_map/ppermute | solution.py:348
  753.2 4.1 fusion.104
  767.9 6.0 replace.2
  780.3 3.9 collective-permute-done.77
  785.8 8.1 collective-permute-done.67
  808.0 5.9 replace.3
  (660 shorter events, 291.1 us)
Async XLA Ops:
  7.2 278.1 %all-gather.5.cloned.1.call-start = ((), (), s32[]{:S(2)}) async-start(), calls=%async_computation.6 | async-start | bytes 25165824 | tf_op jit(solution)/shard_map/all_gather | solution.py:376
  9.3 32.4 %collective-permute-start = (s32[2,15]{1,0:T(2,128)S(1)}, s32[2,15]{1,0:T(2,128)}, u32[]{:S(2)}, u32[]{:S(2)}) collective-permute-start(s32[2,15]{1,0:T(2,128)S(1)} %pad_add_fusion), channel_id=1, source_target_pairs={{0,4},{4,8},{8,12},{12,0},{1,5},{5,9},{9,13},{13,1},{2,6},{6,10},{... | collective-permute-start | bytes 368 | tf_op jit(solution)/shard_map/ppermute | solution.py:345
  12.3 29.4 %collective-permute-start.1 = (s32[2,15]{1,0:T(2,128)S(1)}, s32[2,15]{1,0:T(2,128)}, u32[]{:S(2)}, u32[]{:S(2)}) collective-permute-start(s32[2,15]{1,0:T(2,128)S(1)} %pad_add_fusion), channel_id=1, source_target_pairs={{0,8},{4,12},{8,0},{12,4},{1,9},{5,13},{9,1},{13,5},{2,10},{6,14},... | collective-permute-start | bytes 368 | tf_op jit(solution)/shard_map/ppermute | solution.py:345
  14.9 26.8 %collective-permute-start.2 = (s32[2,15]{1,0:T(2,128)S(1)}, s32[2,15]{1,0:T(2,128)}, u32[]{:S(2)}, u32[]{:S(2)}) collective-permute-start(s32[2,15]{1,0:T(2,128)S(1)} %pad_add_fusion), channel_id=1, source_target_pairs={{0,12},{4,0},{8,4},{12,8},{1,13},{5,1},{9,5},{13,9},{2,14},{6,2},{... | collective-permute-start | bytes 368 | tf_op jit(solution)/shard_map/ppermute | solution.py:345
  19.4 53.1 %collective-permute-start.5 = (bf16[1024,384]{1,0:T(8,128)(2,1)}, bf16[1024,384]{1,0:T(8,128)(2,1)}, u32[]{:S(2)}, u32[]{:S(2)}) collective-permute-start(bf16[1024,384]{1,0:T(8,128)(2,1)} %pad_maximum_fusion.28), channel_id=1, source_target_pairs={{0,16},{16,0},{1,17},{17,1},{2,18},{18,2},{3,19},{19,3},{4,20},{20... | collective-permute-start | bytes 2359304 | tf_op jit(solution)/shard_map/ppermute | solution.py:342
  23.2 151.3 %collective-permute-start.25 = (bf16[512,1024]{1,0:T(8,128)(2,1)}, bf16[512,1024]{1,0:T(8,128)(2,1)}, u32[]{:S(2)}, u32[]{:S(2)}) collective-permute-start(bf16[512,1024]{1,0:T(8,128)(2,1)} %fusion.119), channel_id=1, source_target_pairs={{0,16},{16,0},{1,17},{17,1},{2,18},{18,2},{3,19},{19,3},{4,20},{20... | collective-permute-start | bytes 3145736 | tf_op jit(solution)/shard_map/ppermute | solution.py:342
  30.8 310.3 %all-gather.7.cloned.1.call-start = ((), (), s32[]{:S(2)}) async-start(), calls=%async_computation.7 | async-start | bytes 3932160 | tf_op jit(solution)/shard_map/all_gather | solution.py:472
  48.0 19.5 %collective-permute-start.3 = (bf16[128,2048]{1,0:T(8,128)(2,1)S(1)}, bf16[128,2048]{1,0:T(8,128)(2,1)S(1)}, u32[]{:S(2)}, u32[]{:S(2)}) collective-permute-start(bf16[128,2048]{1,0:T(8,128)(2,1)S(1)} %get-tuple-element.226), channel_id=1, source_target_pairs={{0,4},{4,8},{8,12},{12,0},{1,5},{5,9},{9,13},{13,1},{2,6},{6,10},{... | collective-permute-start | bytes 1572872 | tf_op jit(solution)/shard_map/ppermute | solution.py:345
  67.5 14.2 %collective-permute-start.4 = (bf16[128,2048]{1,0:T(8,128)(2,1)S(1)}, bf16[128,2048]{1,0:T(8,128)(2,1)}, u32[]{:S(2)}, u32[]{:S(2)}) collective-permute-start(bf16[128,2048]{1,0:T(8,128)(2,1)S(1)} %collective-permute-done.3), channel_id=1, source_target_pairs={{0,4},{4,8},{8,12},{12,0},{1,5},{5,9},{9,13},{13,1},{2,6},{6,10},{... | collective-permute-start | bytes 1572872 | tf_op jit(solution)/shard_map/ppermute | solution.py:345
  70.0 15.8 %collective-permute-start.16 = (bf16[128,2048]{1,0:T(8,128)(2,1)S(1)}, bf16[128,2048]{1,0:T(8,128)(2,1)}, u32[]{:S(2)}, u32[]{:S(2)}) collective-permute-start(bf16[128,2048]{1,0:T(8,128)(2,1)S(1)} %collective-permute-done.3), channel_id=1, source_target_pairs={{0,2},{1,3},{2,0},{3,1},{4,6},{5,7},{6,4},{7,5},{8,10},{9,11},{10,... | collective-permute-start | bytes 1572872 | tf_op jit(solution)/shard_map/ppermute | solution.py:348
  81.7 13.5 %collective-permute-start.6 = (bf16[128,2048]{1,0:T(8,128)(2,1)}, bf16[128,2048]{1,0:T(8,128)(2,1)}, u32[]{:S(2)}, u32[]{:S(2)}) collective-permute-start(bf16[128,2048]{1,0:T(8,128)(2,1)} %collective-permute-done.4), channel_id=1, source_target_pairs={{0,4},{4,8},{8,12},{12,0},{1,5},{5,9},{9,13},{13,1},{2,6},{6,10},{... | collective-permute-start | bytes 1572872 | tf_op jit(solution)/shard_map/ppermute | solution.py:345
  84.2 15.6 %collective-permute-start.18 = (bf16[128,2048]{1,0:T(8,128)(2,1)}, bf16[128,2048]{1,0:T(8,128)(2,1)}, u32[]{:S(2)}, u32[]{:S(2)}) collective-permute-start(bf16[128,2048]{1,0:T(8,128)(2,1)} %collective-permute-done.4), channel_id=1, source_target_pairs={{0,2},{1,3},{2,0},{3,1},{4,6},{5,7},{6,4},{7,5},{8,10},{9,11},{10,... | collective-permute-start | bytes 1572872 | tf_op jit(solution)/shard_map/ppermute | solution.py:348
  87.7 24.4 %collective-permute-start.17 = (bf16[256,2048]{1,0:T(8,128)(2,1)}, bf16[256,2048]{1,0:T(8,128)(2,1)}, u32[]{:S(2)}, u32[]{:S(2)}) collective-permute-start(bf16[256,2048]{1,0:T(8,128)(2,1)} %constant_dynamic-update-slice_fusion.6), channel_id=1, source_target_pairs={{0,1},{1,0},{2,3},{3,2},{4,5},{5,4},{6,7},{7,6},{8,9},{9,8},{10,11... | collective-permute-start | bytes 3145736 | tf_op jit(solution)/shard_map/ppermute | solution.py:348
  99.7 12.3 %collective-permute-start.7 = (bf16[128,2048]{1,0:T(8,128)(2,1)}, bf16[128,2048]{1,0:T(8,128)(2,1)S(1)}, u32[]{:S(2)}, u32[]{:S(2)}) collective-permute-start(bf16[128,2048]{1,0:T(8,128)(2,1)} %get-tuple-element.87), channel_id=1, source_target_pairs={{0,4},{4,8},{8,12},{12,0},{1,5},{5,9},{9,13},{13,1},{2,6},{6,10},{... | collective-permute-start | bytes 1572872 | tf_op jit(solution)/shard_map/ppermute | solution.py:345
  101.7 12.4 %collective-permute-start.19 = (bf16[256,2048]{1,0:T(8,128)(2,1)}, bf16[256,2048]{1,0:T(8,128)(2,1)S(1)}, u32[]{:S(2)}, u32[]{:S(2)}) collective-permute-start(bf16[256,2048]{1,0:T(8,128)(2,1)} %constant_dynamic-update-slice_fusion.8), channel_id=1, source_target_pairs={{0,1},{1,0},{2,3},{3,2},{4,5},{5,4},{6,7},{7,6},{8,9},{9,8},{10,11... | collective-permute-start | bytes 3145736 | tf_op jit(solution)/shard_map/ppermute | solution.py:348
  108.3 19.8 %collective-permute-start.21 = (bf16[256,2048]{1,0:T(8,128)(2,1)S(1)}, bf16[256,2048]{1,0:T(8,128)(2,1)S(1)}, u32[]{:S(2)}, u32[]{:S(2)}) collective-permute-start(bf16[256,2048]{1,0:T(8,128)(2,1)S(1)} %constant_dynamic-update-slice_fusion.10), channel_id=1, source_target_pairs={{0,1},{1,0},{2,3},{3,2},{4,5},{5,4},{6,7},{7,6},{8,9},{9,8},{10,11... | collective-permute-start | bytes 3145736 | tf_op jit(solution)/shard_map/ppermute | solution.py:348
  112.0 12.6 %collective-permute-start.10 = (bf16[128,2048]{1,0:T(8,128)(2,1)S(1)}, bf16[128,2048]{1,0:T(8,128)(2,1)}, u32[]{:S(2)}, u32[]{:S(2)}) collective-permute-start(bf16[128,2048]{1,0:T(8,128)(2,1)S(1)} %collective-permute-done.7), channel_id=1, source_target_pairs={{0,4},{4,8},{8,12},{12,0},{1,5},{5,9},{9,13},{13,1},{2,6},{6,10},{... | collective-permute-start | bytes 1572872 | tf_op jit(solution)/shard_map/ppermute | solution.py:345
  122.8 62.1 %collective-permute-start.9 = (bf16[256,2048]{1,0:T(8,128)(2,1)S(1)}, bf16[256,2048]{1,0:T(8,128)(2,1)}, u32[]{:S(2)}, u32[]{:S(2)}) collective-permute-start(bf16[256,2048]{1,0:T(8,128)(2,1)S(1)} %constant_dynamic-update-slice_fusion), channel_id=1, source_target_pairs={{0,1},{1,0},{2,3},{3,2},{4,5},{5,4},{6,7},{7,6},{8,9},{9,8},{10,11... | collective-permute-start | bytes 3145736 | tf_op jit(solution)/shard_map/ppermute | solution.py:348
  124.6 35.0 %collective-permute-start.13 = (bf16[128,2048]{1,0:T(8,128)(2,1)}, bf16[128,2048]{1,0:T(8,128)(2,1)}, u32[]{:S(2)}, u32[]{:S(2)}) collective-permute-start(bf16[128,2048]{1,0:T(8,128)(2,1)} %collective-permute-done.10), channel_id=1, source_target_pairs={{0,4},{4,8},{8,12},{12,0},{1,5},{5,9},{9,13},{13,1},{2,6},{6,10},{... | collective-permute-start | bytes 1572872 | tf_op jit(solution)/shard_map/ppermute | solution.py:345
  125.3 35.8 %collective-permute-start.11 = (bf16[128,2048]{1,0:T(8,128)(2,1)}, bf16[128,2048]{1,0:T(8,128)(2,1)}, u32[]{:S(2)}, u32[]{:S(2)}) collective-permute-start(bf16[128,2048]{1,0:T(8,128)(2,1)} %collective-permute-done.10), channel_id=1, source_target_pairs={{0,2},{1,3},{2,0},{3,1},{4,6},{5,7},{6,4},{7,5},{8,10},{9,11},{10,... | collective-permute-start | bytes 1572872 | tf_op jit(solution)/shard_map/ppermute | solution.py:348
  163.7 22.7 %collective-permute-start.12 = (bf16[256,2048]{1,0:T(8,128)(2,1)S(1)}, bf16[256,2048]{1,0:T(8,128)(2,1)S(1)}, u32[]{:S(2)}, u32[]{:S(2)}) collective-permute-start(bf16[256,2048]{1,0:T(8,128)(2,1)S(1)} %constant_dynamic-update-slice_fusion.2), channel_id=1, source_target_pairs={{0,1},{1,0},{2,3},{3,2},{4,5},{5,4},{6,7},{7,6},{8,9},{9,8},{10,11... | collective-permute-start | bytes 3145736 | tf_op jit(solution)/shard_map/ppermute | solution.py:348
  171.8 13.0 %collective-permute-start.14 = (bf16[128,2048]{1,0:T(8,128)(2,1)}, bf16[128,2048]{1,0:T(8,128)(2,1)S(1)}, u32[]{:S(2)}, u32[]{:S(2)}) collective-permute-start(bf16[128,2048]{1,0:T(8,128)(2,1)} %collective-permute-done.13), channel_id=1, source_target_pairs={{0,2},{1,3},{2,0},{3,1},{4,6},{5,7},{6,4},{7,5},{8,10},{9,11},{10,... | collective-permute-start | bytes 1572872 | tf_op jit(solution)/shard_map/ppermute | solution.py:348
  186.9 14.4 %collective-permute-start.27 = (bf16[128,2048]{1,0:T(8,128)(2,1)S(1)}, bf16[128,2048]{1,0:T(8,128)(2,1)S(1)}, u32[]{:S(2)}, u32[]{:S(2)}) collective-permute-start(bf16[128,2048]{1,0:T(8,128)(2,1)S(1)} %slice.927), channel_id=1, source_target_pairs={{0,2},{1,3},{2,0},{3,1},{4,6},{5,7},{6,4},{7,5},{8,10},{9,11},{10,... | collective-permute-start | bytes 1572872 | tf_op jit(solution)/shard_map/ppermute | solution.py:348
  222.0 13.4 %collective-permute-start.31 = (bf16[512,128]{1,0:T(8,128)(2,1)}, bf16[512,128]{1,0:T(8,128)(2,1)S(1)}, u32[]{:S(2)}, u32[]{:S(2)}) collective-permute-start(bf16[512,128]{1,0:T(8,128)(2,1)} %bitcast.372), channel_id=1, source_target_pairs={{0,8},{4,12},{8,0},{12,4},{1,9},{5,13},{9,1},{13,5},{2,10},{6,14},... | collective-permute-start | bytes 393224 | tf_op jit(solution)/shard_map/ppermute | solution.py:345
  224.9 15.2 %collective-permute-start.28 = (bf16[128,2048]{1,0:T(8,128)(2,1)S(1)}, bf16[128,2048]{1,0:T(8,128)(2,1)S(1)}, u32[]{:S(2)}, u32[]{:S(2)}) collective-permute-start(bf16[128,2048]{1,0:T(8,128)(2,1)S(1)} %add_convert_fusion.8), channel_id=1, source_target_pairs={{0,2},{1,3},{2,0},{3,1},{4,6},{5,7},{6,4},{7,5},{8,10},{9,11},{10,... | collective-permute-start | bytes 1572872 | tf_op jit(solution)/shard_map/ppermute | solution.py:348
  242.8 14.0 %collective-permute-start.34 = (bf16[128,2048]{1,0:T(8,128)(2,1)S(1)}, bf16[128,2048]{1,0:T(8,128)(2,1)S(1)}, u32[]{:S(2)}, u32[]{:S(2)}) collective-permute-start(bf16[128,2048]{1,0:T(8,128)(2,1)S(1)} %slice.926), channel_id=1, source_target_pairs={{0,2},{1,3},{2,0},{3,1},{4,6},{5,7},{6,4},{7,5},{8,10},{9,11},{10,... | collective-permute-start | bytes 1572872 | tf_op jit(solution)/shard_map/ppermute | solution.py:348
  259.2 13.1 %collective-permute-start.35 = (bf16[128,2048]{1,0:T(8,128)(2,1)S(1)}, bf16[128,2048]{1,0:T(8,128)(2,1)S(1)}, u32[]{:S(2)}, u32[]{:S(2)}) collective-permute-start(bf16[128,2048]{1,0:T(8,128)(2,1)S(1)} %get-tuple-element.176), channel_id=1, source_target_pairs={{0,2},{1,3},{2,0},{3,1},{4,6},{5,7},{6,4},{7,5},{8,10},{9,11},{10,... | collective-permute-start | bytes 1572872 | tf_op jit(solution)/shard_map/ppermute | solution.py:348
  279.8 358.9 %reduce-scatter.4.cloned.1.call-start = ((), (), s32[]{:S(2)}) async-start(), calls=%async_computation.3 | async-start | bytes 5242880 | tf_op jit(solution)/shard_map/reduce_scatter | solution.py:570
  309.2 38.0 %collective-permute-start.38 = (bf16[256,2048]{1,0:T(8,128)(2,1)}, bf16[256,2048]{1,0:T(8,128)(2,1)}, u32[]{:S(2)}, u32[]{:S(2)}) collective-permute-start(bf16[256,2048]{1,0:T(8,128)(2,1)} %fusion.66), channel_id=1, source_target_pairs={{0,1},{1,0},{2,3},{3,2},{4,5},{5,4},{6,7},{7,6},{8,9},{9,8},{10,11... | collective-permute-start | bytes 3145736 | tf_op jit(solution)/shard_map/ppermute | solution.py:348
  329.7 20.8 %collective-permute-start.42 = (bf16[256,2048]{1,0:T(8,128)(2,1)}, bf16[256,2048]{1,0:T(8,128)(2,1)}, u32[]{:S(2)}, u32[]{:S(2)}) collective-permute-start(bf16[256,2048]{1,0:T(8,128)(2,1)} %fusion.65), channel_id=1, source_target_pairs={{0,1},{1,0},{2,3},{3,2},{4,5},{5,4},{6,7},{7,6},{8,9},{9,8},{10,11... | collective-permute-start | bytes 3145736 | tf_op jit(solution)/shard_map/ppermute | solution.py:348
  349.0 14.9 %collective-permute-start.39 = (bf16[128,2048]{1,0:T(8,128)(2,1)S(1)}, bf16[128,2048]{1,0:T(8,128)(2,1)S(1)}, u32[]{:S(2)}, u32[]{:S(2)}) collective-permute-start(bf16[128,2048]{1,0:T(8,128)(2,1)S(1)} %slice.925), channel_id=1, source_target_pairs={{0,2},{1,3},{2,0},{3,1},{4,6},{5,7},{6,4},{7,5},{8,10},{9,11},{10,... | collective-permute-start | bytes 1572872 | tf_op jit(solution)/shard_map/ppermute | solution.py:348
  352.8 21.0 %collective-permute-start.43 = (bf16[128,2048]{1,0:T(8,128)(2,1)S(1)}, bf16[128,2048]{1,0:T(8,128)(2,1)S(1)}, u32[]{:S(2)}, u32[]{:S(2)}) collective-permute-start(bf16[128,2048]{1,0:T(8,128)(2,1)S(1)} %slice.924), channel_id=1, source_target_pairs={{0,2},{1,3},{2,0},{3,1},{4,6},{5,7},{6,4},{7,5},{8,10},{9,11},{10,... | collective-permute-start | bytes 1572872 | tf_op jit(solution)/shard_map/ppermute | solution.py:348
  359.4 93.8 %collective-permute-start.37 = (bf16[2048,1024]{1,0:T(8,128)(2,1)}, bf16[2048,1024]{1,0:T(8,128)(2,1)}, u32[]{:S(2)}, u32[]{:S(2)}) collective-permute-start(bf16[2048,1024]{1,0:T(8,128)(2,1)} %convolution_convert_fusion.1), channel_id=1, source_target_pairs={{0,16},{16,0},{1,17},{17,1},{2,18},{18,2},{3,19},{19,3},{4,20},{20... | collective-permute-start | bytes 12582920 | tf_op jit(solution)/shard_map/ppermute | solution.py:342
  377.2 14.8 %collective-permute-start.44 = (bf16[128,2048]{1,0:T(8,128)(2,1)S(1)}, bf16[128,2048]{1,0:T(8,128)(2,1)S(1)}, u32[]{:S(2)}, u32[]{:S(2)}) collective-permute-start(bf16[128,2048]{1,0:T(8,128)(2,1)S(1)} %get-tuple-element.173), channel_id=1, source_target_pairs={{0,2},{1,3},{2,0},{3,1},{4,6},{5,7},{6,4},{7,5},{8,10},{9,11},{10,... | collective-permute-start | bytes 1572872 | tf_op jit(solution)/shard_map/ppermute | solution.py:348
  378.6 22.5 %collective-permute-start.40 = (bf16[128,2048]{1,0:T(8,128)(2,1)S(1)}, bf16[128,2048]{1,0:T(8,128)(2,1)S(1)}, u32[]{:S(2)}, u32[]{:S(2)}) collective-permute-start(bf16[128,2048]{1,0:T(8,128)(2,1)S(1)} %get-tuple-element.105), channel_id=1, source_target_pairs={{0,2},{1,3},{2,0},{3,1},{4,6},{5,7},{6,4},{7,5},{8,10},{9,11},{10,... | collective-permute-start | bytes 1572872 | tf_op jit(solution)/shard_map/ppermute | solution.py:348
  392.1 17.5 %collective-permute-start.45 = (bf16[256,2048]{1,0:T(8,128)(2,1)S(1)}, bf16[256,2048]{1,0:T(8,128)(2,1)S(1)}, u32[]{:S(2)}, u32[]{:S(2)}) collective-permute-start(bf16[256,2048]{1,0:T(8,128)(2,1)S(1)} %pad_maximum_fusion.25), channel_id=1, source_target_pairs={{0,1},{1,0},{2,3},{3,2},{4,5},{5,4},{6,7},{7,6},{8,9},{9,8},{10,11... | collective-permute-start | bytes 3145736 | tf_op jit(solution)/shard_map/ppermute | solution.py:348
  406.0 186.1 %collective-permute-start.64 = (bf16[1024,2048]{1,0:T(8,128)(2,1)}, bf16[1024,2048]{1,0:T(8,128)(2,1)}, u32[]{:S(2)}, u32[]{:S(2)}) collective-permute-start(bf16[1024,2048]{1,0:T(8,128)(2,1)} %convolution_convert_fusion), channel_id=1, source_target_pairs={{0,16},{16,0},{1,17},{17,1},{2,18},{18,2},{3,19},{19,3},{4,20},{20... | collective-permute-start | bytes 12582920 | tf_op jit(solution)/shard_map/ppermute | solution.py:342
  419.9 23.0 %collective-permute-start.47 = (bf16[2,512,128]{2,1,0:T(8,128)(2,1)S(1)}, bf16[2,512,128]{2,1,0:T(8,128)(2,1)S(1)}, u32[]{:S(2)}, u32[]{:S(2)}) collective-permute-start(bf16[2,512,128]{2,1,0:T(8,128)(2,1)S(1)} %get-tuple-element.221), channel_id=1, source_target_pairs={{0,8},{4,12},{8,0},{12,4},{1,9},{5,13},{9,1},{13,5},{2,10},{6,14},... | collective-permute-start | bytes 786440 | tf_op jit(solution)/shard_map/ppermute | solution.py:345
  421.9 21.7 %collective-permute-start.46 = (bf16[2,512,128]{2,1,0:T(8,128)(2,1)S(1)}, bf16[2,512,128]{2,1,0:T(8,128)(2,1)S(1)}, u32[]{:S(2)}, u32[]{:S(2)}) collective-permute-start(bf16[2,512,128]{2,1,0:T(8,128)(2,1)S(1)} %get-tuple-element.222), channel_id=1, source_target_pairs={{0,4},{4,8},{8,12},{12,0},{1,5},{5,9},{9,13},{13,1},{2,6},{6,10},{... | collective-permute-start | bytes 786440 | tf_op jit(solution)/shard_map/ppermute | solution.py:345
  459.1 263.0 %reduce-scatter.6.cloned.1.call-start = ((), (), s32[]{:S(2)}) async-start(), calls=%async_computation.4 | async-start | bytes 5242880 | tf_op jit(solution)/shard_map/reduce_scatter | solution.py:570
  489.2 24.7 %collective-permute-start.49 = (bf16[512,384]{1,0:T(8,128)(2,1)S(1)}, bf16[512,384]{1,0:T(8,128)(2,1)}, u32[]{:S(2)}, u32[]{:S(2)}) collective-permute-start(bf16[512,384]{1,0:T(8,128)(2,1)S(1)} %bitcast.367), channel_id=1, source_target_pairs={{0,12},{4,0},{8,4},{12,8},{1,13},{5,1},{9,5},{13,9},{2,14},{6,2},{... | collective-permute-start | bytes 1179656 | tf_op jit(solution)/shard_map/ppermute | solution.py:345
  490.1 73.3 %collective-permute-start.50 = (bf16[512,384]{1,0:T(8,128)(2,1)S(1)}, bf16[512,384]{1,0:T(8,128)(2,1)}, u32[]{:S(2)}, u32[]{:S(2)}) collective-permute-start(bf16[512,384]{1,0:T(8,128)(2,1)S(1)} %bitcast.366), channel_id=1, source_target_pairs={{0,8},{4,12},{8,0},{12,4},{1,9},{5,13},{9,1},{13,5},{2,10},{6,14},... | collective-permute-start | bytes 1179656 | tf_op jit(solution)/shard_map/ppermute | solution.py:345
  490.3 73.1 %collective-permute-start.51 = (bf16[512,384]{1,0:T(8,128)(2,1)S(1)}, bf16[512,384]{1,0:T(8,128)(2,1)}, u32[]{:S(2)}, u32[]{:S(2)}) collective-permute-start(bf16[512,384]{1,0:T(8,128)(2,1)S(1)} %bitcast.365), channel_id=1, source_target_pairs={{0,4},{4,8},{8,12},{12,0},{1,5},{5,9},{9,13},{13,1},{2,6},{6,10},{... | collective-permute-start | bytes 1179656 | tf_op jit(solution)/shard_map/ppermute | solution.py:345
  510.1 91.9 %collective-permute-start.55 = (bf16[2,256,2048]{2,1,0:T(8,128)(2,1)}, bf16[2,256,2048]{2,1,0:T(8,128)(2,1)}, u32[]{:S(2)}, u32[]{:S(2)}) collective-permute-start(bf16[2,256,2048]{2,1,0:T(8,128)(2,1)} %fusion.14), channel_id=1, source_target_pairs={{0,1},{1,0},{2,3},{3,2},{4,5},{5,4},{6,7},{7,6},{8,9},{9,8},{10,11... | collective-permute-start | bytes 6291464 | tf_op jit(solution)/shard_map/ppermute | solution.py:348
  587.9 53.5 %collective-permute-start.52 = (bf16[512,384]{1,0:T(8,128)(2,1)}, bf16[512,384]{1,0:T(8,128)(2,1)}, u32[]{:S(2)}, u32[]{:S(2)}) collective-permute-start(bf16[512,384]{1,0:T(8,128)(2,1)} %bitcast.364), channel_id=1, source_target_pairs={{0,12},{4,0},{8,4},{12,8},{1,13},{5,1},{9,5},{13,9},{2,14},{6,2},{... | collective-permute-start | bytes 1179656 | tf_op jit(solution)/shard_map/ppermute | solution.py:345
  587.9 53.5 %collective-permute-start.53 = (bf16[512,384]{1,0:T(8,128)(2,1)}, bf16[512,384]{1,0:T(8,128)(2,1)}, u32[]{:S(2)}, u32[]{:S(2)}) collective-permute-start(bf16[512,384]{1,0:T(8,128)(2,1)} %bitcast.363), channel_id=1, source_target_pairs={{0,8},{4,12},{8,0},{12,4},{1,9},{5,13},{9,1},{13,5},{2,10},{6,14},... | collective-permute-start | bytes 1179656 | tf_op jit(solution)/shard_map/ppermute | solution.py:345
  589.8 51.6 %collective-permute-start.54 = (bf16[512,384]{1,0:T(8,128)(2,1)}, bf16[512,384]{1,0:T(8,128)(2,1)}, u32[]{:S(2)}, u32[]{:S(2)}) collective-permute-start(bf16[512,384]{1,0:T(8,128)(2,1)} %bitcast.362), channel_id=1, source_target_pairs={{0,4},{4,8},{8,12},{12,0},{1,5},{5,9},{9,13},{13,1},{2,6},{6,10},{... | collective-permute-start | bytes 1179656 | tf_op jit(solution)/shard_map/ppermute | solution.py:345
  601.4 19.1 %collective-permute-start.59 = (bf16[256,2048]{1,0:T(8,128)(2,1)}, bf16[256,2048]{1,0:T(8,128)(2,1)S(1)}, u32[]{:S(2)}, u32[]{:S(2)}) collective-permute-start(bf16[256,2048]{1,0:T(8,128)(2,1)} %fusion.64), channel_id=1, source_target_pairs={{0,1},{1,0},{2,3},{3,2},{4,5},{5,4},{6,7},{7,6},{8,9},{9,8},{10,11... | collective-permute-start | bytes 3145736 | tf_op jit(solution)/shard_map/ppermute | solution.py:348
  609.5 26.3 %collective-permute-start.56 = (bf16[1,256,2048]{2,1,0:T(8,128)(2,1)}, bf16[1,256,2048]{2,1,0:T(8,128)(2,1)}, u32[]{:S(2)}, u32[]{:S(2)}) collective-permute-start(bf16[1,256,2048]{2,1,0:T(8,128)(2,1)} %slice.921), channel_id=1, source_target_pairs={{0,2},{1,3},{2,0},{3,1},{4,6},{5,7},{6,4},{7,5},{8,10},{9,11},{10,... | collective-permute-start | bytes 3145736 | tf_op jit(solution)/shard_map/ppermute | solution.py:348
  624.7 22.6 %collective-permute-start.60 = (bf16[128,2048]{1,0:T(8,128)(2,1)}, bf16[128,2048]{1,0:T(8,128)(2,1)}, u32[]{:S(2)}, u32[]{:S(2)}) collective-permute-start(bf16[128,2048]{1,0:T(8,128)(2,1)} %slice.923), channel_id=1, source_target_pairs={{0,2},{1,3},{2,0},{3,1},{4,6},{5,7},{6,4},{7,5},{8,10},{9,11},{10,... | collective-permute-start | bytes 1572872 | tf_op jit(solution)/shard_map/ppermute | solution.py:348
  641.5 136.3 %reduce-scatter.8.cloned.1.call-start = ((), (), s32[]{:S(2)}) async-start(), calls=%async_computation.5 | async-start | bytes 1310720 | tf_op jit(solution)/shard_map/reduce_scatter | solution.py:570
  644.9 19.4 %collective-permute-start.66 = (bf16[512,1024]{1,0:T(8,128)(2,1)S(1)}, bf16[512,1024]{1,0:T(8,128)(2,1)S(1)}, u32[]{:S(2)}, u32[]{:S(2)}) collective-permute-start(bf16[512,1024]{1,0:T(8,128)(2,1)S(1)} %fusion.75), channel_id=1, source_target_pairs={{0,16},{16,0},{1,17},{17,1},{2,18},{18,2},{3,19},{19,3},{4,20},{20... | collective-permute-start | bytes 3145736 | tf_op jit(solution)/shard_map/ppermute | solution.py:342
  672.9 34.9 %collective-permute-start.63 = (bf16[256,2048]{1,0:T(8,128)(2,1)}, bf16[256,2048]{1,0:T(8,128)(2,1)}, u32[]{:S(2)}, u32[]{:S(2)}) collective-permute-start(bf16[256,2048]{1,0:T(8,128)(2,1)} %fusion.63), channel_id=1, source_target_pairs={{0,1},{1,0},{2,3},{3,2},{4,5},{5,4},{6,7},{7,6},{8,9},{9,8},{10,11... | collective-permute-start | bytes 3145736 | tf_op jit(solution)/shard_map/ppermute | solution.py:348
  676.0 28.7 %collective-permute-start.57 = (bf16[2,128,2048]{2,1,0:T(8,128)(2,1)}, bf16[2,128,2048]{2,1,0:T(8,128)(2,1)}, u32[]{:S(2)}, u32[]{:S(2)}) collective-permute-start(bf16[2,128,2048]{2,1,0:T(8,128)(2,1)} %pad_maximum_fusion.26), channel_id=1, source_target_pairs={{0,2},{1,3},{2,0},{3,1},{4,6},{5,7},{6,4},{7,5},{8,10},{9,11},{10,... | collective-permute-start | bytes 3145736 | tf_op jit(solution)/shard_map/ppermute | solution.py:348
  683.2 18.5 %collective-permute-start.75 = (bf16[1024,384]{1,0:T(8,128)(2,1)}, bf16[1024,384]{1,0:T(8,128)(2,1)}, u32[]{:S(2)}, u32[]{:S(2)}) collective-permute-start(bf16[1024,384]{1,0:T(8,128)(2,1)} %add_convert_fusion.6), channel_id=1, source_target_pairs={{0,16},{16,0},{1,17},{17,1},{2,18},{18,2},{3,19},{19,3},{4,20},{20... | collective-permute-start | bytes 2359304 | tf_op jit(solution)/shard_map/ppermute | solution.py:342
  704.4 75.9 %collective-permute-start.76 = (bf16[256,384]{1,0:T(8,128)(2,1)}, bf16[256,384]{1,0:T(8,128)(2,1)S(1)}, u32[]{:S(2)}, u32[]{:S(2)}) collective-permute-start(bf16[256,384]{1,0:T(8,128)(2,1)} %get-tuple-element.229), channel_id=1, source_target_pairs={{0,4},{4,8},{8,12},{12,0},{1,5},{5,9},{9,13},{13,1},{2,6},{6,10},{... | collective-permute-start | bytes 589832 | tf_op jit(solution)/shard_map/ppermute | solution.py:345
  707.9 54.4 %collective-permute-start.58 = (bf16[2,256,2048]{2,1,0:T(8,128)(2,1)}, bf16[2,256,2048]{2,1,0:T(8,128)(2,1)}, u32[]{:S(2)}, u32[]{:S(2)}) collective-permute-start(bf16[2,256,2048]{2,1,0:T(8,128)(2,1)} %pad_maximum_fusion.20), channel_id=1, source_target_pairs={{0,1},{1,0},{2,3},{3,2},{4,5},{5,4},{6,7},{7,6},{8,9},{9,8},{10,11... | collective-permute-start | bytes 6291464 | tf_op jit(solution)/shard_map/ppermute | solution.py:348
  725.7 13.8 %collective-permute-start.65 = (bf16[128,2048]{1,0:T(8,128)(2,1)}, bf16[128,2048]{1,0:T(8,128)(2,1)}, u32[]{:S(2)}, u32[]{:S(2)}) collective-permute-start(bf16[128,2048]{1,0:T(8,128)(2,1)} %slice.922), channel_id=1, source_target_pairs={{0,2},{1,3},{2,0},{3,1},{4,6},{5,7},{6,4},{7,5},{8,10},{9,11},{10,... | collective-permute-start | bytes 1572872 | tf_op jit(solution)/shard_map/ppermute | solution.py:348
  757.2 19.3 %collective-permute-start.61 = (bf16[128,2048]{1,0:T(8,128)(2,1)}, bf16[128,2048]{1,0:T(8,128)(2,1)S(1)}, u32[]{:S(2)}, u32[]{:S(2)}) collective-permute-start(bf16[128,2048]{1,0:T(8,128)(2,1)} %get-tuple-element.216), channel_id=1, source_target_pairs={{0,2},{1,3},{2,0},{3,1},{4,6},{5,7},{6,4},{7,5},{8,10},{9,11},{10,... | collective-permute-start | bytes 1572872 | tf_op jit(solution)/shard_map/ppermute | solution.py:348
  758.7 15.1 %collective-permute-start.72 = (f32[6,256]{1,0:T(8,128)S(1)}, f32[6,256]{1,0:T(8,128)S(1)}, u32[]{:S(2)}, u32[]{:S(2)}) collective-permute-start(f32[6,256]{1,0:T(8,128)S(1)} %get-tuple-element.253), channel_id=1, source_target_pairs={{0,4},{4,8},{8,12},{12,0},{1,5},{5,9},{9,13},{13,1},{2,6},{6,10},{... | collective-permute-start | bytes 18440 | tf_op jit(solution)/shard_map/ppermute | solution.py:345
  760.4 13.5 %collective-permute-start.73 = (f32[6,256]{1,0:T(8,128)S(1)}, f32[6,256]{1,0:T(8,128)S(1)}, u32[]{:S(2)}, u32[]{:S(2)}) collective-permute-start(f32[6,256]{1,0:T(8,128)S(1)} %get-tuple-element.255), channel_id=1, source_target_pairs={{0,8},{4,12},{8,0},{12,4},{1,9},{5,13},{9,1},{13,5},{2,10},{6,14},... | collective-permute-start | bytes 18440 | tf_op jit(solution)/shard_map/ppermute | solution.py:345
  762.3 13.6 %collective-permute-start.74 = (f32[6,256]{1,0:T(8,128)S(1)}, f32[6,256]{1,0:T(8,128)S(1)}, u32[]{:S(2)}, u32[]{:S(2)}) collective-permute-start(f32[6,256]{1,0:T(8,128)S(1)} %get-tuple-element.254), channel_id=1, source_target_pairs={{0,12},{4,0},{8,4},{12,8},{1,13},{5,1},{9,5},{13,9},{2,14},{6,2},{... | collective-permute-start | bytes 18440 | tf_op jit(solution)/shard_map/ppermute | solution.py:345
  777.6 29.3 %collective-permute-start.62 = (bf16[256,2048]{1,0:T(8,128)(2,1)S(1)}, bf16[256,2048]{1,0:T(8,128)(2,1)}, u32[]{:S(2)}, u32[]{:S(2)}) collective-permute-start(bf16[256,2048]{1,0:T(8,128)(2,1)S(1)} %pad_maximum_fusion.27.refs_0_), channel_id=1, source_target_pairs={{0,1},{1,0},{2,3},{3,2},{4,5},{5,4},{6,7},{7,6},{8,9},{9,8},{10,11... | collective-permute-start | bytes 3145736 | tf_op jit(solution)/shard_map/ppermute | solution.py:348
  779.7 14.1 %collective-permute-start.67 = (bf16[128,2048]{1,0:T(8,128)(2,1)S(1)}, bf16[128,2048]{1,0:T(8,128)(2,1)S(1)}, u32[]{:S(2)}, u32[]{:S(2)}) collective-permute-start(bf16[128,2048]{1,0:T(8,128)(2,1)S(1)} %copy-done.50), channel_id=1, source_target_pairs={{0,2},{1,3},{2,0},{3,1},{4,6},{5,7},{6,4},{7,5},{8,10},{9,11},{10,... | collective-permute-start | bytes 1572872 | tf_op jit(solution)/shard_map/ppermute | solution.py:348
  (159 other events, 1425.2 us)
Sparse Core Ops, SparseCore 0:
  31.0 209.5 all-gather.4
  279.9 61.1 all-gather.6
  459.2 100.7 reduce-scatter.3
  641.6 80.4 reduce-scatter.5
  730.5 26.7 reduce-scatter.7
